TPU v7x, 32 devices: a whole 2x2x4 slice. The times are simulated.
32 devices in a mesh: groups: 2 (over y), seq: 8 (over z, x), vocab: 2 (over core).
Axes of the slice: x: 2, y: 2, z: 4, core: 2. Of those that a mesh axis runs over, the one named last changes fastest.
Arguments:
- features: bfloat16 [2, 2048, 8192], P('vocab', 'groups', 'seq'), parts along dimension 1, may hold values from -1000 to 1000
- positions: int32 [2, 2048], P('vocab', ('groups', 'seq')), parts along dimension 1, may hold values from 0 to 511, as said below
- token_ids: int32 [2, 2048], P(None, ('groups', 'seq')), parts along dimension 1, may hold values from 0 to 1023
- valid: int32 [2, 2048], P(None, ('groups', 'seq')), parts along dimension 1, may hold values 0 or 1
- teacher_logits: bfloat16 [2, 2048, 1024], P(None, ('groups', 'seq'), 'vocab'), parts along dimension 1, may hold values from -260 to 260
- in_gain: bfloat16 [8192], replicated, may hold values from 0.5 to 1.5
- final_gain: bfloat16 [8192], replicated, may hold values from 0.5 to 1.5
- w_in: bfloat16 [64, 8192], replicated, may hold values from -0.0625 to 0.0625
- w_out: bfloat16 [64, 8192], replicated, may hold values from -0.75 to 0.75
- head: bfloat16 [1024, 8192], P('vocab'), may hold values from -8 to 8
Outputs:
- grads: float32 [16384, 128], P(('groups', 'seq', 'vocab')), parts along dimension 0
- row_loss: float32 [2, 2048], P(None, ('groups', 'seq')), parts along dimension 1
There are 2 independent parts, one for each index of `groups`. A program takes and returns all parts, laid end to end along the dimension named above; an argument that names none is the same for every part. Nothing has to cross between parts.
Inputs may be any that keep to these rules, and one draw needn't show every extreme that they name: `positions`: each stream begins a document at its first token and at every multiple of 512 tokens, and may begin others between; inside a document the position rises by one from token to token.
All inputs are finite; a program needn't handle non-finite values. No bound on the sum of `valid` on one device may be relied on, other than what follows from the above.
Results may differ from a plain program's by a relative error of at most 0.012.
Values may be sent and summed in bfloat16 or wider, within the bound.
No kernel may reach another device: no remote copies, remote signals or barrier semaphores. Data moves between devices by JAX's collectives and lax.ppermute only.
A program may use at most 128 MiB of HBM per device.

v0:
```python
import math

import jax
import jax.numpy as jnp
from jax import lax
from jax.sharding import PartitionSpec as P

EPSILON = 1e-05
HARD_WEIGHT = 0.5
ROPE_BASE = 10000.0


def merged_2(value, axis, join):
    pieces = jax.tree.map(lambda part: lax.all_gather(part, axis), value)
    head = jax.tree.map(lambda part: part[0], pieces)
    tail = jax.tree.map(lambda part: part[1:], pieces)
    total, _ = lax.scan(lambda total, share: (join(total, share), None), head, tail)
    return total


def rotation(positions, halfway):
    freqs = jnp.exp(-math.log(ROPE_BASE) * jnp.arange(halfway, dtype=jnp.float32) / halfway)
    angles = positions.astype(jnp.float32)[:, None] * freqs[None, :]
    return (jnp.cos(angles), jnp.sin(angles))


def combine_stats(former, latter):
    student_top = jnp.maximum(former[0], latter[0])
    teacher_top = jnp.maximum(former[2], latter[2])
    former_s = jnp.exp(former[0] - student_top)
    latter_s = jnp.exp(latter[0] - student_top)
    former_t = jnp.exp(former[2] - teacher_top)
    latter_t = jnp.exp(latter[2] - teacher_top)
    return (
        student_top,
        former[1] * former_s + latter[1] * latter_s,
        teacher_top,
        former[3] * former_t + latter[3] * latter_t,
        former[4] * former_t + latter[4] * latter_t,
        former[5] + latter[5],
    )


def on_device(
    features, positions, token_ids, valid, teacher_logits, in_gain, final_gain, w_in, w_out, head
):
    seq_count = lax.axis_size("seq")
    vocab_index = lax.axis_index("vocab")
    halfway = w_in.shape[0] // 2
    slice_width = head.shape[0]
    stacked = features.reshape(seq_count, features.shape[1] // seq_count, features.shape[2])
    values = lax.all_to_all(stacked, "seq", split_axis=0, concat_axis=2, tiled=True).astype(
        jnp.float32
    )
    inverse_in = lax.rsqrt(jnp.mean(values * values, axis=-1, keepdims=True) + EPSILON)
    normed_part = (values * inverse_in * in_gain.astype(jnp.float32)).astype(jnp.bfloat16)
    latent_part = jnp.einsum("akd,rd->akr", normed_part, w_in, preferred_element_type=jnp.float32)
    normed = normed_part
    latent = latent_part
    normed = normed[0]
    latent = latent[0]
    cosine, sine_part = rotation(positions[0], halfway)
    leading, trailing = (latent[:, :halfway], latent[:, halfway:])
    turned = jnp.concatenate(
        [leading * cosine - trailing * sine_part, leading * sine_part + trailing * cosine], axis=1
    )
    active = jax.nn.silu(turned).astype(jnp.bfloat16)
    hidden = normed.astype(jnp.float32) + jnp.dot(active, w_out, preferred_element_type=jnp.float32)
    inverse_out = lax.rsqrt(jnp.mean(hidden * hidden, axis=-1, keepdims=True) + EPSILON)
    unit_rows = hidden * inverse_out
    out_gain = final_gain.astype(jnp.float32)
    final_norm = (unit_rows * out_gain).astype(jnp.bfloat16)
    logits = jnp.einsum(
        "akd,vd->akv",
        lax.all_gather(final_norm[None], "vocab", axis=0, tiled=True),
        head,
        preferred_element_type=jnp.float32,
    )
    teacher = teacher_logits.astype(jnp.float32)
    columns = vocab_index * slice_width + jnp.arange(slice_width, dtype=jnp.int32)
    label_hits = token_ids[:, :, None] == columns[None, None, :]
    student_top = jnp.max(logits, axis=-1)
    student_total = jnp.sum(jnp.exp(logits - student_top[..., None]), axis=-1)
    teacher_top = jnp.max(teacher, axis=-1)
    teacher_weight = jnp.exp(teacher - teacher_top[..., None])
    teacher_total = jnp.sum(teacher_weight, axis=-1)
    teacher_cross = jnp.sum(teacher_weight * (teacher - logits), axis=-1)
    picked = jnp.sum(jnp.where(label_hits, logits, 0.0), axis=-1)
    merged = merged_2(
        (student_top, student_total, teacher_top, teacher_total, teacher_cross, picked),
        "vocab",
        combine_stats,
    )
    student_lse = merged[0] + jnp.log(merged[1])
    teacher_lse = merged[2] + jnp.log(merged[3])
    row_mask = valid.astype(jnp.float32)
    row_loss = row_mask * (
        merged[4] / merged[3] - teacher_lse + student_lse + HARD_WEIGHT * (student_lse - merged[5])
    )
    prob_student = jnp.exp(logits - student_lse[..., None])
    prob_teacher = jnp.exp(teacher - teacher_lse[..., None])
    grad_logits = (
        row_mask[..., None]
        * (
            prob_student
            - prob_teacher
            + HARD_WEIGHT * (prob_student - label_hits.astype(jnp.float32))
        )
    ).astype(jnp.bfloat16)
    partial_value = jnp.einsum("akv,vd->akd", grad_logits, head, preferred_element_type=jnp.float32)
    summed = lax.psum(partial_value.astype(jnp.bfloat16), "vocab").astype(jnp.float32)
    grad_final = lax.dynamic_index_in_dim(summed, vocab_index, 0, keepdims=False)
    weighted = grad_final * out_gain
    grad_hidden = (
        inverse_out
        * (weighted - unit_rows * jnp.mean(unit_rows * weighted, axis=-1, keepdims=True))
    ).astype(jnp.bfloat16)
    grad_active = jnp.einsum("kd,rd->kr", grad_hidden, w_out, preferred_element_type=jnp.float32)
    sigmoid_value = jax.nn.sigmoid(turned)
    grad_turned = grad_active * sigmoid_value * (1.0 + turned * (1.0 - sigmoid_value))
    lead_grad, trail_grad = (grad_turned[:, :halfway], grad_turned[:, halfway:])
    grad_latent = jnp.concatenate(
        [lead_grad * cosine + trail_grad * sine_part, trail_grad * cosine - lead_grad * sine_part],
        axis=1,
    ).astype(jnp.bfloat16)
    into_grad = jnp.einsum("kd,kr->dr", normed, grad_latent, preferred_element_type=jnp.float32)
    outof_grad = jnp.einsum("kd,kr->dr", grad_hidden, active, preferred_element_type=jnp.float32)
    grad_table = lax.psum_scatter(
        jnp.concatenate([into_grad, outof_grad], axis=1),
        ("seq", "vocab"),
        scatter_dimension=0,
        tiled=True,
    )
    return (grad_table, row_loss)


def solution(mesh):
    placed = (
        P("vocab", "groups", "seq"),
        P("vocab", ("groups", "seq")),
        P(None, ("groups", "seq")),
        P(None, ("groups", "seq")),
        P(None, ("groups", "seq"), "vocab"),
        P(),
        P(),
        P(),
        P(),
        P("vocab", None),
    )
    return jax.shard_map(
        on_device,
        mesh=mesh,
        in_specs=placed,
        out_specs=(P(("groups", "seq", "vocab"), None), P(None, ("groups", "seq"))),
        check_vma=False,
    )
```

profile of v0, /device:TPU:0, one launch (start us, length us, event | category | flops | bytes accessed | tf_op | source)
XLA Modules:
  0.0 232.3 jit_solution(11351482049400875166)
XLA Ops:
  7.2 0.0 copy-start
  7.2 0.0 copy-start.5
  7.2 0.0 copy-start.6
  7.2 7.4 %all-to-all-start = ((bf16[8,128,1024]{2,1,0:T(8,128)(2,1)}), bf16[8,128,1024]{2,1,0:T(8,128)(2,1)S(1)}, u32[]{:S(2)}, u32[]{:S(2)}) async-start(bf16[8,128,1024]{2,1,0:T(8,128)(2,1)} %bitcast.146), calls=%async_computation | async-start | bytes 4194304 | tf_op jit(solution)/shard_map/all_to_all | solution.py:52
  14.6 0.0 all-gather.15.cloned.1.call-start
  14.7 0.0 copy-done.6
  14.8 48.1 %all-to-all-done = bf16[8,128,1024]{2,1,0:T(8,128)(2,1)S(1)} async-done(((bf16[8,128,1024]{2,1,0:T(8,128)(2,1)}), bf16[8,128,1024]{2,1,0:T(8,128)(2,1)S(1)}, u32[]{:S(2)}, u32[]{:S(2)}) %all-to-all-start) | async-done | bytes 2097184 | tf_op jit(solution)/shard_map/all_to_all | solution.py:52
  62.9 0.5 fusion.3
  63.4 0.5 fusion.66
  63.9 0.6 copy.16
  64.4 0.0 copy-start.3
  64.5 0.5 multiply_convert_fusion.2
  65.0 0.7 copy-done.3
  65.7 0.8 fusion.67
  66.5 0.1 fusion.32
  66.7 0.0 copy-done
  66.7 1.0 multiply_reduce_fusion.1
  67.7 1.9 copy-done.1
  69.6 1.9 multiply_convert_fusion.1
  71.5 0.0 all-gather.15.cloned.1.call-update
  71.5 0.0 all-reduce.2.cloned.1.call-start
  71.6 0.1 reduce_max.28
  71.7 1.8 all-gather.9
  73.5 10.9 %all-gather.15.cloned.1.call-done = bf16[256,8192]{1,0:T(8,128)(2,1)} async-done(((bf16[128,8192]{1,0:T(8,128)(2,1)}), bf16[256,8192]{1,0:T(8,128)(2,1)}) %all-gather.15.cloned.1.call-update) | async-done | bytes 4194320 | tf_op jit(solution)/shard_map/all_gather | solution.py:75
  84.4 7.1 %fusion.65 = (f32[2,128]{1,0:T(2,128)S(1)}, f32[2,128,512]{2,1,0:T(8,128)S(1)}) fusion(bf16[2,128,8192]{2,1,0:T(8,128)(2,1)} %bitcast.152, bf16[512,8192]{1,0:T(8,128)(2,1)} %param.19), kind=kOutput, calls=%fused_computation.108 | convolution fusion | flops 2147614464 | bytes 13108224 | tf_op jit(solution)/shard_map/akd,vd->akv/dot_general | solution.py:73
  91.5 1.8 all-gather.7
  93.3 0.0 copy-done.8
  93.3 0.5 fusion.14
  93.8 1.8 all-gather.12
  95.6 1.8 all-gather.11
  97.4 1.8 all-gather.8
  99.2 1.8 all-gather.10
  101.0 0.6 fusion.46
  101.6 7.9 %convolution_convert_fusion = bf16[2,128,8192]{2,1,0:T(8,128)(2,1)} fusion(bf16[512,8192]{1,0:T(8,128)(2,1)} %param.19, bf16[2,128,512]{2,1,0:T(8,128)(2,1)S(1)} %copy-done.4, f32[2,128,512]{2,1,0:T(8,128)S(1)} %get-tuple-element.61, s32[512]{0:T(512)S(1)} %iota_add_fusion, s32[2,128]{1,0:T(2,128)S(1)} %copy-done.8, f32[2,128]{1,0:T(2,128)S(1)} %get-tuple-element.38, ...), kind=kOutput, calls=%fused_computation | convolution fusion | flops 2151022592 | bytes 13375488 | tf_op jit(solution)/shard_map/akv,vd->akd/dot_general | solution.py:110
  109.5 0.0 all-reduce.2.cloned.1.call-update
  109.5 0.2 reduce-scatter.2.cloned.1.call-start
  109.7 29.2 %all-reduce.2.cloned.1.call-done = bf16[2,128,8192]{2,1,0:T(8,128)(2,1)} async-done(((bf16[2,128,8192]{2,1,0:T(8,128)(2,1)}), bf16[2,128,8192]{2,1,0:T(8,128)(2,1)}) %all-reduce.2.cloned.1.call-update) | async-done | bytes 4194320 | tf_op jit(solution)/shard_map/psum | solution.py:111
  138.9 3.8 %multiply_reduce_fusion = f32[128]{0:T(128)S(1)} fusion(f32[128,8192]{1,0:T(8,128)} %copy-done.1, f32[8192]{0:T(1024)S(1)} %convert_element_type.88, f32[128]{0:T(128)S(1)} %add_rsqrt_fusion, bf16[2,128,8192]{2,1,0:T(8,128)(2,1)} %all-reduce.2.cloned.1.call-done, s32[]{:T(128)S(6)} %select_n.8), kind=kLoop, calls=%fused_computation.11 | loop fusion | flops 5242752 | bytes 6325252 | tf_op jit(solution)/shard_map/reduce_sum | solution.py:116
  142.7 0.2 copy-done.2
  143.0 2.6 %multiply_convert_fusion = bf16[128,8192]{1,0:T(8,128)(2,1)S(1)} fusion(f32[128,8192]{1,0:T(8,128)S(1)} %copy-done.2, f32[128]{0:T(128)S(1)} %broadcast_multiply_fusion, f32[8192]{0:T(1024)S(1)} %convert_element_type.88, f32[128]{0:T(128)S(1)} %add_rsqrt_fusion, bf16[2,128,8192]{2,1,0:T(8,128)(2,1)} %all-reduce.2.cloned.1.call-done, s32[]{:T(128)S(6)} %select_n.8), kind=kLoop, calls=%fused_computation.10 | loop fusion | flops 7340032 | bytes 8422404 | tf_op jit(solution)/shard_map/convert_element_type | solution.py:117
  145.6 0.9 fusion.4
  146.5 0.4 fusion.63
  146.9 0.1 fusion.35
  147.1 0.4 fusion.38
  147.5 2.3 pad_maximum_fusion
  149.8 0.0 reduce-scatter.2.cloned.1.call-update
  149.8 74.2 %reduce-scatter.2.cloned.1.call-done = f32[512,128]{0,1:T(8,128)} async-done(((f32[8192,128]{0,1:T(8,128)}), f32[512,128]{0,1:T(8,128)}) %reduce-scatter.2.cloned.1.call-update) | async-done | bytes 262160 | tf_op jit(solution)/shard_map/reduce_scatter | solution.py:128
  224.0 1.8 copy.15
  (20 shorter events, 0.1 us)
Async XLA Ops:
  7.2 59.5 %copy-start = (bf16[64,8192]{1,0:T(8,128)(2,1)S(1)}, bf16[64,8192]{1,0:T(8,128)(2,1)}, u32[]{:S(2)}) copy-start(bf16[64,8192]{1,0:T(8,128)(2,1)} %param.18) | copy-start | bytes 3145732
  7.2 7.5 %copy-start.5 = (bf16[8192]{0:T(1024)(128)(2,1)S(1)}, bf16[8192]{0:T(1024)(128)(2,1)}, u32[]{:S(2)}) copy-start(bf16[8192]{0:T(1024)(128)(2,1)} %param.16) | copy-start | bytes 49156
  7.2 7.5 %copy-start.6 = (bf16[8192]{0:T(1024)(128)(2,1)S(1)}, bf16[8192]{0:T(1024)(128)(2,1)}, u32[]{:S(2)}) copy-start(bf16[8192]{0:T(1024)(128)(2,1)} %param.15) | copy-start | bytes 49156
  7.2 7.5 %copy-start.9 = (s32[1,128]{1,0:T(1,128)S(1)}, s32[1,128]{1,0:T(1,128)}, u32[]{:S(2)}) copy-start(s32[1,128]{1,0:T(1,128)} %param.11) | copy-start | bytes 1540
  7.2 55.7 %all-to-all-start = ((bf16[8,128,1024]{2,1,0:T(8,128)(2,1)}), bf16[8,128,1024]{2,1,0:T(8,128)(2,1)S(1)}, u32[]{:S(2)}, u32[]{:S(2)}) async-start(bf16[8,128,1024]{2,1,0:T(8,128)(2,1)} %bitcast.146), calls=%async_computation | async-start | bytes 4194304 | tf_op jit(solution)/shard_map/all_to_all | solution.py:52
  14.6 69.8 %all-gather.15.cloned.1.call-start = ((), (), s32[]{:S(2)}) async-start(), calls=%async_computation.4 | async-start | bytes 6291456 | tf_op jit(solution)/shard_map/all_gather | solution.py:75
  64.4 1.2 copy-start.3
  67.7 1.9 copy-start.1
  69.6 2.0 copy-start.7
  69.6 2.0 copy-start.4
  71.5 67.4 %all-reduce.2.cloned.1.call-start = ((), (), s32[]{:S(2)}) async-start(), calls=%async_computation.2 | async-start | bytes 8388608 | tf_op jit(solution)/shard_map/psum | solution.py:111
  84.4 8.9 %copy-start.8 = (s32[2,128]{1,0:T(2,128)S(1)}, s32[2,128]{1,0:T(2,128)}, u32[]{:S(2)}) copy-start(s32[2,128]{1,0:T(2,128)} %param.12) | copy-start | bytes 3076
  109.5 114.5 %reduce-scatter.2.cloned.1.call-start = ((), (), s32[]{:S(2)}) async-start(), calls=%async_computation.3 | async-start | bytes 4456448 | tf_op jit(solution)/shard_map/reduce_scatter | solution.py:128
  138.9 4.1 %copy-start.2 = (f32[128,8192]{1,0:T(8,128)S(1)}, f32[128,8192]{1,0:T(8,128)}, u32[]{:S(2)}) copy-start(f32[128,8192]{1,0:T(8,128)} %copy-done.1) | copy-start | bytes 12582916
Sparse Core Ops, SparseCore 0:
  71.6 12.7 all-gather.14
  109.6 29.2 all-reduce.1
  149.9 73.9 reduce-scatter.1
where the time goes:
time: 233 us; the launch traced here: 232 us
  waiting for transfers between devices  162 us (70%)
  matrix products  18.6 us (8%)
  between operations  14 us (6%)
  other arithmetic  13.6 us (6%)
  blocking collectives  10.8 us (5%)
  starting transfers between devices  7.73 us (3%)
  local copies, waits for them, and re-layouts  5.28 us (2%)
    reduce_scatter x1, waiting for transfers between devices, on_device(): lax.psum_scatter(jnp.concatenate([into_grad, outof_grad], axis=1), ('seq'...  74.2 us
    all_to_all x1, waiting for transfers between devices, on_device(): lax.all_to_all(stacked, 'seq', split_axis=0, concat_axis=2, tiled=True)  48.1 us
    psum x1, waiting for transfers between devices, on_device(): lax.psum(partial_value.astype(jnp.bfloat16), 'vocab').astype(jnp.float32)  29.2 us
    all_gather x1, waiting for transfers between devices, on_device(): lax.all_gather(final_norm[None], 'vocab', axis=0, tiled=True)  10.9 us
    all_gather x6, blocking collectives, merged_2(): pieces = jax.tree.map(lambda part: lax.all_gather(part, axis), value)  10.8 us
    dot_general x1, matrix products, on_device(): jnp.einsum('akv,vd->akd', grad_logits, head, preferred_element_type=jnp.f...  7.9 us
    all_to_all x1, starting transfers between devices, on_device(): lax.all_to_all(stacked, 'seq', split_axis=0, concat_axis=2, tiled=True)  7.42 us
    dot_general x1, matrix products, on_device(): jnp.einsum('akd,vd->akv', lax.all_gather(final_norm[None], 'vocab', axis=...  7.11 us
  transfers between devices with their start and end apart: 4, of which 4 were waited for; matrix products, arithmetic and copies ran while one was open for 0% of the time, Pallas kernels for 0%

commit v1 on v0

v1 whole, which is shorter than its diff:
```python
import functools
import math

import jax
import jax.numpy as jnp
from jax import lax
from jax.experimental import pallas as pl
from jax.experimental.pallas import tpu as pltpu
from jax.sharding import PartitionSpec as P

EPSILON = 1e-05
HARD_WEIGHT = 0.5
ROPE_BASE = 10000.0
LANES = 128
F32 = jnp.float32
BF16 = jnp.bfloat16
PAIR = [(0, 1), (1, 0)]


def mirrored(place, bits):
    out = 0
    for bit in range(bits):
        out = out | (((place >> bit) & 1) << (bits - 1 - bit))
    return out


def swap_with(value, bit, count):
    return lax.ppermute(value, "seq", [(i, i ^ bit) for i in range(count)])


def swap_cores(value):
    return lax.ppermute(value, "vocab", PAIR)


def mm(lhs, rhs, lhs_dim, rhs_dim):
    return lax.dot_general(
        lhs, rhs, (((lhs_dim,), (rhs_dim,)), ((), ())), preferred_element_type=F32
    )


def partial_kernel(bits, block, pieces, index_ref, x_ref, gain_ref, *refs):
    tables, (send_ref, keep_ref, scaled_ref) = refs[:-3], refs[-3:]
    row = 0
    for table_ref, (first, count, gain_row) in zip(tables, pieces):
        scaled_ref[row : row + count, :] = (
            table_ref[first : first + count, :].astype(F32) * gain_ref[gain_row : gain_row + 1, :]
        ).astype(BF16)
        row += count
    half = 1 << (bits - 1)
    group = min(4, half)
    for base, out_ref in ((half, send_ref), (0, keep_ref)):

        def body(step, carry, base=base, out_ref=out_ref):
            rows = []
            for offset in range(group):
                owner = mirrored(base + step * group + offset, bits) ^ index_ref[0]
                rows.append(x_ref[pl.ds(pl.multiple_of(owner * block, block), block), :])
            product = mm(jnp.concatenate(rows, axis=0), scaled_ref[...], 1, 1)
            out_ref[pl.ds(step * group, group)] = product.reshape(
                group, block, product.shape[1]
            ).astype(out_ref.dtype)
            return carry

        if half == group:
            body(0, 0)
        else:
            lax.fori_loop(0, half // group, body, 0)


def partial_products(index, x, gains, tables, pieces, count, block):
    bits = count.bit_length() - 1
    width = sum(piece[1] for piece in pieces)
    columns = x.shape[1]
    local = pl.BlockSpec((x.shape[0], columns), lambda i, at: (0, 0))

    def table_spec(table):
        if table.shape[1] == columns:
            return pl.BlockSpec(table.shape, lambda i, at: (0, 0))
        return pl.BlockSpec((table.shape[0], columns), lambda i, at: (0, at[0]))

    half = count // 2
    shape = (half, block, width)
    return pl.pallas_call(
        functools.partial(partial_kernel, bits, block, pieces),
        grid_spec=pltpu.PrefetchScalarGridSpec(
            num_scalar_prefetch=1,
            grid=(1,),
            in_specs=[local, pl.BlockSpec((8, columns), lambda i, at: (0, at[0]))]
            + [table_spec(table) for table in tables],
            out_specs=[pl.BlockSpec(shape, lambda i, at: (0, 0, 0))] * 2,
            scratch_shapes=[pltpu.VMEM((width, columns), BF16)],
        ),
        out_shape=[jax.ShapeDtypeStruct(shape, BF16), jax.ShapeDtypeStruct(shape, F32)],
        cost_estimate=pl.CostEstimate(
            flops=2 * x.shape[0] * columns * width,
            bytes_accessed=2 * x.shape[0] * columns + 2 * width * columns + 6 * half * block * width,
            transcendentals=0,
        ),
        name="partial",
    )(index, x, gains, *tables)


def owner_kernel(depth, chunks, *refs):
    keeps, gots = refs[:chunks], refs[chunks : 2 * chunks]
    stats_ref, marks_ref, turn_ref, own_t_ref, far_t_ref, own_h_ref, far_h_ref, gram_ref = refs[
        2 * chunks : 2 * chunks + 8
    ]
    loss_ref, factor_ref, table_ref, table_send_ref = refs[2 * chunks + 8 :]
    sums = [keep[0] + got[0].astype(F32) for keep, got in zip(keeps, gots)]
    rank2 = LANES
    rank = rank2 // 2
    half = rank // 2
    raw_latent = sums[0][:, :rank]
    raw_cross = sums[0][:, rank:rank2]
    raw_logits = jnp.concatenate([sums[0][:, rank2:]] + sums[1:], axis=1)
    inverse_in = lax.rsqrt(stats_ref[:, 0:1] * (1.0 / depth) + EPSILON)
    latent = raw_latent * inverse_in
    cosine = turn_ref[:, :rank]
    sine = turn_ref[:, rank:rank2]

    def swapped(value):
        return jnp.concatenate([value[:, half:], value[:, :half]], axis=1)

    turned = latent * cosine + swapped(latent) * sine
    sigmoid = 1.0 / (1.0 + jnp.exp(-turned))
    active = (turned * sigmoid).astype(BF16)
    active_wide = active.astype(F32)
    gram_part = mm(active, gram_ref[...].astype(BF16), 1, 0)
    cross = raw_cross * inverse_in
    square = (
        inverse_in * inverse_in * stats_ref[:, 1:2]
        + jnp.sum(active_wide * (2.0 * cross + gram_part), axis=1, keepdims=True)
    )
    inverse_out = lax.rsqrt(jnp.maximum(square, 0.0) * (1.0 / depth) + EPSILON)
    head_out = jnp.concatenate([own_h_ref[...], far_h_ref[...]], axis=1)
    head_high = head_out.astype(BF16)
    head_low = (head_out - head_high.astype(F32)).astype(BF16)
    logits = inverse_out * (
        raw_logits * inverse_in + (mm(active, head_high, 1, 0) + mm(active, head_low, 1, 0))
    )
    teacher = jnp.concatenate([own_t_ref[...], far_t_ref[...]], axis=1).astype(F32)
    student_top = jnp.max(logits, axis=1, keepdims=True)
    student = jnp.exp(logits - student_top)
    student_total = jnp.sum(student, axis=1, keepdims=True)
    student_lse = student_top + jnp.log(student_total)
    teacher_top = jnp.max(teacher, axis=1, keepdims=True)
    weight = jnp.exp(teacher - teacher_top)
    teacher_total = jnp.sum(weight, axis=1, keepdims=True)
    teacher_lse = teacher_top + jnp.log(teacher_total)
    prob_teacher = weight * (1.0 / teacher_total)
    prob_student = student * (1.0 / student_total)
    hits = lax.broadcasted_iota(jnp.int32, logits.shape, 1) == marks_ref[:, 0:1]
    picked = jnp.sum(jnp.where(hits, logits, 0.0), axis=1, keepdims=True)
    mask = marks_ref[:, 1:2].astype(F32)
    overlap = jnp.sum(prob_teacher * (teacher - logits), axis=1, keepdims=True)
    loss_ref[...] = mask * (
        overlap - teacher_lse + student_lse + HARD_WEIGHT * (student_lse - picked)
    )
    grad_logits = (
        mask
        * (
            prob_student
            - prob_teacher
            + HARD_WEIGHT * (prob_student - jnp.where(hits, 1.0, 0.0))
        )
    ).astype(BF16)
    mean = jnp.sum(grad_logits.astype(F32) * logits, axis=1, keepdims=True) * (1.0 / depth)
    through = mm(grad_logits, head_high, 1, 1) + mm(grad_logits, head_low, 1, 1)
    grad_active = inverse_out * (through - mean * inverse_out * (cross + gram_part))
    grad_turned = grad_active * sigmoid * (1.0 + turned * (1.0 - sigmoid))
    grad_latent = grad_turned * cosine - swapped(grad_turned) * sine
    weight_back = -inverse_out * inverse_out * mean
    factor_ref[...] = jnp.concatenate(
        [inverse_in * grad_latent, (inverse_in * weight_back) * active_wide], axis=1
    ).astype(BF16)
    table = mm((inverse_out * active_wide).astype(BF16), grad_logits, 0, 0)
    slice_width = own_h_ref.shape[1]
    parts = slice_width // LANES
    for part in range(parts):
        table_ref[part * rank : (part + 1) * rank, :] = table[:, part * LANES : (part + 1) * LANES]
        table_send_ref[part * rank : (part + 1) * rank, :] = table[
            :, slice_width + part * LANES : slice_width + (part + 1) * LANES
        ].astype(BF16)
    own_gram = mm((weight_back * active_wide).astype(BF16), active, 0, 0)
    table_ref[parts * rank :, :] = jnp.concatenate([own_gram, jnp.zeros_like(own_gram)], axis=1)


def owner_step(depth, rank, keeps, gots, stats, marks, turn, teachers, heads, gram):
    block = stats.shape[0]
    slice_width = heads[0].shape[1]
    parts = slice_width // LANES
    spec = pl.BlockSpec(memory_space=pltpu.VMEM)
    operands = [*keeps, *gots, stats, marks, turn, *teachers, *heads, gram]
    return pl.pallas_call(
        functools.partial(owner_kernel, depth, len(keeps)),
        in_specs=[spec] * len(operands),
        out_specs=[spec] * 4,
        out_shape=[
            jax.ShapeDtypeStruct((block, 1), F32),
            jax.ShapeDtypeStruct((block, 2 * rank), BF16),
            jax.ShapeDtypeStruct(((parts + 1) * rank, LANES), F32),
            jax.ShapeDtypeStruct((parts * rank, LANES), BF16),
        ],
        name="owner",
    )(*operands)


def final_kernel(bits, block, rank, index_ref, x_ref, gain_ref, head_ref, out_w_ref, factor_ref,
                 table_ref, out_ref, order_ref):
    count = 1 << bits

    def body(place, carry):
        owner = mirrored(place, bits) ^ index_ref[0]
        order_ref[pl.ds(pl.multiple_of(owner * block, block), block), :] = factor_ref[
            pl.ds(pl.multiple_of(place * block, block), block), :
        ]
        return carry

    if count <= 8:
        for place in range(count):
            body(place, 0)
    else:
        lax.fori_loop(0, count, body, 0)
    slice_width = head_ref.shape[0]
    parts = slice_width // LANES
    from_x = mm(order_ref[...], x_ref[...], 0, 0) * gain_ref[1:2, :]
    table = jnp.concatenate(
        [table_ref[part * rank : (part + 1) * rank, :] for part in range(parts)], axis=1
    ).astype(BF16)
    from_head = mm(table, head_ref[...], 1, 0) * gain_ref[2:3, :]
    gram = table_ref[parts * rank :, :][:, :rank].astype(BF16)
    from_out = mm(gram, out_w_ref[...], 1, 0)
    total = jnp.concatenate([from_x[:rank], from_x[rank:] + from_head + from_out], axis=0)
    out_ref[...] = total.T


def final_step(index, x, gains, head, out_w, factor, table, count, block, pieces):
    bits = count.bit_length() - 1
    columns = x.shape[1] // pieces
    rank = out_w.shape[0]
    at_wide = lambda i, at: (0, at[0] * pieces + at[1])
    whole = lambda i, at: (0, 0)
    return pl.pallas_call(
        functools.partial(final_kernel, bits, block, rank),
        grid_spec=pltpu.PrefetchScalarGridSpec(
            num_scalar_prefetch=1,
            grid=(1,),
            in_specs=[
                pl.BlockSpec((x.shape[0], columns), lambda i, at: (0, at[1])),
                pl.BlockSpec((8, columns), at_wide),
                pl.BlockSpec((head.shape[0], columns), at_wide),
                pl.BlockSpec((rank, columns), at_wide),
                pl.BlockSpec(factor.shape, whole),
                pl.BlockSpec(table.shape, whole),
            ],
            out_specs=pl.BlockSpec((columns, 2 * rank), whole),
            scratch_shapes=[pltpu.VMEM(factor.shape, BF16)],
        ),
        out_shape=jax.ShapeDtypeStruct((columns, 2 * rank), F32),
        cost_estimate=pl.CostEstimate(
            flops=2 * x.shape[0] * columns * 2 * rank,
            bytes_accessed=2 * x.shape[0] * columns,
            transcendentals=0,
        ),
        name="final",
    )(index, x, gains, head, out_w, factor, table)


def on_device(
    features, positions, token_ids, valid, teacher_logits, in_gain, final_gain, w_in, w_out, head
):
    count = lax.axis_size("seq")
    bits = count.bit_length() - 1
    here = lax.axis_index("seq")
    core = lax.axis_index("vocab")
    x = features[0]
    block = x.shape[0] // count
    columns = x.shape[1]
    rank, depth = w_in.shape
    half = rank // 2
    slice_width = head.shape[0]
    vocabulary = 2 * slice_width

    far_head = swap_cores(lax.dynamic_slice_in_dim(head, here * columns, columns, axis=1))
    own_teacher = lax.dynamic_index_in_dim(teacher_logits, core, 0, keepdims=False)
    far_teacher = swap_cores(lax.dynamic_index_in_dim(teacher_logits, 1 - core, 0, keepdims=False))

    in_wide, final_wide = in_gain.astype(F32), final_gain.astype(F32)
    gains = jnp.stack([in_wide * final_wide, in_wide, final_wide] + [jnp.zeros_like(in_wide)] * 5)
    index = jnp.stack([here, core]).astype(jnp.int32)

    first = 256
    middle = (vocabulary - first) // 2
    inside = slice_width - first
    plans = [
        ([w_in, w_out, head], [(0, rank, 1), (0, rank, 1), (0, first, 0)]),
        ([head, far_head], [(first, inside, 0), (0, middle - inside, 0)]),
        ([far_head], [(middle - inside, slice_width - (middle - inside), 0)]),
    ]
    squares = jnp.square(x.astype(F32))
    in_columns = lax.dynamic_slice_in_dim(in_wide, here * columns, columns, axis=0)
    sums = jnp.stack([jnp.sum(squares, axis=1), jnp.sum(squares * jnp.square(in_columns), axis=1)])
    order = jnp.array([mirrored(place, bits) for place in range(count)], jnp.int32) ^ here
    stats = jnp.take(sums.reshape(2, count, block), order, axis=1)

    sends, keeps = [], []
    for tables, pieces in plans:
        send, keep = partial_products(index, x, gains, tables, pieces, count, block)
        sends.append(send)
        keeps.append(keep)
    for step in range(bits):
        bit = 1 << step
        gots = [swap_with(send, bit, count) for send in sends]
        left = count >> (step + 1)
        stats = stats[:, :left] + swap_with(stats[:, left:], bit, count)
        if step == bits - 1:
            break
        total = [keep + got.astype(F32) for keep, got in zip(keeps, gots)]
        sends = [value[left // 2 :].astype(BF16) for value in total]
        keeps = [value[: left // 2] for value in total]

    scaled_out = (w_out.astype(F32) * final_wide).astype(BF16)
    own_out = mm(scaled_out, head, 1, 1)
    far_out = swap_cores(own_out)
    gram = mm(w_out, w_out, 1, 1)

    freqs = jnp.exp(-math.log(ROPE_BASE) * jnp.arange(half, dtype=F32) / half)
    angles = positions[0].astype(F32)[:, None] * freqs[None, :]
    cosine, sine = jnp.cos(angles), jnp.sin(angles)
    turn = jnp.concatenate([cosine, cosine, -sine, sine], axis=1)
    labels = lax.dynamic_index_in_dim(token_ids, core, 0, keepdims=False)
    labels = lax.rem(labels + core * slice_width, vocabulary)
    marks = jnp.stack([labels, lax.dynamic_index_in_dim(valid, core, 0, keepdims=False)], axis=1)

    loss, factor, table, table_send = owner_step(
        depth,
        rank,
        keeps,
        gots,
        stats[:, 0].T,
        marks,
        turn,
        (own_teacher, far_teacher),
        (own_out, far_out),
        gram,
    )

    own_loss = loss.reshape(1, block)
    far_loss = swap_cores(own_loss)
    row_loss = jnp.where(
        core == 0,
        jnp.concatenate([own_loss, far_loss]),
        jnp.concatenate([far_loss, own_loss]),
    )

    got = swap_cores(table_send)
    table = jnp.concatenate([table[: got.shape[0]] + got.astype(F32), table[got.shape[0] :]])
    for step in reversed(range(bits)):
        rows = factor.shape[0]
        got = swap_with(jnp.concatenate([factor, table.astype(BF16)]), 1 << step, count)
        factor = jnp.concatenate([factor, got[:rows]])
        table = table + got[rows:].astype(F32)

    finish = functools.partial(
        final_step, x=x, gains=gains, head=head, out_w=w_out, factor=factor, table=table,
        count=count, block=block,
    )
    if (columns // 2) % LANES == 0:
        away = finish(index=jnp.stack([here, 1 - core]).astype(jnp.int32), pieces=2)
        near = finish(index=index, pieces=2)
    else:
        both = finish(index=jnp.stack([here, jnp.zeros_like(here)]).astype(jnp.int32), pieces=1)
        near = lax.dynamic_slice_in_dim(both, core * (columns // 2), columns // 2, axis=0)
        away = lax.dynamic_slice_in_dim(both, (1 - core) * (columns // 2), columns // 2, axis=0)
    return (near + swap_cores(away), row_loss)


def solution(mesh):
    placed = (
        P("vocab", "groups", "seq"),
        P("vocab", ("groups", "seq")),
        P(None, ("groups", "seq")),
        P(None, ("groups", "seq")),
        P(None, ("groups", "seq"), "vocab"),
        P(),
        P(),
        P(),
        P(),
        P("vocab", None),
    )
    return jax.shard_map(
        on_device,
        mesh=mesh,
        in_specs=placed,
        out_specs=(P(("groups", "seq", "vocab"), None), P(None, ("groups", "seq"))),
        check_vma=False,
    )
```

time: 233 us -> 124 us (0.53)
  waiting for transfers between devices: 162 us -> 36.5 us
  Pallas kernels: 0 us -> 25.3 us
  starting transfers between devices: 7.73 us -> 23.2 us
  between operations: 14 us -> 0.99 us
  matrix products: 18.6 us -> 7.06 us
  blocking collectives: 10.8 us -> 0 us
  local copies, waits for them, and re-layouts: 5.28 us -> 11.5 us
  other arithmetic: 13.6 us -> 18.2 us
    reduce_scatter x1 -> x0, waiting for transfers between devices: 74.2 us -> none  [on_device(): lax.psum_scatter(jnp.concatenate([into_grad, outof_grad], axis=1), ('seq'...]
    all_to_all x1 -> x0, waiting for transfers between devices: 48.1 us -> none  [on_device(): lax.all_to_all(stacked, 'seq', split_axis=0, concat_axis=2, tiled=True)]
    ppermute x0 -> x21, waiting for transfers between devices: none -> 36.5 us  [the longest x15 34.7 us: swap_with(): return lax.ppermute(value, 'seq', [(i, i ^ bit) for i in range(count)])]
    psum x1 -> x0, waiting for transfers between devices: 29.2 us -> none  [on_device(): lax.psum(partial_value.astype(jnp.bfloat16), 'vocab').astype(jnp.float32)]
    pallas_call x0 -> x6, Pallas kernels: none -> 25.3 us  [the longest x3 14.7 us: partial_products(): pl.pallas_call(functools.partial(partial_kernel, bits, block, pieces), gr...]
    ppermute x0 -> x21, starting transfers between devices: none -> 23.2 us  [the longest x15 22.1 us: swap_with(): return lax.ppermute(value, 'seq', [(i, i ^ bit) for i in range(count)])]
    dot_general x7 -> x2, matrix products: 18.6 us -> 7.06 us  [mm(): lax.dot_general(lhs, rhs, (((lhs_dim,), (rhs_dim,)), ((), ())), preferred...]
    all_gather x1 -> x0, waiting for transfers between devices: 10.9 us -> none  [on_device(): lax.all_gather(final_norm[None], 'vocab', axis=0, tiled=True)]
  transfers between devices with their start and end apart: 4 -> 21, of which waited for: 4 -> 11; matrix products, arithmetic and copies ran while one was open for 0% -> 18% of each run, Pallas kernels for 0% -> 15%
where the time goes in v1:
time: 124 us; the launch traced here: 123 us
  waiting for transfers between devices  36.5 us (29%)
  Pallas kernels  25.3 us (20%)
  starting transfers between devices  23.2 us (19%)
  other arithmetic  18.2 us (15%)
  local copies, waits for them, and re-layouts  11.5 us (9%)
  matrix products  7.06 us (6%)
    ppermute x15, waiting for transfers between devices, swap_with(): return lax.ppermute(value, 'seq', [(i, i ^ bit) for i in range(count)])  34.7 us
    ppermute x15, starting transfers between devices, swap_with(): return lax.ppermute(value, 'seq', [(i, i ^ bit) for i in range(count)])  22.1 us
    pallas_call x3, Pallas kernels, partial_products(): pl.pallas_call(functools.partial(partial_kernel, bits, block, pieces), gr...  14.7 us
    dot_general x2, matrix products, mm(): lax.dot_general(lhs, rhs, (((lhs_dim,), (rhs_dim,)), ((), ())), preferred...  7.06 us
    pallas_call x2, Pallas kernels, final_step(): pl.pallas_call(functools.partial(final_kernel, bits, block, rank), grid_s...  6.98 us
    pallas_call x1, Pallas kernels, owner_step(): pl.pallas_call(functools.partial(owner_kernel, depth, len(keeps)), in_spe...  3.65 us
    add x6, other arithmetic, on_device(): total = [keep + got.astype(F32) for keep, got in zip(keeps, gots)]  2.49 us
  transfers between devices with their start and end apart: 21, of which 11 were waited for; matrix products, arithmetic and copies ran while one was open for 18% of the time, Pallas kernels for 15%

profile of v1, /device:TPU:0, one launch (start us, length us, event | category | flops | bytes accessed | tf_op | source)
XLA Modules:
  0.0 122.8 jit_solution(12901363072143122052)
XLA Ops:
  0.7 0.8 convert_element_type.70
  2.1 2.4 %fusion = (f32[1024]{0:T(1024)S(1)}, f32[1024]{0:T(1024)S(1)}) fusion(bf16[1,1024,1024]{2,1,0:T(8,128)(2,1)} %param.11, f32[1024]{0:T(1024)S(1)} %dynamic-slice_multiply_fusion), kind=kLoop, calls=%fused_computation.3 | loop fusion | flops 5240832 | bytes 2109440 | tf_op jit(solution)/shard_map/reduce_sum | solution.py:302
  5.5 0.7 slice.125
  6.2 3.0 %collective-permute-start.10 = (f32[2,4,128]{0,2,1:T(8,128)}, f32[2,4,128]{0,2,1:T(8,128)}, u32[]{:S(2)}, u32[]{:S(2)}) collective-permute-start(f32[2,4,128]{0,2,1:T(8,128)} %slice.125), channel_id=1, source_target_pairs={{0,2},{2,0},{4,6},{6,4},{8,10},{10,8},{12,14},{14,12},{1,3},{3,1},... | collective-permute-start | bytes 12296 | tf_op jit(solution)/shard_map/ppermute | solution.py:28
  9.1 2.3 %constant_dynamic-slice_fusion.2 = bf16[512,1024]{1,0:T(8,128)(2,1)} fusion(bf16[512,8192]{1,0:T(8,128)(2,1)} %head_ref.3, s32[]{:T(128)S(6)} %select_n.31), kind=kLoop, calls=%fused_computation.51 | loop fusion | bytes 2097156 | tf_op jit(solution)/shard_map/dynamic_slice | solution.py:284
  12.1 0.9 stack.54.gain_ref
  13.1 5.0 %partial.3 = (bf16[4,128,384]{2,1,0:T(8,128)(2,1)}, f32[4,128,384]{2,1,0:T(8,128)}) custom-call(s32[2]{0:T(128)} %pad_add_fusion.1.index_ref, bf16[1024,1024]{1,0:T(8,128)(2,1)} %bitcast.32, f32[8,8192]{1,0:T(8,128)} %stack.54.gain_ref, bf16[64,8192]{1,0:T(8,128)(2,1)} %refs_0_.2, bf16[64,8192]{1,0:T(8,128)(2,1)} %out_w_ref.3, bf16[512,8192]{1,0:T(8,128)(2,1)} %head_ref.3), custom_call_target="tpu_custom_call" | custom-call | flops 805306368 | bytes 4063232 | tf_op jit(solution)/shard_map/partial/pallas_call | solution.py:83
  18.0 0.7 dynamic-slice_bitcast_fusion
  19.3 6.0 %fusion.1.refs_11_ = f32[64,512]{1,0:T(8,128)S(1)} fusion(bf16[512,8192]{1,0:T(8,128)(2,1)} %head_ref.3, bf16[64,8192]{1,0:T(8,128)(2,1)S(1)} %copy-done.1, f32[8192]{0:T(1024)S(1)} %convert_element_type.71), kind=kOutput, calls=%fused_computation.5 | convolution fusion | flops 538443776 | bytes 9601024 | tf_op jit(solution)/shard_map/dot_general | solution.py:36
  25.7 0.7 pad_maximum_fusion.5.refs_8_
  26.5 1.0 fusion.12.refs_13_
  27.5 0.7 copy.32.refs_7_
  28.3 1.0 slice_add_fusion.3
  29.9 2.1 %collective-permute-start.11 = (f32[2,2,128]{0,2,1:T(8,128)}, f32[2,2,128]{0,2,1:T(8,128)S(1)}, u32[]{:S(2)}, u32[]{:S(2)}) collective-permute-start(f32[2,2,128]{0,2,1:T(8,128)} %slice.127), channel_id=1, source_target_pairs={{0,4},{2,6},{4,0},{6,2},{8,12},{10,14},{12,8},{14,10},{1,5},{3,7},... | collective-permute-start | bytes 6152 | tf_op jit(solution)/shard_map/ppermute | solution.py:28
  32.0 1.1 convert_add_fusion.2
  33.3 1.0 copy-done.2
  34.2 4.7 %partial.5 = (bf16[4,128,384]{2,1,0:T(8,128)(2,1)}, f32[4,128,384]{2,1,0:T(8,128)}) custom-call(s32[2]{0:T(128)} %pad_add_fusion.1.index_ref, bf16[1024,1024]{1,0:T(8,128)(2,1)} %bitcast.33, f32[8,8192]{1,0:T(8,128)} %stack.54.gain_ref, bf16[512,1024]{1,0:T(8,128)(2,1)} %copy-done.2), custom_call_target="tpu_custom_call" | custom-call | flops 805306368 | bytes 4063232 | tf_op jit(solution)/shard_map/partial/pallas_call | solution.py:83
  38.9 1.9 %collective-permute-start.5 = (bf16[4,128,384]{2,1,0:T(8,128)(2,1)}, bf16[4,128,384]{2,1,0:T(8,128)(2,1)S(1)}, u32[]{:S(2)}, u32[]{:S(2)}) collective-permute-start(bf16[4,128,384]{2,1,0:T(8,128)(2,1)} %get-tuple-element.17), channel_id=1, source_target_pairs={{0,2},{2,0},{4,6},{6,4},{8,10},{10,8},{12,14},{14,12},{1,3},{3,1},... | collective-permute-start | bytes 1179656 | tf_op jit(solution)/shard_map/ppermute | solution.py:28
  40.9 2.7 %collective-permute-start.12 = (f32[2,1,128]{0,2,1:T(8,128)S(1)}, f32[2,1,128]{0,2,1:T(8,128)S(1)}, u32[]{:S(2)}, u32[]{:S(2)}) collective-permute-start(f32[2,1,128]{0,2,1:T(8,128)S(1)} %slice.129), channel_id=1, source_target_pairs={{0,8},{2,10},{4,12},{6,14},{8,0},{10,2},{12,4},{14,6},{1,9},{3,11}... | collective-permute-start | bytes 3080 | tf_op jit(solution)/shard_map/ppermute | solution.py:28
  43.6 5.0 %partial.4 = (bf16[4,128,384]{2,1,0:T(8,128)(2,1)}, f32[4,128,384]{2,1,0:T(8,128)}) custom-call(s32[2]{0:T(128)} %pad_add_fusion.1.index_ref, bf16[1024,1024]{1,0:T(8,128)(2,1)} %bitcast.34, f32[8,8192]{1,0:T(8,128)} %stack.54.gain_ref, bf16[512,8192]{1,0:T(8,128)(2,1)} %head_ref.3, bf16[512,1024]{1,0:T(8,128)(2,1)} %copy-done.2), custom_call_target="tpu_custom_call" | custom-call | flops 805306368 | bytes 4063232 | tf_op jit(solution)/shard_map/partial/pallas_call | solution.py:83
  49.2 0.9 collective-permute-done.5
  50.1 4.0 %collective-permute-start.7 = (bf16[1,128,384]{2,1,0:T(8,128)(2,1)S(1)}, bf16[1,128,384]{2,1,0:T(8,128)(2,1)S(1)}, u32[]{:S(2)}, u32[]{:S(2)}) collective-permute-start(bf16[1,128,384]{2,1,0:T(8,128)(2,1)S(1)} %slice.166), channel_id=1, source_target_pairs={{0,8},{2,10},{4,12},{6,14},{8,0},{10,2},{12,4},{14,6},{1,9},{3,11}... | collective-permute-start | bytes 294920 | tf_op jit(solution)/shard_map/ppermute | solution.py:28
  54.3 4.6 %collective-permute-done.3 = bf16[4,128,384]{2,1,0:T(8,128)(2,1)S(1)} collective-permute-done((bf16[4,128,384]{2,1,0:T(8,128)(2,1)}, bf16[4,128,384]{2,1,0:T(8,128)(2,1)S(1)}, u32[]{:S(2)}, u32[]{:S(2)}) %collective-permute-start.3) | collective-permute-done | bytes 393248 | tf_op jit(solution)/shard_map/ppermute | solution.py:28
  58.9 1.6 %collective-permute-start.6 = (bf16[2,128,384]{2,1,0:T(8,128)(2,1)S(1)}, bf16[2,128,384]{2,1,0:T(8,128)(2,1)S(1)}, u32[]{:S(2)}, u32[]{:S(2)}) collective-permute-start(bf16[2,128,384]{2,1,0:T(8,128)(2,1)S(1)} %slice.161), channel_id=1, source_target_pairs={{0,4},{2,6},{4,0},{6,2},{8,12},{10,14},{12,8},{14,10},{1,5},{3,7},... | collective-permute-start | bytes 589832 | tf_op jit(solution)/shard_map/ppermute | solution.py:28
  60.5 1.2 %convert_add_fusion.1 = f32[4,128,384]{2,1,0:T(8,128)S(1)} fusion(f32[4,128,384]{2,1,0:T(8,128)} %get-tuple-element.14, bf16[4,128,384]{2,1,0:T(8,128)(2,1)S(1)} %collective-permute-done.3), kind=kLoop, calls=%fused_computation.8 | loop fusion | flops 393216 | bytes 1966080 | tf_op jit(solution)/shard_map/add | solution.py:318
  61.8 3.1 %collective-permute-done.6 = bf16[2,128,384]{2,1,0:T(8,128)(2,1)S(1)} collective-permute-done((bf16[2,128,384]{2,1,0:T(8,128)(2,1)S(1)}, bf16[2,128,384]{2,1,0:T(8,128)(2,1)S(1)}, u32[]{:S(2)}, u32[]{:S(2)}) %collective-permute-start.6) | collective-permute-done | bytes 196640 | tf_op jit(solution)/shard_map/ppermute | solution.py:28
  64.9 1.6 %collective-permute-start.4 = (bf16[2,128,384]{2,1,0:T(8,128)(2,1)S(1)}, bf16[2,128,384]{2,1,0:T(8,128)(2,1)S(1)}, u32[]{:S(2)}, u32[]{:S(2)}) collective-permute-start(bf16[2,128,384]{2,1,0:T(8,128)(2,1)S(1)} %slice.162), channel_id=1, source_target_pairs={{0,4},{2,6},{4,0},{6,2},{8,12},{10,14},{12,8},{14,10},{1,5},{3,7},... | collective-permute-start | bytes 589832 | tf_op jit(solution)/shard_map/ppermute | solution.py:28
  66.5 5.1 %collective-permute-done.4 = bf16[2,128,384]{2,1,0:T(8,128)(2,1)S(1)} collective-permute-done((bf16[2,128,384]{2,1,0:T(8,128)(2,1)S(1)}, bf16[2,128,384]{2,1,0:T(8,128)(2,1)S(1)}, u32[]{:S(2)}, u32[]{:S(2)}) %collective-permute-start.4) | collective-permute-done | bytes 196640 | tf_op jit(solution)/shard_map/ppermute | solution.py:28
  71.6 2.0 %collective-permute-start.9 = (bf16[1,128,384]{2,1,0:T(8,128)(2,1)S(1)}, bf16[1,128,384]{2,1,0:T(8,128)(2,1)S(1)}, u32[]{:S(2)}, u32[]{:S(2)}) collective-permute-start(bf16[1,128,384]{2,1,0:T(8,128)(2,1)S(1)} %slice.164), channel_id=1, source_target_pairs={{0,8},{2,10},{4,12},{6,14},{8,0},{10,2},{12,4},{14,6},{1,9},{3,11}... | collective-permute-start | bytes 294920 | tf_op jit(solution)/shard_map/ppermute | solution.py:28
  73.7 0.9 collective-permute-start.8
  77.4 0.8 collective-permute-done.9.refs_5_
  78.2 2.1 %collective-permute-done.8.refs_4_ = bf16[1,128,384]{2,1,0:T(8,128)(2,1)S(1)} collective-permute-done((bf16[1,128,384]{2,1,0:T(8,128)(2,1)S(1)}, bf16[1,128,384]{2,1,0:T(8,128)(2,1)S(1)}, u32[]{:S(2)}, u32[]{:S(2)}) %collective-permute-start.8) | collective-permute-done | bytes 98336 | tf_op jit(solution)/shard_map/ppermute | solution.py:28
  81.0 3.7 %owner.1 = (f32[128,1]{1,0:T(8,128)}, bf16[128,128]{1,0:T(8,128)(2,1)}, f32[320,128]{1,0:T(8,128)}, bf16[256,128]{1,0:T(8,128)(2,1)}) custom-call(f32[1,128,384]{2,1,0:T(8,128)} %slice.114.refs_0_, f32[1,128,384]{2,1,0:T(8,128)} %slice.117.refs_1_, f32[1,128,384]{2,1,0:T(8,128)} %slice.120.refs_2_, bf16[1,128,384]{2,1,0:T(8,128)(2,1)} %copy-done.7, ...), custom_call_target="tpu_custom_call" | custom-call | tf_op jit(solution)/shard_map/owner/pallas_call | solution.py:194
  84.6 0.8 slice.103
  86.1 0.9 convert_add_fusion.6
  87.0 0.8 pad_maximum_fusion.4
  87.8 7.9 %collective-permute-done.16 = bf16[448,128]{1,0:T(8,128)(2,1)S(1)} collective-permute-done((bf16[448,128]{1,0:T(8,128)(2,1)S(1)}, bf16[448,128]{1,0:T(8,128)(2,1)S(1)}, u32[]{:S(2)}, u32[]{:S(2)}) %collective-permute-start.16) | collective-permute-done | bytes 114720 | tf_op jit(solution)/shard_map/ppermute | solution.py:28
  95.7 0.8 pad_maximum_fusion.3
  96.6 5.8 %collective-permute-done.17 = bf16[576,128]{1,0:T(8,128)(2,1)S(1)} collective-permute-done((bf16[576,128]{1,0:T(8,128)(2,1)S(1)}, bf16[576,128]{1,0:T(8,128)(2,1)S(1)}, u32[]{:S(2)}, u32[]{:S(2)}) %collective-permute-start.17) | collective-permute-done | bytes 147488 | tf_op jit(solution)/shard_map/ppermute | solution.py:28
  102.4 0.8 pad_maximum_fusion.1
  103.2 1.6 %collective-permute-start.18 = (bf16[832,128]{1,0:T(8,128)(2,1)S(1)}, bf16[832,128]{1,0:T(8,128)(2,1)S(1)}, u32[]{:S(2)}, u32[]{:S(2)}) collective-permute-start(bf16[832,128]{1,0:T(8,128)(2,1)S(1)} %pad_maximum_fusion.1), channel_id=1, source_target_pairs={{0,2},{2,0},{4,6},{6,4},{8,10},{10,8},{12,14},{14,12},{1,3},{3,1},... | collective-permute-start | bytes 638984 | tf_op jit(solution)/shard_map/ppermute | solution.py:28
  105.3 4.3 %collective-permute-done.18 = bf16[832,128]{1,0:T(8,128)(2,1)S(1)} collective-permute-done((bf16[832,128]{1,0:T(8,128)(2,1)S(1)}, bf16[832,128]{1,0:T(8,128)(2,1)S(1)}, u32[]{:S(2)}, u32[]{:S(2)}) %collective-permute-start.18) | collective-permute-done | bytes 213024 | tf_op jit(solution)/shard_map/ppermute | solution.py:28
  109.6 1.5 %pad_maximum_fusion.factor_ref = bf16[1024,128]{1,0:T(8,128)(2,1)} fusion(bf16[512,128]{1,0:T(8,128)(2,1)S(1)} %slice.134, bf16[256,128]{1,0:T(8,128)(2,1)S(1)} %slice.132, bf16[128,128]{1,0:T(8,128)(2,1)S(1)} %slice.130, bf16[128,128]{1,0:T(8,128)(2,1)} %get-tuple-element.18), kind=kLoop, calls=%fused_computation.17 | loop fusion | flops 1048576 | bytes 524288 | tf_op jit(solution)/shard_map/concatenate | solution.py:361
  111.1 0.7 convert_add_fusion.3.table_ref
  111.8 3.6 %final.3 = f32[512,128]{1,0:T(8,128)} custom-call(s32[2]{0:T(128)} %pad_add_fusion.2.index_ref, bf16[1024,1024]{1,0:T(8,128)(2,1)} %bitcast.35, f32[8,8192]{1,0:T(8,128)} %stack.54.gain_ref, bf16[512,8192]{1,0:T(8,128)(2,1)} %head_ref.3, bf16[64,8192]{1,0:T(8,128)(2,1)} %out_w_ref.3, bf16[1024,128]{1,0:T(8,128)(2,1)} %pad_maximum_fusion.factor_ref, ...), custom_call_target="tpu_custom_call" | custom-call | flops 134217728 | bytes 1048576 | tf_op jit(solution)/shard_map/final/pallas_call | solution.py:243
  116.0 1.1 collective-permute-done.20
  117.7 3.4 %final.2 = f32[512,128]{1,0:T(8,128)} custom-call(s32[2]{0:T(128)} %pad_add_fusion.1.index_ref, bf16[1024,1024]{1,0:T(8,128)(2,1)} %bitcast.36, f32[8,8192]{1,0:T(8,128)} %stack.54.gain_ref, bf16[512,8192]{1,0:T(8,128)(2,1)} %head_ref.3, bf16[64,8192]{1,0:T(8,128)(2,1)} %out_w_ref.3, bf16[1024,128]{1,0:T(8,128)(2,1)} %pad_maximum_fusion.factor_ref, ...), custom_call_target="tpu_custom_call" | custom-call | flops 134217728 | bytes 1048576 | tf_op jit(solution)/shard_map/final/pallas_call | solution.py:243
  121.1 1.7 %add.97 = f32[512,128]{1,0:T(8,128)} add(f32[512,128]{1,0:T(8,128)} %final.2, f32[512,128]{1,0:T(8,128)S(1)} %collective-permute-done.19) | non-fusion elementwise | flops 65536 | bytes 786432 | tf_op jit(solution)/shard_map/add | solution.py:375
  (95 shorter events, 10.8 us)
Async XLA Ops:
  0.6 25.9 %copy-start = (s32[2,128]{1,0:T(2,128)S(1)}, s32[2,128]{1,0:T(2,128)}, u32[]{:S(2)}) copy-start(s32[2,128]{1,0:T(2,128)} %param.14) | copy-start | bytes 3076
  0.6 10.8 %copy-start.12 = (bf16[8192]{0:T(1024)(128)(2,1)S(1)}, bf16[8192]{0:T(1024)(128)(2,1)}, u32[]{:S(2)}) copy-start(bf16[8192]{0:T(1024)(128)(2,1)} %param.16) | copy-start | bytes 49156
  0.7 10.8 %copy-start.11 = (bf16[8192]{0:T(1024)(128)(2,1)S(1)}, bf16[8192]{0:T(1024)(128)(2,1)}, u32[]{:S(2)}) copy-start(bf16[8192]{0:T(1024)(128)(2,1)} %param.17) | copy-start | bytes 49156
  6.2 22.1 %collective-permute-start.10 = (f32[2,4,128]{0,2,1:T(8,128)}, f32[2,4,128]{0,2,1:T(8,128)}, u32[]{:S(2)}, u32[]{:S(2)}) collective-permute-start(f32[2,4,128]{0,2,1:T(8,128)} %slice.125), channel_id=1, source_target_pairs={{0,2},{2,0},{4,6},{6,4},{8,10},{10,8},{12,14},{14,12},{1,3},{3,1},... | collective-permute-start | bytes 12296 | tf_op jit(solution)/shard_map/ppermute | solution.py:28
  11.4 21.8 %collective-permute-start.2 = (bf16[512,1024]{1,0:T(8,128)(2,1)}, bf16[512,1024]{1,0:T(8,128)(2,1)S(1)}, u32[]{:S(2)}, u32[]{:S(2)}) collective-permute-start(bf16[512,1024]{1,0:T(8,128)(2,1)} %constant_dynamic-slice_fusion.2), channel_id=1, source_target_pairs={{0,1},{1,0},{2,3},{3,2},{4,5},{5,4},{6,7},{7,6},{8,9},{9,8},{10,11... | collective-permute-start | bytes 3145736 | tf_op jit(solution)/shard_map/ppermute | solution.py:32
  13.1 5.0 %copy-start.6 = (bf16[2,128,512]{2,1,0:T(8,128)(2,1)S(1)}, bf16[2,128,512]{2,1,0:T(8,128)(2,1)}, u32[]{:S(2)}) copy-start(bf16[2,128,512]{2,1,0:T(8,128)(2,1)} %param.15) | copy-start | bytes 786436
  13.1 6.2 %copy-start.1 = (bf16[64,8192]{1,0:T(8,128)(2,1)S(1)}, bf16[64,8192]{1,0:T(8,128)(2,1)}, u32[]{:S(2)}) copy-start(bf16[64,8192]{1,0:T(8,128)(2,1)} %out_w_ref.3) | copy-start | bytes 3145732
  18.0 14.0 %collective-permute-start = (bf16[4,128,384]{2,1,0:T(8,128)(2,1)}, bf16[4,128,384]{2,1,0:T(8,128)(2,1)}, u32[]{:S(2)}, u32[]{:S(2)}) collective-permute-start(bf16[4,128,384]{2,1,0:T(8,128)(2,1)} %get-tuple-element.13), channel_id=1, source_target_pairs={{0,2},{2,0},{4,6},{6,4},{8,10},{10,8},{12,14},{14,12},{1,3},{3,1},... | collective-permute-start | bytes 1179656 | tf_op jit(solution)/shard_map/ppermute | solution.py:28
  18.7 6.7 %copy-start.14 = (s32[1,128]{1,0:T(1,128)S(1)}, s32[1,128]{1,0:T(1,128)}, u32[]{:S(2)}) copy-start(s32[1,128]{1,0:T(1,128)} %param.12) | copy-start | bytes 1540
  18.7 8.8 %copy-start.13 = (s32[2,128]{1,0:T(2,128)S(1)}, s32[2,128]{1,0:T(2,128)}, u32[]{:S(2)}) copy-start(s32[2,128]{1,0:T(2,128)} %param.13) | copy-start | bytes 3076
  18.8 58.6 %collective-permute-start.13 = (bf16[128,512]{1,0:T(8,128)(2,1)}, bf16[128,512]{1,0:T(8,128)(2,1)}, u32[]{:S(2)}, u32[]{:S(2)}) collective-permute-start(bf16[128,512]{1,0:T(8,128)(2,1)} %get-tuple-element.26), channel_id=1, source_target_pairs={{0,1},{1,0},{2,3},{3,2},{4,5},{5,4},{6,7},{7,6},{8,9},{9,8},{10,11... | collective-permute-start | bytes 393224 | tf_op jit(solution)/shard_map/ppermute | solution.py:32
  25.3 13.6 %copy-start.5 = (f32[64,512]{1,0:T(8,128)}, f32[64,512]{1,0:T(8,128)S(1)}, u32[]{:S(2)}) copy-start(f32[64,512]{1,0:T(8,128)S(1)} %fusion.1.refs_11_) | copy-start | bytes 393220
  25.3 6.7 %copy-start.3 = (f32[4,128,384]{2,1,0:T(8,128)S(1)}, f32[4,128,384]{2,1,0:T(8,128)}, u32[]{:S(2)}) copy-start(f32[4,128,384]{2,1,0:T(8,128)} %get-tuple-element.12) | copy-start | bytes 2359300
  25.3 52.1 %collective-permute-start.14 = (f32[64,512]{1,0:T(8,128)S(1)}, f32[64,512]{1,0:T(8,128)}, u32[]{:S(2)}, u32[]{:S(2)}) collective-permute-start(f32[64,512]{1,0:T(8,128)S(1)} %fusion.1.refs_11_), channel_id=1, source_target_pairs={{0,1},{1,0},{2,3},{3,2},{4,5},{5,4},{6,7},{7,6},{8,9},{9,8},{10,11... | collective-permute-start | bytes 393224 | tf_op jit(solution)/shard_map/ppermute | solution.py:32
  29.9 10.9 %collective-permute-start.11 = (f32[2,2,128]{0,2,1:T(8,128)}, f32[2,2,128]{0,2,1:T(8,128)S(1)}, u32[]{:S(2)}, u32[]{:S(2)}) collective-permute-start(f32[2,2,128]{0,2,1:T(8,128)} %slice.127), channel_id=1, source_target_pairs={{0,4},{2,6},{4,0},{6,2},{8,12},{10,14},{12,8},{14,10},{1,5},{3,7},... | collective-permute-start | bytes 6152 | tf_op jit(solution)/shard_map/ppermute | solution.py:28
  33.2 15.4 %collective-permute-start.1 = (bf16[2,128,384]{2,1,0:T(8,128)(2,1)S(1)}, bf16[2,128,384]{2,1,0:T(8,128)(2,1)S(1)}, u32[]{:S(2)}, u32[]{:S(2)}) collective-permute-start(bf16[2,128,384]{2,1,0:T(8,128)(2,1)S(1)} %slice.163), channel_id=1, source_target_pairs={{0,4},{2,6},{4,0},{6,2},{8,12},{10,14},{12,8},{14,10},{1,5},{3,7},... | collective-permute-start | bytes 589832 | tf_op jit(solution)/shard_map/ppermute | solution.py:28
  33.2 1.0 copy-start.2
  38.9 11.2 %collective-permute-start.5 = (bf16[4,128,384]{2,1,0:T(8,128)(2,1)}, bf16[4,128,384]{2,1,0:T(8,128)(2,1)S(1)}, u32[]{:S(2)}, u32[]{:S(2)}) collective-permute-start(bf16[4,128,384]{2,1,0:T(8,128)(2,1)} %get-tuple-element.17), channel_id=1, source_target_pairs={{0,2},{2,0},{4,6},{6,4},{8,10},{10,8},{12,14},{14,12},{1,3},{3,1},... | collective-permute-start | bytes 1179656 | tf_op jit(solution)/shard_map/ppermute | solution.py:28
  40.9 13.3 %copy-start.4 = (f32[4,128,384]{2,1,0:T(8,128)S(1)}, f32[4,128,384]{2,1,0:T(8,128)}, u32[]{:S(2)}) copy-start(f32[4,128,384]{2,1,0:T(8,128)} %get-tuple-element.16) | copy-start | bytes 2359300
  40.9 32.8 %collective-permute-start.12 = (f32[2,1,128]{0,2,1:T(8,128)S(1)}, f32[2,1,128]{0,2,1:T(8,128)S(1)}, u32[]{:S(2)}, u32[]{:S(2)}) collective-permute-start(f32[2,1,128]{0,2,1:T(8,128)S(1)} %slice.129), channel_id=1, source_target_pairs={{0,8},{2,10},{4,12},{6,14},{8,0},{10,2},{12,4},{14,6},{1,9},{3,11}... | collective-permute-start | bytes 3080 | tf_op jit(solution)/shard_map/ppermute | solution.py:28
  48.6 10.3 %collective-permute-start.3 = (bf16[4,128,384]{2,1,0:T(8,128)(2,1)}, bf16[4,128,384]{2,1,0:T(8,128)(2,1)S(1)}, u32[]{:S(2)}, u32[]{:S(2)}) collective-permute-start(bf16[4,128,384]{2,1,0:T(8,128)(2,1)} %get-tuple-element.15), channel_id=1, source_target_pairs={{0,2},{2,0},{4,6},{6,4},{8,10},{10,8},{12,14},{14,12},{1,3},{3,1},... | collective-permute-start | bytes 1179656 | tf_op jit(solution)/shard_map/ppermute | solution.py:28
  50.1 27.3 %collective-permute-start.7 = (bf16[1,128,384]{2,1,0:T(8,128)(2,1)S(1)}, bf16[1,128,384]{2,1,0:T(8,128)(2,1)S(1)}, u32[]{:S(2)}, u32[]{:S(2)}) collective-permute-start(bf16[1,128,384]{2,1,0:T(8,128)(2,1)S(1)} %slice.166), channel_id=1, source_target_pairs={{0,8},{2,10},{4,12},{6,14},{8,0},{10,2},{12,4},{14,6},{1,9},{3,11}... | collective-permute-start | bytes 294920 | tf_op jit(solution)/shard_map/ppermute | solution.py:28
  58.9 6.0 %collective-permute-start.6 = (bf16[2,128,384]{2,1,0:T(8,128)(2,1)S(1)}, bf16[2,128,384]{2,1,0:T(8,128)(2,1)S(1)}, u32[]{:S(2)}, u32[]{:S(2)}) collective-permute-start(bf16[2,128,384]{2,1,0:T(8,128)(2,1)S(1)} %slice.161), channel_id=1, source_target_pairs={{0,4},{2,6},{4,0},{6,2},{8,12},{10,14},{12,8},{14,10},{1,5},{3,7},... | collective-permute-start | bytes 589832 | tf_op jit(solution)/shard_map/ppermute | solution.py:28
  64.9 6.7 %collective-permute-start.4 = (bf16[2,128,384]{2,1,0:T(8,128)(2,1)S(1)}, bf16[2,128,384]{2,1,0:T(8,128)(2,1)S(1)}, u32[]{:S(2)}, u32[]{:S(2)}) collective-permute-start(bf16[2,128,384]{2,1,0:T(8,128)(2,1)S(1)} %slice.162), channel_id=1, source_target_pairs={{0,4},{2,6},{4,0},{6,2},{8,12},{10,14},{12,8},{14,10},{1,5},{3,7},... | collective-permute-start | bytes 589832 | tf_op jit(solution)/shard_map/ppermute | solution.py:28
  71.6 6.6 %collective-permute-start.9 = (bf16[1,128,384]{2,1,0:T(8,128)(2,1)S(1)}, bf16[1,128,384]{2,1,0:T(8,128)(2,1)S(1)}, u32[]{:S(2)}, u32[]{:S(2)}) collective-permute-start(bf16[1,128,384]{2,1,0:T(8,128)(2,1)S(1)} %slice.164), channel_id=1, source_target_pairs={{0,8},{2,10},{4,12},{6,14},{8,0},{10,2},{12,4},{14,6},{1,9},{3,11}... | collective-permute-start | bytes 294920 | tf_op jit(solution)/shard_map/ppermute | solution.py:28
  73.7 6.6 %collective-permute-start.8 = (bf16[1,128,384]{2,1,0:T(8,128)(2,1)S(1)}, bf16[1,128,384]{2,1,0:T(8,128)(2,1)S(1)}, u32[]{:S(2)}, u32[]{:S(2)}) collective-permute-start(bf16[1,128,384]{2,1,0:T(8,128)(2,1)S(1)} %slice.165), channel_id=1, source_target_pairs={{0,8},{2,10},{4,12},{6,14},{8,0},{10,2},{12,4},{14,6},{1,9},{3,11}... | collective-permute-start | bytes 294920 | tf_op jit(solution)/shard_map/ppermute | solution.py:28
  77.4 3.0 %copy-start.7 = (bf16[1,128,384]{2,1,0:T(8,128)(2,1)}, bf16[1,128,384]{2,1,0:T(8,128)(2,1)S(1)}, u32[]{:S(2)}) copy-start(bf16[1,128,384]{2,1,0:T(8,128)(2,1)S(1)} %collective-permute-done.7.refs_3_) | copy-start | bytes 294916
  78.2 2.2 %copy-start.8 = (bf16[1,128,384]{2,1,0:T(8,128)(2,1)}, bf16[1,128,384]{2,1,0:T(8,128)(2,1)S(1)}, u32[]{:S(2)}) copy-start(bf16[1,128,384]{2,1,0:T(8,128)(2,1)S(1)} %collective-permute-done.9.refs_5_) | copy-start | bytes 294916
  80.3 0.6 copy-start.9
  84.6 1.5 %collective-permute-start.15 = (bf16[256,128]{1,0:T(8,128)(2,1)}, bf16[256,128]{1,0:T(8,128)(2,1)S(1)}, u32[]{:S(2)}, u32[]{:S(2)}) collective-permute-start(bf16[256,128]{1,0:T(8,128)(2,1)} %get-tuple-element.20), channel_id=1, source_target_pairs={{0,1},{1,0},{2,3},{3,2},{4,5},{5,4},{6,7},{7,6},{8,9},{9,8},{10,11... | collective-permute-start | bytes 196616 | tf_op jit(solution)/shard_map/ppermute | solution.py:32
  87.8 7.9 %collective-permute-start.16 = (bf16[448,128]{1,0:T(8,128)(2,1)S(1)}, bf16[448,128]{1,0:T(8,128)(2,1)S(1)}, u32[]{:S(2)}, u32[]{:S(2)}) collective-permute-start(bf16[448,128]{1,0:T(8,128)(2,1)S(1)} %pad_maximum_fusion.4), channel_id=1, source_target_pairs={{0,8},{2,10},{4,12},{6,14},{8,0},{10,2},{12,4},{14,6},{1,9},{3,11}... | collective-permute-start | bytes 344072 | tf_op jit(solution)/shard_map/ppermute | solution.py:28
  96.5 5.9 %collective-permute-start.17 = (bf16[576,128]{1,0:T(8,128)(2,1)S(1)}, bf16[576,128]{1,0:T(8,128)(2,1)S(1)}, u32[]{:S(2)}, u32[]{:S(2)}) collective-permute-start(bf16[576,128]{1,0:T(8,128)(2,1)S(1)} %pad_maximum_fusion.3), channel_id=1, source_target_pairs={{0,4},{2,6},{4,0},{6,2},{8,12},{10,14},{12,8},{14,10},{1,5},{3,7},... | collective-permute-start | bytes 442376 | tf_op jit(solution)/shard_map/ppermute | solution.py:28
  103.2 6.4 %collective-permute-start.18 = (bf16[832,128]{1,0:T(8,128)(2,1)S(1)}, bf16[832,128]{1,0:T(8,128)(2,1)S(1)}, u32[]{:S(2)}, u32[]{:S(2)}) collective-permute-start(bf16[832,128]{1,0:T(8,128)(2,1)S(1)} %pad_maximum_fusion.1), channel_id=1, source_target_pairs={{0,2},{2,0},{4,6},{6,4},{8,10},{10,8},{12,14},{14,12},{1,3},{3,1},... | collective-permute-start | bytes 638984 | tf_op jit(solution)/shard_map/ppermute | solution.py:28
  111.8 3.6 %copy-start.10 = (f32[128,1]{1,0:T(8,128)S(1)}, f32[128,1]{1,0:T(8,128)}, u32[]{:S(2)}) copy-start(f32[128,1]{1,0:T(8,128)} %get-tuple-element.21) | copy-start | bytes 1540
  115.3 5.7 %collective-permute-start.19 = (f32[512,128]{1,0:T(8,128)}, f32[512,128]{1,0:T(8,128)S(1)}, u32[]{:S(2)}, u32[]{:S(2)}) collective-permute-start(f32[512,128]{1,0:T(8,128)} %final.3), channel_id=1, source_target_pairs={{0,1},{1,0},{2,3},{3,2},{4,5},{5,4},{6,7},{7,6},{8,9},{9,8},{10,11... | collective-permute-start | bytes 786440 | tf_op jit(solution)/shard_map/ppermute | solution.py:32
  115.5 1.6 %collective-permute-start.20 = (f32[1,128]{1,0:T(1,128)S(1)}, f32[1,128]{1,0:T(1,128)S(1)}, u32[]{:S(2)}, u32[]{:S(2)}) collective-permute-start(f32[1,128]{1,0:T(1,128)S(1)} %bitcast.44), channel_id=1, source_target_pairs={{0,1},{1,0},{2,3},{3,2},{4,5},{5,4},{6,7},{7,6},{8,9},{9,8},{10,11... | collective-permute-start | bytes 1544 | tf_op jit(solution)/shard_map/ppermute | solution.py:32

commit v2 on v1

v2 whole, which is shorter than its diff:
```python
import functools
import math

import jax
import jax.numpy as jnp
from jax import lax
from jax.experimental import pallas as pl
from jax.experimental.pallas import tpu as pltpu
from jax.sharding import PartitionSpec as P

EPSILON = 1e-05
HARD_WEIGHT = 0.5
ROPE_BASE = 10000.0
LANES = 128
F32 = jnp.float32
BF16 = jnp.bfloat16
PAIR = [(0, 1), (1, 0)]
VMEM = pl.BlockSpec(memory_space=pltpu.VMEM)
ANY = pl.BlockSpec(memory_space=pl.ANY)


def mirrored(place, bits):
    out = 0
    for bit in range(bits):
        out = out | (((place >> bit) & 1) << (bits - 1 - bit))
    return out


def swap_with(value, bit, count):
    return lax.ppermute(value, "seq", [(i, i ^ bit) for i in range(count)])


def swap_cores(value):
    return lax.ppermute(value, "vocab", PAIR)


def mm(lhs, rhs, lhs_dim, rhs_dim):
    return lax.dot_general(
        lhs, rhs, (((lhs_dim,), (rhs_dim,)), ((), ())), preferred_element_type=F32
    )


def block_products(here, bits, block, chunks, x_ref, table_ref, outs):
    quarter = 1 << (bits - 2)
    if quarter <= 2:
        group, merged = quarter, ((2, 3), (0, 1))
    else:
        group, merged = 4, ((2,), (3,), (0,), (1,))
    for quarters in merged:

        def body(step, carry, quarters=quarters):
            rows = []
            for part in quarters:
                for offset in range(group):
                    owner = mirrored(part * quarter + step * group + offset, bits) ^ here
                    rows.append(x_ref[pl.ds(pl.multiple_of(owner * block, block), block), :])
            product = mm(jnp.concatenate(rows, axis=0), table_ref[...], 1, 1)
            product = product.reshape(len(quarters), group, block, product.shape[1])
            for slot, part in enumerate(quarters):
                for (first, width, flip), (send_ref, keep_ref) in zip(chunks, outs):
                    place = (part >> 1) | ((part & 1) << 1) if flip else part
                    out_ref = send_ref if place >= 2 else keep_ref
                    out_ref[pl.ds((place & 1) * quarter + step * group, group)] = product[
                        slot, :, :, first : first + width
                    ].astype(out_ref.dtype)
            return carry

        if group == quarter:
            body(0, 0)
        else:
            lax.fori_loop(0, quarter // group, body, 0)


def chunk_shapes(chunks, count, block):
    return [
        jax.ShapeDtypeStruct((count // 2, block, width), kind)
        for _, width, _ in chunks
        for kind in (BF16, F32)
    ]


def own_kernel(bits, block, chunks, x_hbm, head_hbm, in_hbm, out_hbm, gain_in_ref, gain_out_ref, *refs):
    outs, scaled_ref = refs[: 2 * len(chunks)], refs[2 * len(chunks)]
    x_ref, head_ref, small_ref, table_ref, sems = refs[2 * len(chunks) + 1 :]
    here = lax.axis_index("seq")
    columns = x_ref.shape[1]
    rank = in_hbm.shape[0]
    mine = pl.ds(pl.multiple_of(here * columns, LANES), columns)
    copies = [
        pltpu.make_async_copy(head_hbm.at[:, mine], head_ref, sems.at[0]),
        pltpu.make_async_copy(in_hbm.at[:, mine], small_ref.at[:rank], sems.at[1]),
        pltpu.make_async_copy(out_hbm.at[:, mine], small_ref.at[rank:], sems.at[2]),
        pltpu.make_async_copy(x_hbm, x_ref, sems.at[3]),
    ]
    for copy in copies:
        copy.start()
    gain_in = gain_in_ref[:, mine].astype(F32)
    gain_both = gain_in * gain_out_ref[:, mine].astype(F32)
    copies[0].wait()
    scaled_ref[...] = (head_ref[...].astype(F32) * gain_both).astype(BF16)
    table_ref[2 * rank :, :] = scaled_ref[...]
    copies[1].wait()
    copies[2].wait()
    table_ref[: 2 * rank, :] = (small_ref[...].astype(F32) * gain_in).astype(BF16)
    copies[3].wait()
    pairs = list(zip(outs[0::2], outs[1::2]))
    block_products(here, bits, block, chunks, x_ref, table_ref, pairs)


def own_products(x, head, w_in, w_out, in_row, out_row, chunks, count, block):
    bits = count.bit_length() - 1
    columns = x.shape[1]
    width = sum(chunk[1] for chunk in chunks)
    shapes = chunk_shapes(chunks, count, block)
    shapes.append(jax.ShapeDtypeStruct((head.shape[0], columns), BF16))
    return pl.pallas_call(
        functools.partial(own_kernel, bits, block, chunks),
        in_specs=[ANY] * 4 + [VMEM] * 2,
        out_specs=[VMEM] * len(shapes),
        out_shape=shapes,
        scratch_shapes=[
            pltpu.VMEM(x.shape, BF16),
            pltpu.VMEM((head.shape[0], columns), BF16),
            pltpu.VMEM((2 * w_in.shape[0], columns), BF16),
            pltpu.VMEM((width, columns), BF16),
            pltpu.SemaphoreType.DMA((4,)),
        ],
        cost_estimate=pl.CostEstimate(
            flops=2 * x.shape[0] * columns * width,
            bytes_accessed=2 * x.shape[0] * columns + 2 * width * columns,
            transcendentals=0,
        ),
        name="own_products",
    )(x, head, w_in, w_out, in_row, out_row)


def far_kernel(bits, block, chunks, x_ref, table_ref, *outs):
    pairs = list(zip(outs[0::2], outs[1::2]))
    block_products(lax.axis_index("seq"), bits, block, chunks, x_ref, table_ref, pairs)


def far_products(x, table, chunks, count, block):
    bits = count.bit_length() - 1
    shapes = chunk_shapes(chunks, count, block)
    return pl.pallas_call(
        functools.partial(far_kernel, bits, block, chunks),
        in_specs=[VMEM] * 2,
        out_specs=[VMEM] * len(shapes),
        out_shape=shapes,
        cost_estimate=pl.CostEstimate(
            flops=2 * x.shape[0] * x.shape[1] * table.shape[0],
            bytes_accessed=2 * x.shape[0] * x.shape[1] + 2 * table.shape[0] * x.shape[1],
            transcendentals=0,
        ),
        name="far_products",
    )(x, table)


def owner_kernel(depth, slots, chunks, *refs):
    keeps, gots = refs[:chunks], refs[chunks : 2 * chunks]
    stats_ref, marks_ref, turn_ref, own_t_ref, far_t_ref, own_h_ref, far_h_ref, gram_ref = refs[
        2 * chunks : 2 * chunks + 8
    ]
    factor_ref, table_ref, away_ref, gram_out_ref = refs[2 * chunks + 8 :]
    sums = [None] * chunks
    for slot, keep, got in zip(slots, keeps, gots):
        sums[slot] = keep[0] + got[0].astype(F32)
    rank2 = LANES
    rank = rank2 // 2
    half = rank // 2
    raw_latent = sums[0][:, :rank]
    raw_cross = sums[0][:, rank:rank2]
    raw_logits = jnp.concatenate([sums[0][:, rank2:]] + sums[1:], axis=1)
    inverse_in = lax.rsqrt(stats_ref[:, 0:1] * (1.0 / depth) + EPSILON)
    latent = raw_latent * inverse_in
    cosine = turn_ref[:, :rank]
    sine = turn_ref[:, rank:rank2]

    def swapped(value):
        return jnp.concatenate([value[:, half:], value[:, :half]], axis=1)

    turned = latent * cosine + swapped(latent) * sine
    sigmoid = 1.0 / (1.0 + jnp.exp(-turned))
    active = (turned * sigmoid).astype(BF16)
    active_wide = active.astype(F32)
    gram_part = mm(active, gram_ref[...].astype(BF16), 1, 0)
    cross = raw_cross * inverse_in
    square = (
        inverse_in * inverse_in * stats_ref[:, 1:2]
        + jnp.sum(active_wide * (2.0 * cross + gram_part), axis=1, keepdims=True)
    )
    inverse_out = lax.rsqrt(jnp.maximum(square, 0.0) * (1.0 / depth) + EPSILON)
    head_out = jnp.concatenate([own_h_ref[...], far_h_ref[...]], axis=1)
    head_high = head_out.astype(BF16)
    head_low = (head_out - head_high.astype(F32)).astype(BF16)
    logits = inverse_out * (
        raw_logits * inverse_in + (mm(active, head_high, 1, 0) + mm(active, head_low, 1, 0))
    )
    teacher = jnp.concatenate([own_t_ref[...], far_t_ref[...]], axis=1).astype(F32)
    student_top = jnp.max(logits, axis=1, keepdims=True)
    student = jnp.exp(logits - student_top)
    student_total = jnp.sum(student, axis=1, keepdims=True)
    student_lse = student_top + jnp.log(student_total)
    teacher_top = jnp.max(teacher, axis=1, keepdims=True)
    weight = jnp.exp(teacher - teacher_top)
    teacher_total = jnp.sum(weight, axis=1, keepdims=True)
    teacher_lse = teacher_top + jnp.log(teacher_total)
    prob_teacher = weight * (1.0 / teacher_total)
    prob_student = student * (1.0 / student_total)
    hits = lax.broadcasted_iota(jnp.int32, logits.shape, 1) == marks_ref[:, 0:1]
    picked = jnp.sum(jnp.where(hits, logits, 0.0), axis=1, keepdims=True)
    mask = marks_ref[:, 1:2].astype(F32)
    overlap = jnp.sum(prob_teacher * (teacher - logits), axis=1, keepdims=True)
    loss = mask * (overlap - teacher_lse + student_lse + HARD_WEIGHT * (student_lse - picked))
    grad_logits = (
        mask
        * (
            prob_student
            - prob_teacher
            + HARD_WEIGHT * (prob_student - jnp.where(hits, 1.0, 0.0))
        )
    ).astype(BF16)
    mean = jnp.sum(grad_logits.astype(F32) * logits, axis=1, keepdims=True) * (1.0 / depth)
    through = mm(grad_logits, head_high, 1, 1) + mm(grad_logits, head_low, 1, 1)
    grad_active = inverse_out * (through - mean * inverse_out * (cross + gram_part))
    grad_turned = grad_active * sigmoid * (1.0 + turned * (1.0 - sigmoid))
    grad_latent = grad_turned * cosine - swapped(grad_turned) * sine
    weight_back = -inverse_out * inverse_out * mean
    factor_ref[...] = jnp.concatenate(
        [inverse_in * grad_latent, (inverse_in * weight_back) * active_wide], axis=1
    ).astype(BF16)
    table = mm((inverse_out * active_wide).astype(BF16), grad_logits, 0, 0)
    slice_width = own_h_ref.shape[1]
    parts = slice_width // LANES
    for part in range(parts):
        table_ref[part * rank : (part + 1) * rank, :] = table[:, part * LANES : (part + 1) * LANES]
        away_ref[part * rank : (part + 1) * rank, :] = table[
            :, slice_width + part * LANES : slice_width + (part + 1) * LANES
        ]
    lines = jnp.broadcast_to(loss, (loss.shape[0], LANES)).T[:8]
    table_ref[parts * rank :, :] = lines
    away_ref[parts * rank :, :] = lines
    own_gram = mm((weight_back * active_wide).astype(BF16), active, 0, 0)
    gram_out_ref[...] = jnp.concatenate([own_gram[:half], own_gram[half:]], axis=1).astype(BF16)


def owner_step(depth, rank, slots, keeps, gots, stats, marks, turn, teachers, heads, gram):
    block = stats.shape[0]
    rows = heads[0].shape[1] // LANES * rank + 8
    operands = [*keeps, *gots, stats, marks, turn, *teachers, *heads, gram]
    return pl.pallas_call(
        functools.partial(owner_kernel, depth, slots, len(keeps)),
        in_specs=[VMEM] * len(operands),
        out_specs=[VMEM] * 4,
        out_shape=[
            jax.ShapeDtypeStruct((block, 2 * rank), BF16),
            jax.ShapeDtypeStruct((rows, block), F32),
            jax.ShapeDtypeStruct((rows, block), F32),
            jax.ShapeDtypeStruct((rank // 2, 2 * rank), BF16),
        ],
        name="owner",
    )(*operands)


def final_kernel(bits, block, rank, x_ref, head_hbm, out_hbm, gain_in_ref, gain_out_ref, mine_ref,
                 got_ref, out_ref, head_ref, small_ref, order_ref, sems):
    here = lax.axis_index("seq")
    columns = x_ref.shape[1]
    mine = pl.ds(pl.multiple_of(here * columns, LANES), columns)
    copies = [
        pltpu.make_async_copy(head_hbm.at[:, mine], head_ref, sems.at[0]),
        pltpu.make_async_copy(out_hbm.at[:, mine], small_ref, sems.at[1]),
    ]
    for copy in copies:
        copy.start()
    half = 1 << (bits - 1)
    for base, source in ((0, mine_ref), (half, got_ref)):

        def body(place, carry, base=base, source=source):
            owner = mirrored(base + place, bits) ^ here
            order_ref[pl.ds(pl.multiple_of(owner * block, block), block), :] = source[
                pl.ds(pl.multiple_of(place * block, block), block), :
            ]
            return carry

        if half <= 8:
            for place in range(half):
                body(place, 0)
        else:
            lax.fori_loop(0, half, body, 0)
    parts = head_ref.shape[0] // LANES
    rows = half * block
    summed = mine_ref[rows:, :].astype(F32) + got_ref[rows:, :].astype(F32)
    table = jnp.concatenate(
        [summed[part * rank : (part + 1) * rank, :] for part in range(parts)], axis=1
    ).astype(BF16)
    packed = summed[parts * rank :, :]
    gram = jnp.concatenate([packed[:, :rank], packed[:, rank:]], axis=0).astype(BF16)
    from_x = mm(order_ref[...], x_ref[...], 0, 0) * gain_in_ref[:, mine].astype(F32)
    for copy in copies:
        copy.wait()
    from_head = mm(table, head_ref[...], 1, 0) * gain_out_ref[:, mine].astype(F32)
    from_out = mm(gram, small_ref[...], 1, 0)
    total = jnp.concatenate([from_x[:rank], from_x[rank:] + from_head + from_out], axis=0)
    out_ref[...] = total.T


def final_step(x, head, w_out, in_row, out_row, mine, got, count, block):
    bits = count.bit_length() - 1
    columns = x.shape[1]
    rank = w_out.shape[0]
    return pl.pallas_call(
        functools.partial(final_kernel, bits, block, rank),
        in_specs=[VMEM, ANY, ANY, VMEM, VMEM, VMEM, VMEM],
        out_specs=VMEM,
        out_shape=jax.ShapeDtypeStruct((columns, 2 * rank), F32),
        scratch_shapes=[
            pltpu.VMEM((head.shape[0], columns), BF16),
            pltpu.VMEM((rank, columns), BF16),
            pltpu.VMEM((x.shape[0], 2 * rank), BF16),
            pltpu.SemaphoreType.DMA((2,)),
        ],
        name="final",
    )(x, head, w_out, in_row, out_row, mine, got)


def on_device(
    features, positions, token_ids, valid, teacher_logits, in_gain, final_gain, w_in, w_out, head
):
    count = lax.axis_size("seq")
    bits = count.bit_length() - 1
    here = lax.axis_index("seq")
    core = lax.axis_index("vocab")
    x = features[0]
    block = x.shape[0] // count
    columns = x.shape[1]
    rank, depth = w_in.shape
    half = rank // 2
    slice_width = head.shape[0]
    vocabulary = 2 * slice_width
    in_row, out_row = in_gain.reshape(1, depth), final_gain.reshape(1, depth)

    width = 2 * rank + slice_width
    early = [(0, width - 256, False), (width - 256, 256, True)]
    late = [(0, slice_width // 2, False), (slice_width // 2, slice_width // 2, False)]
    made = own_products(x, head, w_in, w_out, in_row, out_row, early, count, block)
    far_table = swap_cores(made[-1])
    more = far_products(x, far_table, late, count, block)
    sends = [made[0], made[2], more[0], more[2]]
    keeps = [made[1], made[3], more[1], more[3]]
    flips = [chunk[2] for chunk in early + late]

    x_late, late_args, more = lax.optimization_barrier(
        (x, (positions, token_ids, valid, teacher_logits, in_gain, final_gain, w_out, head), more)
    )
    positions, token_ids, valid, teacher_logits, in_gain, final_gain, w_late, head_late = late_args
    in_wide, final_wide = in_gain.astype(F32), final_gain.astype(F32)
    squares = jnp.square(x_late.astype(F32))
    in_columns = lax.dynamic_slice_in_dim(in_wide, here * columns, columns, axis=0)
    sums = jnp.stack([jnp.sum(squares, axis=1), jnp.sum(squares * jnp.square(in_columns), axis=1)])
    order = jnp.array([mirrored(place, bits) for place in range(count)], jnp.int32) ^ here
    stats = jnp.take(sums.reshape(2, count, block), order, axis=1)
    own_teacher = lax.dynamic_index_in_dim(teacher_logits, core, 0, keepdims=False)
    far_teacher = swap_cores(lax.dynamic_index_in_dim(teacher_logits, 1 - core, 0, keepdims=False))

    scaled_out = (w_late.astype(F32) * final_wide).astype(BF16)
    own_out = mm(scaled_out, head_late, 1, 1)
    far_out = swap_cores(own_out)
    gram = mm(w_late, w_late, 1, 1)

    freqs = jnp.exp(-math.log(ROPE_BASE) * jnp.arange(half, dtype=F32) / half)
    angles = positions[0].astype(F32)[:, None] * freqs[None, :]
    cosine, sine = jnp.cos(angles), jnp.sin(angles)
    turn = jnp.concatenate([cosine, cosine, -sine, sine], axis=1)
    labels = lax.dynamic_index_in_dim(token_ids, core, 0, keepdims=False)
    labels = lax.rem(labels + core * slice_width, vocabulary)
    marks = jnp.stack([labels, lax.dynamic_index_in_dim(valid, core, 0, keepdims=False)], axis=1)

    for step in range(bits):
        gots = [
            swap_with(send, (1 << (1 - step if flip and step < 2 else step)), count)
            for send, flip in zip(sends, flips)
        ]
        left = count >> (step + 1)
        stats = stats[:, :left] + swap_with(stats[:, left:], 1 << step, count)
        if step == bits - 1:
            break
        keeps = [keep[:left] + got.astype(F32) for keep, got in zip(keeps, gots)]
        sends = [value[left // 2 :].astype(BF16) for value in keeps]

    factor, table, away, gram_out = owner_step(
        depth, rank, (0, 1, 2, 3), keeps, gots, stats[:, 0].T, marks, turn,
        (own_teacher, far_teacher), (own_out, far_out), gram,
    )
    got = swap_cores(away)
    rows = table.shape[0] - 8
    payload = jnp.concatenate([factor, (table[:rows] + got[:rows]).astype(BF16), gram_out])
    own_loss, far_loss = table[rows : rows + 1], got[rows : rows + 1]
    row_loss = jnp.where(
        core == 0,
        jnp.concatenate([own_loss, far_loss]),
        jnp.concatenate([far_loss, own_loss]),
    )
    split = block
    for step in reversed(range(bits)):
        got = swap_with(payload, 1 << step, count)
        if step:
            added = payload[split:].astype(F32) + got[split:].astype(F32)
            payload = jnp.concatenate([payload[:split], got[:split], added.astype(BF16)])
            split *= 2
            if step == 1:
                payload, row_loss = lax.optimization_barrier((payload, row_loss))

    both = final_step(x, head, w_out, in_row, out_row, payload, got, count, block)
    near = lax.dynamic_slice_in_dim(both, core * (columns // 2), columns // 2, axis=0)
    away = lax.dynamic_slice_in_dim(both, (1 - core) * (columns // 2), columns // 2, axis=0)
    return (near + swap_cores(away), row_loss)


def solution(mesh):
    placed = (
        P("vocab", "groups", "seq"),
        P("vocab", ("groups", "seq")),
        P(None, ("groups", "seq")),
        P(None, ("groups", "seq")),
        P(None, ("groups", "seq"), "vocab"),
        P(),
        P(),
        P(),
        P(),
        P("vocab", None),
    )
    return jax.shard_map(
        on_device,
        mesh=mesh,
        in_specs=placed,
        out_specs=(P(("groups", "seq", "vocab"), None), P(None, ("groups", "seq"))),
        check_vma=False,
    )
```

time: 124 us -> 125 us (level)
  waiting for transfers between devices: 36.5 us -> 51.8 us
  Pallas kernels: 25.3 us -> 18.7 us
  starting transfers between devices: 23.2 us -> 19.2 us
  local copies, waits for them, and re-layouts: 11.5 us -> 9.4 us
  other arithmetic: 18.2 us -> 16.6 us
    ppermute x15 -> x18, waiting for transfers between devices: 34.7 us -> 48.8 us  [swap_with(): return lax.ppermute(value, 'seq', [(i, i ^ bit) for i in range(count)])]
    pallas_call x6 -> x4, Pallas kernels: 25.3 us -> 18.7 us  [the longest x1 6.08 us: own_products(): pl.pallas_call(functools.partial(own_kernel, bits, block, chunks), in_spe...]
    ppermute x15 -> x18, starting transfers between devices: 22.1 us -> 18.6 us  [swap_with(): return lax.ppermute(value, 'seq', [(i, i ^ bit) for i in range(count)])]
    reshape x0 -> x2, local copies, waits for them, and re-layouts: none -> 2.7 us  [on_device(): in_row, out_row = (in_gain.reshape(1, depth), final_gain.reshape(1, depth))]
    slice x16 -> x15, local copies, waits for them, and re-layouts: 4.33 us -> 2.15 us  [the longest x8 1.42 us: on_device(): sends = [value[left // 2:].astype(BF16) for value in keeps]]
    reduce_sum x1, other arithmetic: 2.42 us -> 0.8 us  [on_device(): jnp.sum(squares, axis=1)]
    convert_element_type x3, other arithmetic: 0.06 us -> 1.66 us  [the longest x1 0.92 us: on_device(): (table[:rows] + got[:rows]).astype(BF16)]
    concatenate x4 -> x3, other arithmetic: 3.78 us -> 2.33 us  [the longest x2 1.54 us: on_device(): jnp.concatenate([payload[:split], got[:split], added.astype(BF16)])]
  transfers between devices with their start and end apart: 21 -> 23, of which waited for: 11 -> 15; matrix products, arithmetic and copies ran while one was open for 18% -> 18% of each run, Pallas kernels for 15% -> 3%
where the time goes in v2:
time: 125 us; the launch traced here: 124 us
  waiting for transfers between devices  51.8 us (41%)
  starting transfers between devices  19.2 us (15%)
  Pallas kernels  18.7 us (15%)
  other arithmetic  16.6 us (13%)
  local copies, waits for them, and re-layouts  9.4 us (8%)
  matrix products  7.17 us (6%)
    ppermute x18, waiting for transfers between devices, swap_with(): return lax.ppermute(value, 'seq', [(i, i ^ bit) for i in range(count)])  48.8 us
    ppermute x18, starting transfers between devices, swap_with(): return lax.ppermute(value, 'seq', [(i, i ^ bit) for i in range(count)])  18.6 us
    dot_general x2, matrix products, mm(): lax.dot_general(lhs, rhs, (((lhs_dim,), (rhs_dim,)), ((), ())), preferred...  7.17 us
    pallas_call x1, Pallas kernels, own_products(): pl.pallas_call(functools.partial(own_kernel, bits, block, chunks), in_spe...  6.08 us
    pallas_call x1, Pallas kernels, final_step(): pl.pallas_call(functools.partial(final_kernel, bits, block, rank), in_spe...  4.61 us
    add x8, other arithmetic, on_device(): keeps = [keep[:left] + got.astype(F32) for keep, got in zip(keeps, gots)]  4.5 us
    pallas_call x1, Pallas kernels, far_products(): pl.pallas_call(functools.partial(far_kernel, bits, block, chunks), in_spe...  4.24 us
    pallas_call x1, Pallas kernels, owner_step(): pl.pallas_call(functools.partial(owner_kernel, depth, slots, len(keeps)),...  3.81 us
  transfers between devices with their start and end apart: 23, of which 15 were waited for; matrix products, arithmetic and copies ran while one was open for 18% of the time, Pallas kernels for 3%

profile of v2, /device:TPU:0, one launch (start us, length us, event | category | flops | bytes accessed | tf_op | source)
XLA Modules:
  0.0 124.1 jit_solution(12514180652137711316)
XLA Ops:
  0.6 1.4 %reshape.64.gain_in_ref = bf16[1,8192]{1,0:T(2,128)(2,1)} reshape(bf16[8192]{0:T(1024)(128)(2,1)} %param.16) | data formatting | bytes 32768 | tf_op jit(solution)/shard_map/reshape | solution.py:341
  2.0 1.3 %reshape.65.gain_out_ref = bf16[1,8192]{1,0:T(2,128)(2,1)} reshape(bf16[8192]{0:T(1024)(128)(2,1)} %param.17) | data formatting | bytes 32768 | tf_op jit(solution)/shard_map/reshape | solution.py:341
  3.3 6.1 %own_products.1 = (bf16[4,128,384]{2,1,0:T(8,128)(2,1)}, f32[4,128,384]{2,1,0:T(8,128)}, bf16[4,128,256]{2,1,0:T(8,128)(2,1)}, f32[4,128,256]{2,1,0:T(8,128)}, bf16[512,1024]{1,0:T(8,128)(2,1)}) custom-call(bf16[1024,1024]{1,0:T(8,128)(2,1)} %bitcast.23, bf16[512,8192]{1,0:T(8,128)(2,1)} %head_hbm.3, bf16[64,8192]{1,0:T(8,128)(2,1)} %in_hbm.1, ...), custom_call_target="tpu_custom_call" | custom-call | flops 1342177280 | bytes 3407872 | tf_op jit(solution)/shard_map/own_products/pallas_call | solution.py:116
  9.4 3.1 %collective-permute-start.2 = (bf16[4,128,256]{2,1,0:T(8,128)(2,1)}, bf16[4,128,256]{2,1,0:T(8,128)(2,1)S(1)}, u32[]{:S(2)}, u32[]{:S(2)}) collective-permute-start(bf16[4,128,256]{2,1,0:T(8,128)(2,1)} %get-tuple-element.29), channel_id=1, source_target_pairs={{0,4},{2,6},{4,0},{6,2},{8,12},{10,14},{12,8},{14,10},{1,5},{3,7},... | collective-permute-start | bytes 786440 | tf_op jit(solution)/shard_map/ppermute | solution.py:30
  12.5 1.5 %collective-permute-start = (bf16[4,128,384]{2,1,0:T(8,128)(2,1)}, bf16[4,128,384]{2,1,0:T(8,128)(2,1)S(1)}, u32[]{:S(2)}, u32[]{:S(2)}) collective-permute-start(bf16[4,128,384]{2,1,0:T(8,128)(2,1)} %get-tuple-element.27), channel_id=1, source_target_pairs={{0,2},{2,0},{4,6},{6,4},{8,10},{10,8},{12,14},{14,12},{1,3},{3,1},... | collective-permute-start | bytes 1179656 | tf_op jit(solution)/shard_map/ppermute | solution.py:30
  14.1 5.0 %collective-permute-done.2 = bf16[4,128,256]{2,1,0:T(8,128)(2,1)S(1)} collective-permute-done((bf16[4,128,256]{2,1,0:T(8,128)(2,1)}, bf16[4,128,256]{2,1,0:T(8,128)(2,1)S(1)}, u32[]{:S(2)}, u32[]{:S(2)}) %collective-permute-start.2) | collective-permute-done | bytes 262176 | tf_op jit(solution)/shard_map/ppermute | solution.py:30
  19.1 1.1 convert_add_fusion.3
  20.2 1.7 %collective-permute-start.3 = (bf16[2,128,256]{2,1,0:T(8,128)(2,1)S(1)}, bf16[2,128,256]{2,1,0:T(8,128)(2,1)S(1)}, u32[]{:S(2)}, u32[]{:S(2)}) collective-permute-start(bf16[2,128,256]{2,1,0:T(8,128)(2,1)S(1)} %slice.168), channel_id=1, source_target_pairs={{0,2},{2,0},{4,6},{6,4},{8,10},{10,8},{12,14},{14,12},{1,3},{3,1},... | collective-permute-start | bytes 393224 | tf_op jit(solution)/shard_map/ppermute | solution.py:30
  21.9 2.6 %collective-permute-done = bf16[4,128,384]{2,1,0:T(8,128)(2,1)S(1)} collective-permute-done((bf16[4,128,384]{2,1,0:T(8,128)(2,1)}, bf16[4,128,384]{2,1,0:T(8,128)(2,1)S(1)}, u32[]{:S(2)}, u32[]{:S(2)}) %collective-permute-start) | collective-permute-done | bytes 393248 | tf_op jit(solution)/shard_map/ppermute | solution.py:30
  24.5 1.2 convert_add_fusion
  26.8 2.6 %collective-permute-start.10 = (bf16[1,128,256]{2,1,0:T(8,128)(2,1)}, bf16[1,128,256]{2,1,0:T(8,128)(2,1)}, u32[]{:S(2)}, u32[]{:S(2)}) collective-permute-start(bf16[1,128,256]{2,1,0:T(8,128)(2,1)} %slice.172), channel_id=1, source_target_pairs={{0,8},{2,10},{4,12},{6,14},{8,0},{10,2},{12,4},{14,6},{1,9},{3,11}... | collective-permute-start | bytes 196616 | tf_op jit(solution)/shard_map/ppermute | solution.py:30
  29.4 4.1 %collective-permute-done.1 = bf16[2,128,384]{2,1,0:T(8,128)(2,1)S(1)} collective-permute-done((bf16[2,128,384]{2,1,0:T(8,128)(2,1)S(1)}, bf16[2,128,384]{2,1,0:T(8,128)(2,1)S(1)}, u32[]{:S(2)}, u32[]{:S(2)}) %collective-permute-start.1) | collective-permute-done | bytes 196640 | tf_op jit(solution)/shard_map/ppermute | solution.py:30
  33.5 0.7 slice.169
  34.2 1.8 %collective-permute-start.9 = (bf16[1,128,384]{2,1,0:T(8,128)(2,1)}, bf16[1,128,384]{2,1,0:T(8,128)(2,1)}, u32[]{:S(2)}, u32[]{:S(2)}) collective-permute-start(bf16[1,128,384]{2,1,0:T(8,128)(2,1)} %slice.169), channel_id=1, source_target_pairs={{0,8},{2,10},{4,12},{6,14},{8,0},{10,2},{12,4},{14,6},{1,9},{3,11}... | collective-permute-start | bytes 294920 | tf_op jit(solution)/shard_map/ppermute | solution.py:30
  36.1 4.2 %far_products.1 = (bf16[4,128,256]{2,1,0:T(8,128)(2,1)}, f32[4,128,256]{2,1,0:T(8,128)}, bf16[4,128,256]{2,1,0:T(8,128)(2,1)}, f32[4,128,256]{2,1,0:T(8,128)}) custom-call(bf16[1024,1024]{1,0:T(8,128)(2,1)} %bitcast.24, bf16[512,1024]{1,0:T(8,128)(2,1)} %collective-permute-done.4.table_ref), custom_call_target="tpu_custom_call" | custom-call | flops 1073741824 | bytes 3145728 | tf_op jit(solution)/shard_map/far_products/pallas_call | solution.py:145
  40.3 1.5 %collective-permute-start.5 = (bf16[4,128,256]{2,1,0:T(8,128)(2,1)}, bf16[4,128,256]{2,1,0:T(8,128)(2,1)}, u32[]{:S(2)}, u32[]{:S(2)}) collective-permute-start(bf16[4,128,256]{2,1,0:T(8,128)(2,1)} %get-tuple-element.32), channel_id=1, source_target_pairs={{0,2},{2,0},{4,6},{6,4},{8,10},{10,8},{12,14},{14,12},{1,3},{3,1},... | collective-permute-start | bytes 786440 | tf_op jit(solution)/shard_map/ppermute | solution.py:30
  42.3 1.2 convert_bitcast_fusion
  43.5 1.3 %convert_element_type.91 = f32[8192]{0:T(1024)} convert(bf16[8192]{0:T(1024)(128)(2,1)} %param.17) | non-fusion elementwise | flops 8192 | bytes 49152 | tf_op jit(solution)/shard_map/convert_element_type | solution.py:357
  44.8 1.0 fusion.10.refs_15_
  45.9 0.7 convert_multiply_fusion.1
  46.6 0.8 fusion
  48.3 1.6 %collective-permute-start.13 = (f32[2,4,128]{0,2,1:T(8,128)S(1)}, f32[2,4,128]{0,2,1:T(8,128)S(1)}, u32[]{:S(2)}, u32[]{:S(2)}) collective-permute-start(f32[2,4,128]{0,2,1:T(8,128)S(1)} %slice.131), channel_id=1, source_target_pairs={{0,2},{2,0},{4,6},{6,4},{8,10},{10,8},{12,14},{14,12},{1,3},{3,1},... | collective-permute-start | bytes 12296 | tf_op jit(solution)/shard_map/ppermute | solution.py:30
  49.9 6.1 %fusion.1.refs_13_ = f32[64,512]{1,0:T(8,128)S(1)} fusion(bf16[512,8192]{1,0:T(8,128)(2,1)} %head_hbm.3, bf16[64,8192]{1,0:T(8,128)(2,1)S(1)} %copy-done.1, f32[8192]{0:T(1024)} %convert_element_type.91), kind=kOutput, calls=%fused_computation.5 | convolution fusion | flops 538443776 | bytes 9601024 | tf_op jit(solution)/shard_map/dot_general | solution.py:38
  57.1 0.8 pad_maximum_fusion.3.refs_10_
  58.0 0.7 copy.32.refs_9_
  58.7 4.2 %collective-permute-done.14 = f32[2,2,128]{0,2,1:T(8,128)S(1)} collective-permute-done((f32[2,2,128]{0,2,1:T(8,128)S(1)}, f32[2,2,128]{0,2,1:T(8,128)S(1)}, u32[]{:S(2)}, u32[]{:S(2)}) %collective-permute-start.14) | collective-permute-done | bytes 2080 | tf_op jit(solution)/shard_map/ppermute | solution.py:30
  63.6 1.0 convert_add_fusion.2
  64.7 1.0 convert_add_fusion.1
  65.8 4.4 %collective-permute-done.6 = bf16[2,128,256]{2,1,0:T(8,128)(2,1)S(1)} collective-permute-done((bf16[2,128,256]{2,1,0:T(8,128)(2,1)S(1)}, bf16[2,128,256]{2,1,0:T(8,128)(2,1)S(1)}, u32[]{:S(2)}, u32[]{:S(2)}) %collective-permute-start.6) | collective-permute-done | bytes 131104 | tf_op jit(solution)/shard_map/ppermute | solution.py:30
  70.4 4.6 %collective-permute-done.8 = bf16[2,128,256]{2,1,0:T(8,128)(2,1)S(1)} collective-permute-done((bf16[2,128,256]{2,1,0:T(8,128)(2,1)S(1)}, bf16[2,128,256]{2,1,0:T(8,128)(2,1)S(1)}, u32[]{:S(2)}, u32[]{:S(2)}) %collective-permute-start.8) | collective-permute-done | bytes 131104 | tf_op jit(solution)/shard_map/ppermute | solution.py:30
  75.1 0.9 collective-permute-start.15
  76.1 2.1 %collective-permute-start.11 = (bf16[1,128,256]{2,1,0:T(8,128)(2,1)S(1)}, bf16[1,128,256]{2,1,0:T(8,128)(2,1)S(1)}, u32[]{:S(2)}, u32[]{:S(2)}) collective-permute-start(bf16[1,128,256]{2,1,0:T(8,128)(2,1)S(1)} %slice.171), channel_id=1, source_target_pairs={{0,8},{2,10},{4,12},{6,14},{8,0},{10,2},{12,4},{14,6},{1,9},{3,11}... | collective-permute-start | bytes 196616 | tf_op jit(solution)/shard_map/ppermute | solution.py:30
  78.2 4.2 %collective-permute-done.15 = f32[2,1,128]{0,2,1:T(8,128)S(1)} collective-permute-done((f32[2,1,128]{0,2,1:T(8,128)S(1)}, f32[2,1,128]{0,2,1:T(8,128)S(1)}, u32[]{:S(2)}, u32[]{:S(2)}) %collective-permute-start.15) | collective-permute-done | bytes 1056 | tf_op jit(solution)/shard_map/ppermute | solution.py:30
  83.6 4.0 %collective-permute-done.12.refs_7_ = bf16[1,128,256]{2,1,0:T(8,128)(2,1)S(1)} collective-permute-done((bf16[1,128,256]{2,1,0:T(8,128)(2,1)S(1)}, bf16[1,128,256]{2,1,0:T(8,128)(2,1)S(1)}, u32[]{:S(2)}, u32[]{:S(2)}) %collective-permute-start.12) | collective-permute-done | bytes 65568 | tf_op jit(solution)/shard_map/ppermute | solution.py:30
  88.2 3.8 %owner.1 = (bf16[128,128]{1,0:T(8,128)(2,1)}, f32[264,128]{1,0:T(8,128)}, f32[264,128]{1,0:T(8,128)}, bf16[32,128]{1,0:T(8,128)(2,1)}) custom-call(f32[2,128,384]{2,1,0:T(8,128)} %copy-done.3, f32[2,128,256]{2,1,0:T(8,128)} %copy-done.4, f32[2,128,256]{2,1,0:T(8,128)} %copy-done.5, f32[2,128,256]{2,1,0:T(8,128)} %copy-done.6, ...), custom_call_target="tpu_custom_call" | custom-call | tf_op jit(solution)/shard_map/owner/pallas_call | solution.py:251
  92.0 1.6 %collective-permute-done.18 = f32[264,128]{1,0:T(8,128)S(1)} collective-permute-done((f32[264,128]{1,0:T(8,128)}, f32[264,128]{1,0:T(8,128)S(1)}, u32[]{:S(2)}, u32[]{:S(2)}) %collective-permute-start.18) | collective-permute-done | bytes 135200 | tf_op jit(solution)/shard_map/ppermute | solution.py:34
  93.6 0.9 fusion.3
  94.5 0.8 pad_maximum_fusion.2
  95.3 5.9 %collective-permute-done.19 = bf16[416,128]{1,0:T(8,128)(2,1)S(1)} collective-permute-done((bf16[416,128]{1,0:T(8,128)(2,1)S(1)}, bf16[416,128]{1,0:T(8,128)(2,1)S(1)}, u32[]{:S(2)}, u32[]{:S(2)}) %collective-permute-start.19) | collective-permute-done | bytes 106528 | tf_op jit(solution)/shard_map/ppermute | solution.py:30
  101.3 0.7 add_convert_fusion.1
  102.0 0.8 pad_maximum_fusion.1
  104.1 3.8 %collective-permute-done.20 = bf16[544,128]{1,0:T(8,128)(2,1)S(1)} collective-permute-done((bf16[544,128]{1,0:T(8,128)(2,1)S(1)}, bf16[544,128]{1,0:T(8,128)(2,1)S(1)}, u32[]{:S(2)}, u32[]{:S(2)}) %collective-permute-start.20) | collective-permute-done | bytes 139296 | tf_op jit(solution)/shard_map/ppermute | solution.py:30
  107.9 0.8 pad_maximum_fusion.mine_ref
  109.3 5.2 %collective-permute-done.21.got_ref = bf16[800,128]{1,0:T(8,128)(2,1)S(1)} collective-permute-done((bf16[800,128]{1,0:T(8,128)(2,1)S(1)}, bf16[800,128]{1,0:T(8,128)(2,1)S(1)}, u32[]{:S(2)}, u32[]{:S(2)}) %collective-permute-start.21) | collective-permute-done | bytes 204832 | tf_op jit(solution)/shard_map/ppermute | solution.py:30
  115.2 4.6 %final.1 = f32[1024,128]{1,0:T(8,128)} custom-call(bf16[1024,1024]{1,0:T(8,128)(2,1)} %bitcast.25, bf16[512,8192]{1,0:T(8,128)(2,1)} %head_hbm.3, bf16[64,8192]{1,0:T(8,128)(2,1)} %out_hbm.3, bf16[1,8192]{1,0:T(2,128)(2,1)} %reshape.64.gain_in_ref, bf16[1,8192]{1,0:T(2,128)(2,1)} %reshape.65.gain_out_ref, bf16[800,128]{1,0:T(8,128)(2,1)} %copy-done.7, ...), custom_call_target="tpu_custom_call" | custom-call | tf_op jit(solution)/shard_map/final/pallas_call | solution.py:312
  119.8 1.0 constant_dynamic-slice_fusion
  120.9 1.5 %collective-permute-done.22 = f32[512,128]{1,0:T(8,128)S(1)} collective-permute-done((f32[512,128]{1,0:T(8,128)S(1)}, f32[512,128]{1,0:T(8,128)S(1)}, u32[]{:S(2)}, u32[]{:S(2)}) %collective-permute-start.22) | collective-permute-done | bytes 262176 | tf_op jit(solution)/shard_map/ppermute | solution.py:34
  122.4 1.7 %dynamic-slice_add_fusion = f32[512,128]{1,0:T(8,128)} fusion(f32[512,128]{1,0:T(8,128)S(1)} %collective-permute-done.22, f32[1024,128]{1,0:T(8,128)} %final.1, s32[]{:T(128)S(6)} %select_n.43), kind=kLoop, calls=%fused_computation.20 | loop fusion | flops 65536 | bytes 786436 | tf_op jit(solution)/shard_map/add | solution.py:417
  (99 shorter events, 9.4 us)
Async XLA Ops:
  0.6 49.2 %copy-start = (s32[2,128]{1,0:T(2,128)S(1)}, s32[2,128]{1,0:T(2,128)}, u32[]{:S(2)}) copy-start(s32[2,128]{1,0:T(2,128)} %param.14) | copy-start | bytes 3076
  3.3 10.7 %copy-start.18 = (s32[8]{0:T(128)S(1)}, s32[8]{0:T(128)}, u32[]{:S(2)}) copy-start(s32[8]{0:T(128)} %constant.61.clone) | copy-start | bytes 100
  9.4 9.6 %collective-permute-start.2 = (bf16[4,128,256]{2,1,0:T(8,128)(2,1)}, bf16[4,128,256]{2,1,0:T(8,128)(2,1)S(1)}, u32[]{:S(2)}, u32[]{:S(2)}) collective-permute-start(bf16[4,128,256]{2,1,0:T(8,128)(2,1)} %get-tuple-element.29), channel_id=1, source_target_pairs={{0,4},{2,6},{4,0},{6,2},{8,12},{10,14},{12,8},{14,10},{1,5},{3,7},... | collective-permute-start | bytes 786440 | tf_op jit(solution)/shard_map/ppermute | solution.py:30
  12.5 12.0 %collective-permute-start = (bf16[4,128,384]{2,1,0:T(8,128)(2,1)}, bf16[4,128,384]{2,1,0:T(8,128)(2,1)S(1)}, u32[]{:S(2)}, u32[]{:S(2)}) collective-permute-start(bf16[4,128,384]{2,1,0:T(8,128)(2,1)} %get-tuple-element.27), channel_id=1, source_target_pairs={{0,2},{2,0},{4,6},{6,4},{8,10},{10,8},{12,14},{14,12},{1,3},{3,1},... | collective-permute-start | bytes 1179656 | tf_op jit(solution)/shard_map/ppermute | solution.py:30
  14.0 22.0 %collective-permute-start.4 = (bf16[512,1024]{1,0:T(8,128)(2,1)}, bf16[512,1024]{1,0:T(8,128)(2,1)}, u32[]{:S(2)}, u32[]{:S(2)}) collective-permute-start(bf16[512,1024]{1,0:T(8,128)(2,1)} %get-tuple-element.30), channel_id=1, source_target_pairs={{0,1},{1,0},{2,3},{3,2},{4,5},{5,4},{6,7},{7,6},{8,9},{9,8},{10,11... | collective-permute-start | bytes 3145736 | tf_op jit(solution)/shard_map/ppermute | solution.py:34
  20.2 24.6 %copy-start.1 = (bf16[64,8192]{1,0:T(8,128)(2,1)S(1)}, bf16[64,8192]{1,0:T(8,128)(2,1)}, u32[]{:S(2)}) copy-start(bf16[64,8192]{1,0:T(8,128)(2,1)} %out_hbm.3) | copy-start | bytes 3145732
  20.2 5.9 %collective-permute-start.3 = (bf16[2,128,256]{2,1,0:T(8,128)(2,1)S(1)}, bf16[2,128,256]{2,1,0:T(8,128)(2,1)S(1)}, u32[]{:S(2)}, u32[]{:S(2)}) collective-permute-start(bf16[2,128,256]{2,1,0:T(8,128)(2,1)S(1)} %slice.168), channel_id=1, source_target_pairs={{0,2},{2,0},{4,6},{6,4},{8,10},{10,8},{12,14},{14,12},{1,3},{3,1},... | collective-permute-start | bytes 393224 | tf_op jit(solution)/shard_map/ppermute | solution.py:30
  25.8 20.8 %copy-start.2 = (bf16[1,1024,1024]{2,1,0:T(8,128)(2,1)S(1)}, bf16[1,1024,1024]{2,1,0:T(8,128)(2,1)}, u32[]{:S(2)}) copy-start(bf16[1,1024,1024]{2,1,0:T(8,128)(2,1)} %param.11) | copy-start | bytes 6291460
  25.8 7.7 %collective-permute-start.1 = (bf16[2,128,384]{2,1,0:T(8,128)(2,1)S(1)}, bf16[2,128,384]{2,1,0:T(8,128)(2,1)S(1)}, u32[]{:S(2)}, u32[]{:S(2)}) collective-permute-start(bf16[2,128,384]{2,1,0:T(8,128)(2,1)S(1)} %slice.165), channel_id=1, source_target_pairs={{0,4},{2,6},{4,0},{6,2},{8,12},{10,14},{12,8},{14,10},{1,5},{3,7},... | collective-permute-start | bytes 589832 | tf_op jit(solution)/shard_map/ppermute | solution.py:30
  26.2 3.2 %copy-start.4 = (f32[2,128,256]{2,1,0:T(8,128)}, f32[2,128,256]{2,1,0:T(8,128)S(1)}, u32[]{:S(2)}) copy-start(f32[2,128,256]{2,1,0:T(8,128)S(1)} %slice_add_fusion.4.refs_1_) | copy-start | bytes 786436
  26.8 49.3 %collective-permute-start.10 = (bf16[1,128,256]{2,1,0:T(8,128)(2,1)}, bf16[1,128,256]{2,1,0:T(8,128)(2,1)}, u32[]{:S(2)}, u32[]{:S(2)}) collective-permute-start(bf16[1,128,256]{2,1,0:T(8,128)(2,1)} %slice.172), channel_id=1, source_target_pairs={{0,8},{2,10},{4,12},{6,14},{8,0},{10,2},{12,4},{14,6},{1,9},{3,11}... | collective-permute-start | bytes 196616 | tf_op jit(solution)/shard_map/ppermute | solution.py:30
  33.5 13.8 %copy-start.3 = (f32[2,128,384]{2,1,0:T(8,128)}, f32[2,128,384]{2,1,0:T(8,128)S(1)}, u32[]{:S(2)}) copy-start(f32[2,128,384]{2,1,0:T(8,128)S(1)} %slice_add_fusion.refs_0_) | copy-start | bytes 1179652
  34.2 48.8 %collective-permute-start.9 = (bf16[1,128,384]{2,1,0:T(8,128)(2,1)}, bf16[1,128,384]{2,1,0:T(8,128)(2,1)}, u32[]{:S(2)}, u32[]{:S(2)}) collective-permute-start(bf16[1,128,384]{2,1,0:T(8,128)(2,1)} %slice.169), channel_id=1, source_target_pairs={{0,8},{2,10},{4,12},{6,14},{8,0},{10,2},{12,4},{14,6},{1,9},{3,11}... | collective-permute-start | bytes 294920 | tf_op jit(solution)/shard_map/ppermute | solution.py:30
  40.3 22.7 %collective-permute-start.5 = (bf16[4,128,256]{2,1,0:T(8,128)(2,1)}, bf16[4,128,256]{2,1,0:T(8,128)(2,1)}, u32[]{:S(2)}, u32[]{:S(2)}) collective-permute-start(bf16[4,128,256]{2,1,0:T(8,128)(2,1)} %get-tuple-element.32), channel_id=1, source_target_pairs={{0,2},{2,0},{4,6},{6,4},{8,10},{10,8},{12,14},{14,12},{1,3},{3,1},... | collective-permute-start | bytes 786440 | tf_op jit(solution)/shard_map/ppermute | solution.py:30
  41.8 22.8 %collective-permute-start.7 = (bf16[4,128,256]{2,1,0:T(8,128)(2,1)}, bf16[4,128,256]{2,1,0:T(8,128)(2,1)}, u32[]{:S(2)}, u32[]{:S(2)}) collective-permute-start(bf16[4,128,256]{2,1,0:T(8,128)(2,1)} %get-tuple-element.34), channel_id=1, source_target_pairs={{0,2},{2,0},{4,6},{6,4},{8,10},{10,8},{12,14},{14,12},{1,3},{3,1},... | collective-permute-start | bytes 786440 | tf_op jit(solution)/shard_map/ppermute | solution.py:30
  48.3 9.5 %collective-permute-start.13 = (f32[2,4,128]{0,2,1:T(8,128)S(1)}, f32[2,4,128]{0,2,1:T(8,128)S(1)}, u32[]{:S(2)}, u32[]{:S(2)}) collective-permute-start(f32[2,4,128]{0,2,1:T(8,128)S(1)} %slice.131), channel_id=1, source_target_pairs={{0,2},{2,0},{4,6},{6,4},{8,10},{10,8},{12,14},{14,12},{1,3},{3,1},... | collective-permute-start | bytes 12296 | tf_op jit(solution)/shard_map/ppermute | solution.py:30
  49.9 6.2 %copy-start.17 = (f32[128]{0:T(128)S(1)}, f32[128]{0:T(128)}, u32[]{:S(2)}) copy-start(f32[128]{0:T(128)} %convert_bitcast_fusion) | copy-start | bytes 1540
  49.9 6.5 %copy-start.11 = (bf16[2,128,512]{2,1,0:T(8,128)(2,1)S(1)}, bf16[2,128,512]{2,1,0:T(8,128)(2,1)}, u32[]{:S(2)}) copy-start(bf16[2,128,512]{2,1,0:T(8,128)(2,1)} %param.15) | copy-start | bytes 786436
  49.9 7.9 %copy-start.19 = (s32[2,128]{1,0:T(2,128)S(1)}, s32[2,128]{1,0:T(2,128)}, u32[]{:S(2)}) copy-start(s32[2,128]{1,0:T(2,128)} %param.13) | copy-start | bytes 3076
  49.9 13.7 %copy-start.10 = (f32[4,128,256]{2,1,0:T(8,128)S(1)}, f32[4,128,256]{2,1,0:T(8,128)}, u32[]{:S(2)}) copy-start(f32[4,128,256]{2,1,0:T(8,128)} %get-tuple-element.31) | copy-start | bytes 1572868
  56.0 31.5 %copy-start.8 = (f32[64,512]{1,0:T(8,128)}, f32[64,512]{1,0:T(8,128)S(1)}, u32[]{:S(2)}) copy-start(f32[64,512]{1,0:T(8,128)S(1)} %fusion.1.refs_13_) | copy-start | bytes 393220
  56.1 8.7 %copy-start.9 = (f32[4,128,256]{2,1,0:T(8,128)S(1)}, f32[4,128,256]{2,1,0:T(8,128)}, u32[]{:S(2)}) copy-start(f32[4,128,256]{2,1,0:T(8,128)} %get-tuple-element.33) | copy-start | bytes 1572868
  57.9 5.0 %collective-permute-start.14 = (f32[2,2,128]{0,2,1:T(8,128)S(1)}, f32[2,2,128]{0,2,1:T(8,128)S(1)}, u32[]{:S(2)}, u32[]{:S(2)}) collective-permute-start(f32[2,2,128]{0,2,1:T(8,128)S(1)} %slice.133), channel_id=1, source_target_pairs={{0,4},{2,6},{4,0},{6,2},{8,12},{10,14},{12,8},{14,10},{1,5},{3,7},... | collective-permute-start | bytes 6152 | tf_op jit(solution)/shard_map/ppermute | solution.py:30
  63.0 20.1 %collective-permute-start.17 = (f32[64,512]{1,0:T(8,128)S(1)}, f32[64,512]{1,0:T(8,128)S(1)}, u32[]{:S(2)}, u32[]{:S(2)}) collective-permute-start(f32[64,512]{1,0:T(8,128)S(1)} %fusion.1.refs_13_), channel_id=1, source_target_pairs={{0,1},{1,0},{2,3},{3,2},{4,5},{5,4},{6,7},{7,6},{8,9},{9,8},{10,11... | collective-permute-start | bytes 393224 | tf_op jit(solution)/shard_map/ppermute | solution.py:34
  63.0 20.1 %collective-permute-start.16 = (bf16[128,512]{1,0:T(8,128)(2,1)S(1)}, bf16[128,512]{1,0:T(8,128)(2,1)S(1)}, u32[]{:S(2)}, u32[]{:S(2)}) collective-permute-start(bf16[128,512]{1,0:T(8,128)(2,1)S(1)} %get-tuple-element.54), channel_id=1, source_target_pairs={{0,1},{1,0},{2,3},{3,2},{4,5},{5,4},{6,7},{7,6},{8,9},{9,8},{10,11... | collective-permute-start | bytes 393224 | tf_op jit(solution)/shard_map/ppermute | solution.py:34
  64.6 5.5 %collective-permute-start.6 = (bf16[2,128,256]{2,1,0:T(8,128)(2,1)S(1)}, bf16[2,128,256]{2,1,0:T(8,128)(2,1)S(1)}, u32[]{:S(2)}, u32[]{:S(2)}) collective-permute-start(bf16[2,128,256]{2,1,0:T(8,128)(2,1)S(1)} %slice.167), channel_id=1, source_target_pairs={{0,4},{2,6},{4,0},{6,2},{8,12},{10,14},{12,8},{14,10},{1,5},{3,7},... | collective-permute-start | bytes 393224 | tf_op jit(solution)/shard_map/ppermute | solution.py:30
  70.1 5.0 %collective-permute-start.8 = (bf16[2,128,256]{2,1,0:T(8,128)(2,1)S(1)}, bf16[2,128,256]{2,1,0:T(8,128)(2,1)S(1)}, u32[]{:S(2)}, u32[]{:S(2)}) collective-permute-start(bf16[2,128,256]{2,1,0:T(8,128)(2,1)S(1)} %slice.166), channel_id=1, source_target_pairs={{0,4},{2,6},{4,0},{6,2},{8,12},{10,14},{12,8},{14,10},{1,5},{3,7},... | collective-permute-start | bytes 393224 | tf_op jit(solution)/shard_map/ppermute | solution.py:30
  70.4 17.1 %copy-start.5 = (f32[2,128,256]{2,1,0:T(8,128)}, f32[2,128,256]{2,1,0:T(8,128)S(1)}, u32[]{:S(2)}) copy-start(f32[2,128,256]{2,1,0:T(8,128)S(1)} %slice_add_fusion.3.refs_2_) | copy-start | bytes 786436
  75.1 7.3 %collective-permute-start.15 = (f32[2,1,128]{0,2,1:T(8,128)S(1)}, f32[2,1,128]{0,2,1:T(8,128)S(1)}, u32[]{:S(2)}, u32[]{:S(2)}) collective-permute-start(f32[2,1,128]{0,2,1:T(8,128)S(1)} %slice.135), channel_id=1, source_target_pairs={{0,8},{2,10},{4,12},{6,14},{8,0},{10,2},{12,4},{14,6},{1,9},{3,11}... | collective-permute-start | bytes 3080 | tf_op jit(solution)/shard_map/ppermute | solution.py:30
  76.0 11.5 %copy-start.6 = (f32[2,128,256]{2,1,0:T(8,128)}, f32[2,128,256]{2,1,0:T(8,128)S(1)}, u32[]{:S(2)}) copy-start(f32[2,128,256]{2,1,0:T(8,128)S(1)} %slice_add_fusion.2.refs_3_) | copy-start | bytes 786436
  76.1 7.5 %collective-permute-start.11 = (bf16[1,128,256]{2,1,0:T(8,128)(2,1)S(1)}, bf16[1,128,256]{2,1,0:T(8,128)(2,1)S(1)}, u32[]{:S(2)}, u32[]{:S(2)}) collective-permute-start(bf16[1,128,256]{2,1,0:T(8,128)(2,1)S(1)} %slice.171), channel_id=1, source_target_pairs={{0,8},{2,10},{4,12},{6,14},{8,0},{10,2},{12,4},{14,6},{1,9},{3,11}... | collective-permute-start | bytes 196616 | tf_op jit(solution)/shard_map/ppermute | solution.py:30
  82.4 5.2 %collective-permute-start.12 = (bf16[1,128,256]{2,1,0:T(8,128)(2,1)S(1)}, bf16[1,128,256]{2,1,0:T(8,128)(2,1)S(1)}, u32[]{:S(2)}, u32[]{:S(2)}) collective-permute-start(bf16[1,128,256]{2,1,0:T(8,128)(2,1)S(1)} %slice.170), channel_id=1, source_target_pairs={{0,8},{2,10},{4,12},{6,14},{8,0},{10,2},{12,4},{14,6},{1,9},{3,11}... | collective-permute-start | bytes 196616 | tf_op jit(solution)/shard_map/ppermute | solution.py:30
  83.0 4.5 %copy-start.13 = (f32[64,512]{1,0:T(8,128)}, f32[64,512]{1,0:T(8,128)S(1)}, u32[]{:S(2)}) copy-start(f32[64,512]{1,0:T(8,128)S(1)} %collective-permute-done.17.refs_14_) | copy-start | bytes 393220
  83.1 4.5 %copy-start.14 = (bf16[128,512]{1,0:T(8,128)(2,1)}, bf16[128,512]{1,0:T(8,128)(2,1)S(1)}, u32[]{:S(2)}) copy-start(bf16[128,512]{1,0:T(8,128)(2,1)S(1)} %collective-permute-done.16.refs_12_) | copy-start | bytes 393220
  83.6 4.0 %copy-start.15 = (bf16[1,128,256]{2,1,0:T(8,128)(2,1)}, bf16[1,128,256]{2,1,0:T(8,128)(2,1)S(1)}, u32[]{:S(2)}) copy-start(bf16[1,128,256]{2,1,0:T(8,128)(2,1)S(1)} %collective-permute-done.11.refs_6_) | copy-start | bytes 196612
  87.6 0.6 copy-start.16
  92.0 1.6 %collective-permute-start.18 = (f32[264,128]{1,0:T(8,128)}, f32[264,128]{1,0:T(8,128)S(1)}, u32[]{:S(2)}, u32[]{:S(2)}) collective-permute-start(f32[264,128]{1,0:T(8,128)} %get-tuple-element.46), channel_id=1, source_target_pairs={{0,1},{1,0},{2,3},{3,2},{4,5},{5,4},{6,7},{7,6},{8,9},{9,8},{10,11... | collective-permute-start | bytes 405512 | tf_op jit(solution)/shard_map/ppermute | solution.py:34
  95.3 6.0 %collective-permute-start.19 = (bf16[416,128]{1,0:T(8,128)(2,1)S(1)}, bf16[416,128]{1,0:T(8,128)(2,1)S(1)}, u32[]{:S(2)}, u32[]{:S(2)}) collective-permute-start(bf16[416,128]{1,0:T(8,128)(2,1)S(1)} %pad_maximum_fusion.2), channel_id=1, source_target_pairs={{0,8},{2,10},{4,12},{6,14},{8,0},{10,2},{12,4},{14,6},{1,9},{3,11}... | collective-permute-start | bytes 319496 | tf_op jit(solution)/shard_map/ppermute | solution.py:30
  102.8 5.1 %collective-permute-start.20 = (bf16[544,128]{1,0:T(8,128)(2,1)S(1)}, bf16[544,128]{1,0:T(8,128)(2,1)S(1)}, u32[]{:S(2)}, u32[]{:S(2)}) collective-permute-start(bf16[544,128]{1,0:T(8,128)(2,1)S(1)} %pad_maximum_fusion.1), channel_id=1, source_target_pairs={{0,4},{2,6},{4,0},{6,2},{8,12},{10,14},{12,8},{14,10},{1,5},{3,7},... | collective-permute-start | bytes 417800 | tf_op jit(solution)/shard_map/ppermute | solution.py:30
  108.7 5.8 %copy-start.7 = (bf16[800,128]{1,0:T(8,128)(2,1)}, bf16[800,128]{1,0:T(8,128)(2,1)S(1)}, u32[]{:S(2)}) copy-start(bf16[800,128]{1,0:T(8,128)(2,1)S(1)} %pad_maximum_fusion.mine_ref) | copy-start | bytes 614404
  108.7 5.8 %collective-permute-start.21 = (bf16[800,128]{1,0:T(8,128)(2,1)S(1)}, bf16[800,128]{1,0:T(8,128)(2,1)S(1)}, u32[]{:S(2)}, u32[]{:S(2)}) collective-permute-start(bf16[800,128]{1,0:T(8,128)(2,1)S(1)} %pad_maximum_fusion.mine_ref), channel_id=1, source_target_pairs={{0,2},{2,0},{4,6},{6,4},{8,10},{10,8},{12,14},{14,12},{1,3},{3,1},... | collective-permute-start | bytes 614408 | tf_op jit(solution)/shard_map/ppermute | solution.py:30
  114.5 0.7 copy-start.12
  120.8 1.6 %collective-permute-start.22 = (f32[512,128]{1,0:T(8,128)S(1)}, f32[512,128]{1,0:T(8,128)S(1)}, u32[]{:S(2)}, u32[]{:S(2)}) collective-permute-start(f32[512,128]{1,0:T(8,128)S(1)} %constant_dynamic-slice_fusion), channel_id=1, source_target_pairs={{0,1},{1,0},{2,3},{3,2},{4,5},{5,4},{6,7},{7,6},{8,9},{9,8},{10,11... | collective-permute-start | bytes 786440 | tf_op jit(solution)/shard_map/ppermute | solution.py:34

commit v3 on v2

--- a/solution.py
+++ b/solution.py
@@ -262,8 +262,34 @@
     )(*operands)
 
 
+def first_payload_kernel(factor_ref, table_ref, got_ref, gram_ref, out_ref):
+    block = factor_ref.shape[0]
+    rows = table_ref.shape[0] - 8
+    out_ref[:block, :] = factor_ref[...]
+    out_ref[block : block + rows, :] = (table_ref[:rows, :] + got_ref[:rows, :]).astype(BF16)
+    out_ref[block + rows :, :] = gram_ref[...]
+
+
+def next_payload_kernel(split, mine_ref, got_ref, out_ref):
+    out_ref[:split, :] = mine_ref[:split, :]
+    out_ref[split : 2 * split, :] = got_ref[:split, :]
+    out_ref[2 * split :, :] = (
+        mine_ref[split:, :].astype(F32) + got_ref[split:, :].astype(F32)
+    ).astype(BF16)
+
+
+def joined(kernel, rows, *operands):
+    return pl.pallas_call(
+        kernel,
+        in_specs=[VMEM] * len(operands),
+        out_specs=VMEM,
+        out_shape=jax.ShapeDtypeStruct((rows, LANES), BF16),
+        name="joined",
+    )(*operands)
+
+
 def final_kernel(bits, block, rank, x_ref, head_hbm, out_hbm, gain_in_ref, gain_out_ref, mine_ref,
-                 got_ref, out_ref, head_ref, small_ref, order_ref, sems):
+                 got_ref, near_ref, away_ref, turned_ref, head_ref, small_ref, order_ref, sems):
     here = lax.axis_index("seq")
     columns = x_ref.shape[1]
     mine = pl.ds(pl.multiple_of(here * columns, LANES), columns)
@@ -302,7 +328,11 @@
     from_head = mm(table, head_ref[...], 1, 0) * gain_out_ref[:, mine].astype(F32)
     from_out = mm(gram, small_ref[...], 1, 0)
     total = jnp.concatenate([from_x[:rank], from_x[rank:] + from_head + from_out], axis=0)
-    out_ref[...] = total.T
+    turned_ref[...] = total.T
+    rows = columns // 2
+    core = lax.axis_index("vocab")
+    near_ref[...] = turned_ref[pl.ds(pl.multiple_of(core * rows, 8), rows), :]
+    away_ref[...] = turned_ref[pl.ds(pl.multiple_of((1 - core) * rows, 8), rows), :]
 
 
 def final_step(x, head, w_out, in_row, out_row, mine, got, count, block):
@@ -312,9 +342,10 @@
     return pl.pallas_call(
         functools.partial(final_kernel, bits, block, rank),
         in_specs=[VMEM, ANY, ANY, VMEM, VMEM, VMEM, VMEM],
-        out_specs=VMEM,
-        out_shape=jax.ShapeDtypeStruct((columns, 2 * rank), F32),
+        out_specs=[VMEM] * 2,
+        out_shape=[jax.ShapeDtypeStruct((columns // 2, 2 * rank), F32)] * 2,
         scratch_shapes=[
+            pltpu.VMEM((columns, 2 * rank), F32),
             pltpu.VMEM((head.shape[0], columns), BF16),
             pltpu.VMEM((rank, columns), BF16),
             pltpu.VMEM((x.shape[0], 2 * rank), BF16),
@@ -381,6 +412,9 @@
             swap_with(send, (1 << (1 - step if flip and step < 2 else step)), count)
             for send, flip in zip(sends, flips)
         ]
+        if step == 0:
+            first_gots, _ = lax.optimization_barrier((gots[: len(early)], more[0]))
+            gots = list(first_gots) + gots[len(early) :]
         left = count >> (step + 1)
         stats = stats[:, :left] + swap_with(stats[:, left:], 1 << step, count)
         if step == bits - 1:
@@ -394,7 +428,9 @@
     )
     got = swap_cores(away)
     rows = table.shape[0] - 8
-    payload = jnp.concatenate([factor, (table[:rows] + got[:rows]).astype(BF16), gram_out])
+    payload = joined(
+        first_payload_kernel, block + rows + rank // 2, factor, table, got, gram_out
+    )
     own_loss, far_loss = table[rows : rows + 1], got[rows : rows + 1]
     row_loss = jnp.where(
         core == 0,
@@ -405,15 +441,13 @@
     for step in reversed(range(bits)):
         got = swap_with(payload, 1 << step, count)
         if step:
-            added = payload[split:].astype(F32) + got[split:].astype(F32)
-            payload = jnp.concatenate([payload[:split], got[:split], added.astype(BF16)])
+            kernel = functools.partial(next_payload_kernel, split)
+            payload = joined(kernel, payload.shape[0] + split, payload, got)
             split *= 2
             if step == 1:
                 payload, row_loss = lax.optimization_barrier((payload, row_loss))
 
-    both = final_step(x, head, w_out, in_row, out_row, payload, got, count, block)
-    near = lax.dynamic_slice_in_dim(both, core * (columns // 2), columns // 2, axis=0)
-    away = lax.dynamic_slice_in_dim(both, (1 - core) * (columns // 2), columns // 2, axis=0)
+    near, away = final_step(x, head, w_out, in_row, out_row, payload, got, count, block)
     return (near + swap_cores(away), row_loss)
 
 

time: 125 us -> 126 us (level)
  waiting for transfers between devices: 51.8 us -> 43.1 us
  starting transfers between devices: 19.2 us -> 26.9 us
  other arithmetic: 16.6 us -> 11.5 us
  Pallas kernels: 18.7 us -> 23.7 us
  local copies, waits for them, and re-layouts: 9.4 us -> 12 us
    ppermute x18, waiting for transfers between devices: 48.8 us -> 39.8 us  [swap_with(): return lax.ppermute(value, 'seq', [(i, i ^ bit) for i in range(count)])]
    ppermute x18, starting transfers between devices: 18.6 us -> 26.2 us  [swap_with(): return lax.ppermute(value, 'seq', [(i, i ^ bit) for i in range(count)])]
    pallas_call x0 -> x3, Pallas kernels: none -> 4.96 us  [joined(): pl.pallas_call(kernel, in_specs=[VMEM] * len(operands), out_specs=VMEM, o...]
    concatenate x3 -> x0, other arithmetic: 2.33 us -> none  [the longest x2 1.54 us: on_device(): jnp.concatenate([payload[:split], got[:split], added.astype(BF16)])]
    unnamed x40, local copies, waits for them, and re-layouts: 1.36 us -> 3.3 us
    convert_element_type x3 -> x0, other arithmetic: 1.66 us -> none  [the longest x1 0.92 us: on_device(): (table[:rows] + got[:rows]).astype(BF16)]
where the time goes in v3:
time: 126 us; the launch traced here: 125 us
  waiting for transfers between devices  43.1 us (34%)
  starting transfers between devices  26.9 us (21%)
  Pallas kernels  23.7 us (19%)
  local copies, waits for them, and re-layouts  12 us (10%)
  other arithmetic  11.5 us (9%)
  matrix products  7.15 us (6%)
    ppermute x18, waiting for transfers between devices, swap_with(): return lax.ppermute(value, 'seq', [(i, i ^ bit) for i in range(count)])  39.8 us
    ppermute x18, starting transfers between devices, swap_with(): return lax.ppermute(value, 'seq', [(i, i ^ bit) for i in range(count)])  26.2 us
    dot_general x2, matrix products, mm(): lax.dot_general(lhs, rhs, (((lhs_dim,), (rhs_dim,)), ((), ())), preferred...  7.15 us
    pallas_call x1, Pallas kernels, own_products(): pl.pallas_call(functools.partial(own_kernel, bits, block, chunks), in_spe...  6.08 us
    pallas_call x3, Pallas kernels, joined(): pl.pallas_call(kernel, in_specs=[VMEM] * len(operands), out_specs=VMEM, o...  4.96 us
    pallas_call x1, Pallas kernels, final_step(): pl.pallas_call(functools.partial(final_kernel, bits, block, rank), in_spe...  4.66 us
    add x8, other arithmetic, on_device(): keeps = [keep[:left] + got.astype(F32) for keep, got in zip(keeps, gots)]  4.49 us
    pallas_call x1, Pallas kernels, far_products(): pl.pallas_call(functools.partial(far_kernel, bits, block, chunks), in_spe...  4.19 us
  transfers between devices with their start and end apart: 23, of which 15 were waited for; matrix products, arithmetic and copies ran while one was open for 18% of the time, Pallas kernels for 3%

profile of v3, /device:TPU:0, one launch (start us, length us, event | category | flops | bytes accessed | tf_op | source)
XLA Modules:
  0.0 125.4 jit_solution(10068304290073230414)
XLA Ops:
  0.6 1.3 %reshape.64.gain_in_ref = bf16[1,8192]{1,0:T(2,128)(2,1)} reshape(bf16[8192]{0:T(1024)(128)(2,1)} %param.16) | data formatting | bytes 32768 | tf_op jit(solution)/shard_map/reshape | solution.py:372
  2.0 1.3 %reshape.65.gain_out_ref = bf16[1,8192]{1,0:T(2,128)(2,1)} reshape(bf16[8192]{0:T(1024)(128)(2,1)} %param.17) | data formatting | bytes 32768 | tf_op jit(solution)/shard_map/reshape | solution.py:372
  3.3 6.1 %own_products.1 = (bf16[4,128,384]{2,1,0:T(8,128)(2,1)}, f32[4,128,384]{2,1,0:T(8,128)}, bf16[4,128,256]{2,1,0:T(8,128)(2,1)}, f32[4,128,256]{2,1,0:T(8,128)}, bf16[512,1024]{1,0:T(8,128)(2,1)}) custom-call(bf16[1024,1024]{1,0:T(8,128)(2,1)} %bitcast.23, bf16[512,8192]{1,0:T(8,128)(2,1)} %head_hbm.3, bf16[64,8192]{1,0:T(8,128)(2,1)} %in_hbm.1, ...), custom_call_target="tpu_custom_call" | custom-call | flops 1342177280 | bytes 3407872 | tf_op jit(solution)/shard_map/own_products/pallas_call | solution.py:116
  9.4 3.0 %collective-permute-start = (bf16[4,128,384]{2,1,0:T(8,128)(2,1)}, bf16[4,128,384]{2,1,0:T(8,128)(2,1)S(1)}, u32[]{:S(2)}, u32[]{:S(2)}) collective-permute-start(bf16[4,128,384]{2,1,0:T(8,128)(2,1)} %get-tuple-element.31), channel_id=1, source_target_pairs={{0,2},{2,0},{4,6},{6,4},{8,10},{10,8},{12,14},{14,12},{1,3},{3,1},... | collective-permute-start | bytes 1179656 | tf_op jit(solution)/shard_map/ppermute | solution.py:30
  12.4 1.6 %collective-permute-start.1 = (bf16[4,128,256]{2,1,0:T(8,128)(2,1)}, bf16[4,128,256]{2,1,0:T(8,128)(2,1)S(1)}, u32[]{:S(2)}, u32[]{:S(2)}) collective-permute-start(bf16[4,128,256]{2,1,0:T(8,128)(2,1)} %get-tuple-element.32), channel_id=1, source_target_pairs={{0,4},{2,6},{4,0},{6,2},{8,12},{10,14},{12,8},{14,10},{1,5},{3,7},... | collective-permute-start | bytes 786440 | tf_op jit(solution)/shard_map/ppermute | solution.py:30
  14.1 6.4 %collective-permute-done.1 = bf16[4,128,256]{2,1,0:T(8,128)(2,1)S(1)} collective-permute-done((bf16[4,128,256]{2,1,0:T(8,128)(2,1)}, bf16[4,128,256]{2,1,0:T(8,128)(2,1)S(1)}, u32[]{:S(2)}, u32[]{:S(2)}) %collective-permute-start.1) | collective-permute-done | bytes 262176 | tf_op jit(solution)/shard_map/ppermute | solution.py:30
  20.4 1.3 %collective-permute-done = bf16[4,128,384]{2,1,0:T(8,128)(2,1)S(1)} collective-permute-done((bf16[4,128,384]{2,1,0:T(8,128)(2,1)}, bf16[4,128,384]{2,1,0:T(8,128)(2,1)S(1)}, u32[]{:S(2)}, u32[]{:S(2)}) %collective-permute-start) | collective-permute-done | bytes 393248 | tf_op jit(solution)/shard_map/ppermute | solution.py:30
  21.8 1.1 convert_add_fusion.3
  22.9 1.8 %collective-permute-start.3 = (bf16[2,128,256]{2,1,0:T(8,128)(2,1)S(1)}, bf16[2,128,256]{2,1,0:T(8,128)(2,1)S(1)}, u32[]{:S(2)}, u32[]{:S(2)}) collective-permute-start(bf16[2,128,256]{2,1,0:T(8,128)(2,1)S(1)} %slice.129), channel_id=1, source_target_pairs={{0,2},{2,0},{4,6},{6,4},{8,10},{10,8},{12,14},{14,12},{1,3},{3,1},... | collective-permute-start | bytes 393224 | tf_op jit(solution)/shard_map/ppermute | solution.py:30
  24.7 1.2 convert_add_fusion
  26.0 1.6 %collective-permute-start.2 = (bf16[2,128,384]{2,1,0:T(8,128)(2,1)S(1)}, bf16[2,128,384]{2,1,0:T(8,128)(2,1)S(1)}, u32[]{:S(2)}, u32[]{:S(2)}) collective-permute-start(bf16[2,128,384]{2,1,0:T(8,128)(2,1)S(1)} %slice.126), channel_id=1, source_target_pairs={{0,4},{2,6},{4,0},{6,2},{8,12},{10,14},{12,8},{14,10},{1,5},{3,7},... | collective-permute-start | bytes 589832 | tf_op jit(solution)/shard_map/ppermute | solution.py:30
  28.7 2.8 %collective-permute-start.10 = (bf16[1,128,256]{2,1,0:T(8,128)(2,1)}, bf16[1,128,256]{2,1,0:T(8,128)(2,1)}, u32[]{:S(2)}, u32[]{:S(2)}) collective-permute-start(bf16[1,128,256]{2,1,0:T(8,128)(2,1)} %slice.133), channel_id=1, source_target_pairs={{0,8},{2,10},{4,12},{6,14},{8,0},{10,2},{12,4},{14,6},{1,9},{3,11}... | collective-permute-start | bytes 196616 | tf_op jit(solution)/shard_map/ppermute | solution.py:30
  31.5 0.9 collective-permute-done.2
  33.2 2.4 %collective-permute-start.9 = (bf16[1,128,384]{2,1,0:T(8,128)(2,1)}, bf16[1,128,384]{2,1,0:T(8,128)(2,1)}, u32[]{:S(2)}, u32[]{:S(2)}) collective-permute-start(bf16[1,128,384]{2,1,0:T(8,128)(2,1)} %slice.130), channel_id=1, source_target_pairs={{0,8},{2,10},{4,12},{6,14},{8,0},{10,2},{12,4},{14,6},{1,9},{3,11}... | collective-permute-start | bytes 294920 | tf_op jit(solution)/shard_map/ppermute | solution.py:30
  35.6 4.2 %far_products.1 = (bf16[4,128,256]{2,1,0:T(8,128)(2,1)}, f32[4,128,256]{2,1,0:T(8,128)}, bf16[4,128,256]{2,1,0:T(8,128)(2,1)}, f32[4,128,256]{2,1,0:T(8,128)}) custom-call(bf16[1024,1024]{1,0:T(8,128)(2,1)} %bitcast.24, bf16[512,1024]{1,0:T(8,128)(2,1)} %collective-permute-done.4.table_ref), custom_call_target="tpu_custom_call" | custom-call | flops 1073741824 | bytes 3145728 | tf_op jit(solution)/shard_map/far_products/pallas_call | solution.py:145
  39.8 0.7 collective-permute-start.5
  40.6 1.3 %collective-permute-start.7 = (bf16[4,128,256]{2,1,0:T(8,128)(2,1)}, bf16[4,128,256]{2,1,0:T(8,128)(2,1)}, u32[]{:S(2)}, u32[]{:S(2)}) collective-permute-start(bf16[4,128,256]{2,1,0:T(8,128)(2,1)} %get-tuple-element.40), channel_id=1, source_target_pairs={{0,2},{2,0},{4,6},{6,4},{8,10},{10,8},{12,14},{14,12},{1,3},{3,1},... | collective-permute-start | bytes 786440 | tf_op jit(solution)/shard_map/ppermute | solution.py:30
  42.5 0.8 fusion
  44.3 0.8 collective-permute-start.13
  46.5 1.0 fusion.9.refs_15_
  47.8 1.6 %dynamic-slice_bitcast_fusion = (bf16[128,512]{1,0:T(8,128)(2,1)S(1)}, bf16[128,512]{1,0:T(8,128)(2,1)}) fusion(bf16[2,128,512]{2,1,0:T(8,128)(2,1)} %param.15, s32[]{:T(128)S(6)} %select_n.34, s32[]{:T(128)S(6)} %select_n.33), kind=kLoop, calls=%fused_computation.25 | loop fusion | bytes 524296 | tf_op jit(solution)/shard_map/jit(dynamic_index_in_dim)/squeeze | solution.py:395
  49.4 6.1 %fusion.1.refs_13_ = f32[64,512]{1,0:T(8,128)S(1)} fusion(bf16[512,8192]{1,0:T(8,128)(2,1)} %head_hbm.3, bf16[64,8192]{1,0:T(8,128)(2,1)S(1)} %copy-done.1, f32[8192]{0:T(1024)S(1)} %convert_element_type.70), kind=kOutput, calls=%fused_computation.5 | convolution fusion | flops 538443776 | bytes 9601024 | tf_op jit(solution)/shard_map/dot_general | solution.py:38
  55.6 0.7 pad_maximum_fusion.refs_10_
  56.4 1.5 %collective-permute-start.14 = (f32[2,2,128]{0,2,1:T(8,128)S(1)}, f32[2,2,128]{0,2,1:T(8,128)S(1)}, u32[]{:S(2)}, u32[]{:S(2)}) collective-permute-start(f32[2,2,128]{0,2,1:T(8,128)S(1)} %slice.105), channel_id=1, source_target_pairs={{0,4},{2,6},{4,0},{6,2},{8,12},{10,14},{12,8},{14,10},{1,5},{3,7},... | collective-permute-start | bytes 6152 | tf_op jit(solution)/shard_map/ppermute | solution.py:30
  57.9 0.7 copy.32.refs_9_
  58.7 2.8 %collective-permute-done.14 = f32[2,2,128]{0,2,1:T(8,128)S(1)} collective-permute-done((f32[2,2,128]{0,2,1:T(8,128)S(1)}, f32[2,2,128]{0,2,1:T(8,128)S(1)}, u32[]{:S(2)}, u32[]{:S(2)}) %collective-permute-start.14) | collective-permute-done | bytes 2080 | tf_op jit(solution)/shard_map/ppermute | solution.py:30
  62.1 1.0 convert_add_fusion.2
  63.1 1.5 %collective-permute-start.6 = (bf16[2,128,256]{2,1,0:T(8,128)(2,1)S(1)}, bf16[2,128,256]{2,1,0:T(8,128)(2,1)S(1)}, u32[]{:S(2)}, u32[]{:S(2)}) collective-permute-start(bf16[2,128,256]{2,1,0:T(8,128)(2,1)S(1)} %slice.128), channel_id=1, source_target_pairs={{0,4},{2,6},{4,0},{6,2},{8,12},{10,14},{12,8},{14,10},{1,5},{3,7},... | collective-permute-start | bytes 393224 | tf_op jit(solution)/shard_map/ppermute | solution.py:30
  64.6 1.0 convert_add_fusion.1
  65.7 2.9 %collective-permute-done.6 = bf16[2,128,256]{2,1,0:T(8,128)(2,1)S(1)} collective-permute-done((bf16[2,128,256]{2,1,0:T(8,128)(2,1)S(1)}, bf16[2,128,256]{2,1,0:T(8,128)(2,1)S(1)}, u32[]{:S(2)}, u32[]{:S(2)}) %collective-permute-start.6) | collective-permute-done | bytes 131104 | tf_op jit(solution)/shard_map/ppermute | solution.py:30
  68.6 1.4 %collective-permute-start.8 = (bf16[2,128,256]{2,1,0:T(8,128)(2,1)S(1)}, bf16[2,128,256]{2,1,0:T(8,128)(2,1)S(1)}, u32[]{:S(2)}, u32[]{:S(2)}) collective-permute-start(bf16[2,128,256]{2,1,0:T(8,128)(2,1)S(1)} %slice.127), channel_id=1, source_target_pairs={{0,4},{2,6},{4,0},{6,2},{8,12},{10,14},{12,8},{14,10},{1,5},{3,7},... | collective-permute-start | bytes 393224 | tf_op jit(solution)/shard_map/ppermute | solution.py:30
  70.1 3.5 %collective-permute-done.8 = bf16[2,128,256]{2,1,0:T(8,128)(2,1)S(1)} collective-permute-done((bf16[2,128,256]{2,1,0:T(8,128)(2,1)S(1)}, bf16[2,128,256]{2,1,0:T(8,128)(2,1)S(1)}, u32[]{:S(2)}, u32[]{:S(2)}) %collective-permute-start.8) | collective-permute-done | bytes 131104 | tf_op jit(solution)/shard_map/ppermute | solution.py:30
  74.0 2.6 %collective-permute-start.11 = (bf16[1,128,256]{2,1,0:T(8,128)(2,1)S(1)}, bf16[1,128,256]{2,1,0:T(8,128)(2,1)S(1)}, u32[]{:S(2)}, u32[]{:S(2)}) collective-permute-start(bf16[1,128,256]{2,1,0:T(8,128)(2,1)S(1)} %slice.132), channel_id=1, source_target_pairs={{0,8},{2,10},{4,12},{6,14},{8,0},{10,2},{12,4},{14,6},{1,9},{3,11}... | collective-permute-start | bytes 196616 | tf_op jit(solution)/shard_map/ppermute | solution.py:30
  76.7 2.1 %collective-permute-done.15 = f32[2,1,128]{0,2,1:T(8,128)S(1)} collective-permute-done((f32[2,1,128]{0,2,1:T(8,128)S(1)}, f32[2,1,128]{0,2,1:T(8,128)S(1)}, u32[]{:S(2)}, u32[]{:S(2)}) %collective-permute-start.15) | collective-permute-done | bytes 1056 | tf_op jit(solution)/shard_map/ppermute | solution.py:30
  80.1 1.8 %collective-permute-done.11.refs_6_ = bf16[1,128,256]{2,1,0:T(8,128)(2,1)S(1)} collective-permute-done((bf16[1,128,256]{2,1,0:T(8,128)(2,1)S(1)}, bf16[1,128,256]{2,1,0:T(8,128)(2,1)S(1)}, u32[]{:S(2)}, u32[]{:S(2)}) %collective-permute-start.11) | collective-permute-done | bytes 65568 | tf_op jit(solution)/shard_map/ppermute | solution.py:30
  81.9 2.0 %collective-permute-done.12.refs_7_ = bf16[1,128,256]{2,1,0:T(8,128)(2,1)S(1)} collective-permute-done((bf16[1,128,256]{2,1,0:T(8,128)(2,1)S(1)}, bf16[1,128,256]{2,1,0:T(8,128)(2,1)S(1)}, u32[]{:S(2)}, u32[]{:S(2)}) %collective-permute-start.12) | collective-permute-done | bytes 65568 | tf_op jit(solution)/shard_map/ppermute | solution.py:30
  84.5 3.8 %owner.1 = (bf16[128,128]{1,0:T(8,128)(2,1)}, f32[264,128]{1,0:T(8,128)}, f32[264,128]{1,0:T(8,128)}, bf16[32,128]{1,0:T(8,128)(2,1)}) custom-call(f32[2,128,384]{2,1,0:T(8,128)} %copy-done.3, f32[2,128,256]{2,1,0:T(8,128)} %copy-done.4, f32[2,128,256]{2,1,0:T(8,128)} %copy-done.5, f32[2,128,256]{2,1,0:T(8,128)} %copy-done.6, ...), custom_call_target="tpu_custom_call" | custom-call | tf_op jit(solution)/shard_map/owner/pallas_call | solution.py:251
  88.4 1.6 %collective-permute-done.18.got_ref = f32[264,128]{1,0:T(8,128)S(1)} collective-permute-done((f32[264,128]{1,0:T(8,128)}, f32[264,128]{1,0:T(8,128)S(1)}, u32[]{:S(2)}, u32[]{:S(2)}) %collective-permute-start.18) | collective-permute-done | bytes 135200 | tf_op jit(solution)/shard_map/ppermute | solution.py:34
  90.6 1.6 %joined.3.mine_ref = bf16[416,128]{1,0:T(8,128)(2,1)} custom-call(bf16[128,128]{1,0:T(8,128)(2,1)} %get-tuple-element.50.factor_ref, f32[264,128]{1,0:T(8,128)} %get-tuple-element.51.table_ref, f32[264,128]{1,0:T(8,128)} %copy-done.12, bf16[32,128]{1,0:T(8,128)(2,1)} %get-tuple-element.53.gram_ref), custom_call_target="tpu_custom_call" | custom-call | tf_op jit(solution)/shard_map/joined/pallas_call | solution.py:282
  92.9 7.8 %collective-permute-done.19.got_ref = bf16[416,128]{1,0:T(8,128)(2,1)S(1)} collective-permute-done((bf16[416,128]{1,0:T(8,128)(2,1)}, bf16[416,128]{1,0:T(8,128)(2,1)S(1)}, u32[]{:S(2)}, u32[]{:S(2)}) %collective-permute-start.19) | collective-permute-done | bytes 106528 | tf_op jit(solution)/shard_map/ppermute | solution.py:30
  101.3 1.6 %joined.4.mine_ref = bf16[544,128]{1,0:T(8,128)(2,1)} custom-call(bf16[416,128]{1,0:T(8,128)(2,1)} %joined.3.mine_ref, bf16[416,128]{1,0:T(8,128)(2,1)} %copy-done.15), custom_call_target="tpu_custom_call" | custom-call | tf_op jit(solution)/shard_map/joined/pallas_call | solution.py:282
  104.9 3.2 %collective-permute-done.20.got_ref = bf16[544,128]{1,0:T(8,128)(2,1)S(1)} collective-permute-done((bf16[544,128]{1,0:T(8,128)(2,1)}, bf16[544,128]{1,0:T(8,128)(2,1)S(1)}, u32[]{:S(2)}, u32[]{:S(2)}) %collective-permute-start.20) | collective-permute-done | bytes 139296 | tf_op jit(solution)/shard_map/ppermute | solution.py:30
  108.8 1.7 %joined.5.mine_ref = bf16[800,128]{1,0:T(8,128)(2,1)} custom-call(bf16[544,128]{1,0:T(8,128)(2,1)} %joined.4.mine_ref, bf16[544,128]{1,0:T(8,128)(2,1)} %copy-done.11), custom_call_target="tpu_custom_call" | custom-call | tf_op jit(solution)/shard_map/joined/pallas_call | solution.py:282
  110.5 1.3 %collective-permute-start.21 = (bf16[800,128]{1,0:T(8,128)(2,1)}, bf16[800,128]{1,0:T(8,128)(2,1)S(1)}, u32[]{:S(2)}, u32[]{:S(2)}) collective-permute-start(bf16[800,128]{1,0:T(8,128)(2,1)} %joined.5.mine_ref), channel_id=1, source_target_pairs={{0,2},{2,0},{4,6},{6,4},{8,10},{10,8},{12,14},{14,12},{1,3},{3,1},... | collective-permute-start | bytes 614408 | tf_op jit(solution)/shard_map/ppermute | solution.py:30
  111.8 4.7 %collective-permute-done.21.got_ref = bf16[800,128]{1,0:T(8,128)(2,1)S(1)} collective-permute-done((bf16[800,128]{1,0:T(8,128)(2,1)}, bf16[800,128]{1,0:T(8,128)(2,1)S(1)}, u32[]{:S(2)}, u32[]{:S(2)}) %collective-permute-start.21) | collective-permute-done | bytes 204832 | tf_op jit(solution)/shard_map/ppermute | solution.py:30
  117.2 4.7 %final.1 = (f32[512,128]{1,0:T(8,128)}, f32[512,128]{1,0:T(8,128)}) custom-call(bf16[1024,1024]{1,0:T(8,128)(2,1)} %bitcast.25, bf16[512,8192]{1,0:T(8,128)(2,1)} %head_hbm.3, bf16[64,8192]{1,0:T(8,128)(2,1)} %out_hbm.3, bf16[1,8192]{1,0:T(2,128)(2,1)} %reshape.64.gain_in_ref, bf16[1,8192]{1,0:T(2,128)(2,1)} %reshape.65.gain_out_ref, ...), custom_call_target="tpu_custom_call" | custom-call | tf_op jit(solution)/shard_map/final/pallas_call | solution.py:342
  121.9 1.7 %collective-permute-done.22 = f32[512,128]{1,0:T(8,128)S(1)} collective-permute-done((f32[512,128]{1,0:T(8,128)}, f32[512,128]{1,0:T(8,128)S(1)}, u32[]{:S(2)}, u32[]{:S(2)}) %collective-permute-start.22) | collective-permute-done | bytes 262176 | tf_op jit(solution)/shard_map/ppermute | solution.py:34
  123.7 1.7 %add.88 = f32[512,128]{1,0:T(8,128)} add(f32[512,128]{1,0:T(8,128)} %get-tuple-element.55, f32[512,128]{1,0:T(8,128)S(1)} %collective-permute-done.22) | non-fusion elementwise | flops 65536 | bytes 786432 | tf_op jit(solution)/shard_map/add | solution.py:451
  (93 shorter events, 13.6 us)
Async XLA Ops:
  0.6 46.9 %copy-start = (s32[2,128]{1,0:T(2,128)S(1)}, s32[2,128]{1,0:T(2,128)}, u32[]{:S(2)}) copy-start(s32[2,128]{1,0:T(2,128)} %param.14) | copy-start | bytes 3076
  3.3 10.7 %copy-start.18 = (s32[8]{0:T(128)S(1)}, s32[8]{0:T(128)}, u32[]{:S(2)}) copy-start(s32[8]{0:T(128)} %constant.61.clone) | copy-start | bytes 100
  9.4 12.4 %collective-permute-start = (bf16[4,128,384]{2,1,0:T(8,128)(2,1)}, bf16[4,128,384]{2,1,0:T(8,128)(2,1)S(1)}, u32[]{:S(2)}, u32[]{:S(2)}) collective-permute-start(bf16[4,128,384]{2,1,0:T(8,128)(2,1)} %get-tuple-element.31), channel_id=1, source_target_pairs={{0,2},{2,0},{4,6},{6,4},{8,10},{10,8},{12,14},{14,12},{1,3},{3,1},... | collective-permute-start | bytes 1179656 | tf_op jit(solution)/shard_map/ppermute | solution.py:30
  12.4 8.0 %collective-permute-start.1 = (bf16[4,128,256]{2,1,0:T(8,128)(2,1)}, bf16[4,128,256]{2,1,0:T(8,128)(2,1)S(1)}, u32[]{:S(2)}, u32[]{:S(2)}) collective-permute-start(bf16[4,128,256]{2,1,0:T(8,128)(2,1)} %get-tuple-element.32), channel_id=1, source_target_pairs={{0,4},{2,6},{4,0},{6,2},{8,12},{10,14},{12,8},{14,10},{1,5},{3,7},... | collective-permute-start | bytes 786440 | tf_op jit(solution)/shard_map/ppermute | solution.py:30
  14.0 21.6 %collective-permute-start.4 = (bf16[512,1024]{1,0:T(8,128)(2,1)}, bf16[512,1024]{1,0:T(8,128)(2,1)}, u32[]{:S(2)}, u32[]{:S(2)}) collective-permute-start(bf16[512,1024]{1,0:T(8,128)(2,1)} %get-tuple-element.36), channel_id=1, source_target_pairs={{0,1},{1,0},{2,3},{3,2},{4,5},{5,4},{6,7},{7,6},{8,9},{9,8},{10,11... | collective-permute-start | bytes 3145736 | tf_op jit(solution)/shard_map/ppermute | solution.py:34
  22.9 19.6 %copy-start.2 = (bf16[1,1024,1024]{2,1,0:T(8,128)(2,1)S(1)}, bf16[1,1024,1024]{2,1,0:T(8,128)(2,1)}, u32[]{:S(2)}) copy-start(bf16[1,1024,1024]{2,1,0:T(8,128)(2,1)} %param.11) | copy-start | bytes 6291460
  22.9 5.0 %collective-permute-start.3 = (bf16[2,128,256]{2,1,0:T(8,128)(2,1)S(1)}, bf16[2,128,256]{2,1,0:T(8,128)(2,1)S(1)}, u32[]{:S(2)}, u32[]{:S(2)}) collective-permute-start(bf16[2,128,256]{2,1,0:T(8,128)(2,1)S(1)} %slice.129), channel_id=1, source_target_pairs={{0,2},{2,0},{4,6},{6,4},{8,10},{10,8},{12,14},{14,12},{1,3},{3,1},... | collective-permute-start | bytes 393224 | tf_op jit(solution)/shard_map/ppermute | solution.py:30
  26.0 6.4 %collective-permute-start.2 = (bf16[2,128,384]{2,1,0:T(8,128)(2,1)S(1)}, bf16[2,128,384]{2,1,0:T(8,128)(2,1)S(1)}, u32[]{:S(2)}, u32[]{:S(2)}) collective-permute-start(bf16[2,128,384]{2,1,0:T(8,128)(2,1)S(1)} %slice.126), channel_id=1, source_target_pairs={{0,4},{2,6},{4,0},{6,2},{8,12},{10,14},{12,8},{14,10},{1,5},{3,7},... | collective-permute-start | bytes 589832 | tf_op jit(solution)/shard_map/ppermute | solution.py:30
  28.0 3.5 %copy-start.4 = (f32[2,128,256]{2,1,0:T(8,128)}, f32[2,128,256]{2,1,0:T(8,128)S(1)}, u32[]{:S(2)}) copy-start(f32[2,128,256]{2,1,0:T(8,128)S(1)} %slice_add_fusion.4.refs_1_) | copy-start | bytes 786436
  28.7 17.8 %copy-start.1 = (bf16[64,8192]{1,0:T(8,128)(2,1)S(1)}, bf16[64,8192]{1,0:T(8,128)(2,1)}, u32[]{:S(2)}) copy-start(bf16[64,8192]{1,0:T(8,128)(2,1)} %out_hbm.3) | copy-start | bytes 3145732
  28.7 45.3 %collective-permute-start.10 = (bf16[1,128,256]{2,1,0:T(8,128)(2,1)}, bf16[1,128,256]{2,1,0:T(8,128)(2,1)}, u32[]{:S(2)}, u32[]{:S(2)}) collective-permute-start(bf16[1,128,256]{2,1,0:T(8,128)(2,1)} %slice.133), channel_id=1, source_target_pairs={{0,8},{2,10},{4,12},{6,14},{8,0},{10,2},{12,4},{14,6},{1,9},{3,11}... | collective-permute-start | bytes 196616 | tf_op jit(solution)/shard_map/ppermute | solution.py:30
  32.5 15.0 %copy-start.3 = (f32[2,128,384]{2,1,0:T(8,128)}, f32[2,128,384]{2,1,0:T(8,128)S(1)}, u32[]{:S(2)}) copy-start(f32[2,128,384]{2,1,0:T(8,128)S(1)} %slice_add_fusion.refs_0_) | copy-start | bytes 1179652
  33.2 46.8 %collective-permute-start.9 = (bf16[1,128,384]{2,1,0:T(8,128)(2,1)}, bf16[1,128,384]{2,1,0:T(8,128)(2,1)}, u32[]{:S(2)}, u32[]{:S(2)}) collective-permute-start(bf16[1,128,384]{2,1,0:T(8,128)(2,1)} %slice.130), channel_id=1, source_target_pairs={{0,8},{2,10},{4,12},{6,14},{8,0},{10,2},{12,4},{14,6},{1,9},{3,11}... | collective-permute-start | bytes 294920 | tf_op jit(solution)/shard_map/ppermute | solution.py:30
  39.8 21.7 %collective-permute-start.5 = (bf16[4,128,256]{2,1,0:T(8,128)(2,1)}, bf16[4,128,256]{2,1,0:T(8,128)(2,1)}, u32[]{:S(2)}, u32[]{:S(2)}) collective-permute-start(bf16[4,128,256]{2,1,0:T(8,128)(2,1)} %get-tuple-element.38), channel_id=1, source_target_pairs={{0,2},{2,0},{4,6},{6,4},{8,10},{10,8},{12,14},{14,12},{1,3},{3,1},... | collective-permute-start | bytes 786440 | tf_op jit(solution)/shard_map/ppermute | solution.py:30
  40.6 22.6 %collective-permute-start.7 = (bf16[4,128,256]{2,1,0:T(8,128)(2,1)}, bf16[4,128,256]{2,1,0:T(8,128)(2,1)}, u32[]{:S(2)}, u32[]{:S(2)}) collective-permute-start(bf16[4,128,256]{2,1,0:T(8,128)(2,1)} %get-tuple-element.40), channel_id=1, source_target_pairs={{0,2},{2,0},{4,6},{6,4},{8,10},{10,8},{12,14},{14,12},{1,3},{3,1},... | collective-permute-start | bytes 786440 | tf_op jit(solution)/shard_map/ppermute | solution.py:30
  44.3 12.1 %collective-permute-start.13 = (f32[2,4,128]{0,2,1:T(8,128)S(1)}, f32[2,4,128]{0,2,1:T(8,128)S(1)}, u32[]{:S(2)}, u32[]{:S(2)}) collective-permute-start(f32[2,4,128]{0,2,1:T(8,128)S(1)} %slice.103), channel_id=1, source_target_pairs={{0,2},{2,0},{4,6},{6,4},{8,10},{10,8},{12,14},{14,12},{1,3},{3,1},... | collective-permute-start | bytes 12296 | tf_op jit(solution)/shard_map/ppermute | solution.py:30
  49.4 6.9 %copy-start.19 = (s32[2,128]{1,0:T(2,128)S(1)}, s32[2,128]{1,0:T(2,128)}, u32[]{:S(2)}) copy-start(s32[2,128]{1,0:T(2,128)} %param.13) | copy-start | bytes 3076
  49.4 12.6 %copy-start.9 = (f32[4,128,256]{2,1,0:T(8,128)S(1)}, f32[4,128,256]{2,1,0:T(8,128)}, u32[]{:S(2)}) copy-start(f32[4,128,256]{2,1,0:T(8,128)} %get-tuple-element.37) | copy-start | bytes 1572868
  49.4 15.2 %copy-start.8 = (f32[4,128,256]{2,1,0:T(8,128)S(1)}, f32[4,128,256]{2,1,0:T(8,128)}, u32[]{:S(2)}) copy-start(f32[4,128,256]{2,1,0:T(8,128)} %get-tuple-element.39) | copy-start | bytes 1572868
  55.6 28.3 %copy-start.7 = (f32[64,512]{1,0:T(8,128)}, f32[64,512]{1,0:T(8,128)S(1)}, u32[]{:S(2)}) copy-start(f32[64,512]{1,0:T(8,128)S(1)} %fusion.1.refs_13_) | copy-start | bytes 393220
  56.4 5.0 %collective-permute-start.14 = (f32[2,2,128]{0,2,1:T(8,128)S(1)}, f32[2,2,128]{0,2,1:T(8,128)S(1)}, u32[]{:S(2)}, u32[]{:S(2)}) collective-permute-start(f32[2,2,128]{0,2,1:T(8,128)S(1)} %slice.105), channel_id=1, source_target_pairs={{0,4},{2,6},{4,0},{6,2},{8,12},{10,14},{12,8},{14,10},{1,5},{3,7},... | collective-permute-start | bytes 6152 | tf_op jit(solution)/shard_map/ppermute | solution.py:30
  61.4 18.6 %collective-permute-start.16 = (bf16[128,512]{1,0:T(8,128)(2,1)S(1)}, bf16[128,512]{1,0:T(8,128)(2,1)S(1)}, u32[]{:S(2)}, u32[]{:S(2)}) collective-permute-start(bf16[128,512]{1,0:T(8,128)(2,1)S(1)} %get-tuple-element.62), channel_id=1, source_target_pairs={{0,1},{1,0},{2,3},{3,2},{4,5},{5,4},{6,7},{7,6},{8,9},{9,8},{10,11... | collective-permute-start | bytes 393224 | tf_op jit(solution)/shard_map/ppermute | solution.py:34
  61.5 18.5 %collective-permute-start.17 = (f32[64,512]{1,0:T(8,128)S(1)}, f32[64,512]{1,0:T(8,128)S(1)}, u32[]{:S(2)}, u32[]{:S(2)}) collective-permute-start(f32[64,512]{1,0:T(8,128)S(1)} %fusion.1.refs_13_), channel_id=1, source_target_pairs={{0,1},{1,0},{2,3},{3,2},{4,5},{5,4},{6,7},{7,6},{8,9},{9,8},{10,11... | collective-permute-start | bytes 393224 | tf_op jit(solution)/shard_map/ppermute | solution.py:34
  63.1 5.5 %collective-permute-start.6 = (bf16[2,128,256]{2,1,0:T(8,128)(2,1)S(1)}, bf16[2,128,256]{2,1,0:T(8,128)(2,1)S(1)}, u32[]{:S(2)}, u32[]{:S(2)}) collective-permute-start(bf16[2,128,256]{2,1,0:T(8,128)(2,1)S(1)} %slice.128), channel_id=1, source_target_pairs={{0,4},{2,6},{4,0},{6,2},{8,12},{10,14},{12,8},{14,10},{1,5},{3,7},... | collective-permute-start | bytes 393224 | tf_op jit(solution)/shard_map/ppermute | solution.py:30
  68.6 5.0 %collective-permute-start.8 = (bf16[2,128,256]{2,1,0:T(8,128)(2,1)S(1)}, bf16[2,128,256]{2,1,0:T(8,128)(2,1)S(1)}, u32[]{:S(2)}, u32[]{:S(2)}) collective-permute-start(bf16[2,128,256]{2,1,0:T(8,128)(2,1)S(1)} %slice.127), channel_id=1, source_target_pairs={{0,4},{2,6},{4,0},{6,2},{8,12},{10,14},{12,8},{14,10},{1,5},{3,7},... | collective-permute-start | bytes 393224 | tf_op jit(solution)/shard_map/ppermute | solution.py:30
  70.1 13.8 %copy-start.5 = (f32[2,128,256]{2,1,0:T(8,128)}, f32[2,128,256]{2,1,0:T(8,128)S(1)}, u32[]{:S(2)}) copy-start(f32[2,128,256]{2,1,0:T(8,128)S(1)} %slice_add_fusion.3.refs_2_) | copy-start | bytes 786436
  73.6 5.2 %collective-permute-start.15 = (f32[2,1,128]{0,2,1:T(8,128)S(1)}, f32[2,1,128]{0,2,1:T(8,128)S(1)}, u32[]{:S(2)}, u32[]{:S(2)}) collective-permute-start(f32[2,1,128]{0,2,1:T(8,128)S(1)} %slice.107), channel_id=1, source_target_pairs={{0,8},{2,10},{4,12},{6,14},{8,0},{10,2},{12,4},{14,6},{1,9},{3,11}... | collective-permute-start | bytes 3080 | tf_op jit(solution)/shard_map/ppermute | solution.py:30
  74.0 10.0 %copy-start.6 = (f32[2,128,256]{2,1,0:T(8,128)}, f32[2,128,256]{2,1,0:T(8,128)S(1)}, u32[]{:S(2)}) copy-start(f32[2,128,256]{2,1,0:T(8,128)S(1)} %slice_add_fusion.2.refs_3_) | copy-start | bytes 786436
  74.0 7.9 %collective-permute-start.11 = (bf16[1,128,256]{2,1,0:T(8,128)(2,1)S(1)}, bf16[1,128,256]{2,1,0:T(8,128)(2,1)S(1)}, u32[]{:S(2)}, u32[]{:S(2)}) collective-permute-start(bf16[1,128,256]{2,1,0:T(8,128)(2,1)S(1)} %slice.132), channel_id=1, source_target_pairs={{0,8},{2,10},{4,12},{6,14},{8,0},{10,2},{12,4},{14,6},{1,9},{3,11}... | collective-permute-start | bytes 196616 | tf_op jit(solution)/shard_map/ppermute | solution.py:30
  78.7 5.2 %collective-permute-start.12 = (bf16[1,128,256]{2,1,0:T(8,128)(2,1)S(1)}, bf16[1,128,256]{2,1,0:T(8,128)(2,1)S(1)}, u32[]{:S(2)}, u32[]{:S(2)}) collective-permute-start(bf16[1,128,256]{2,1,0:T(8,128)(2,1)S(1)} %slice.131), channel_id=1, source_target_pairs={{0,8},{2,10},{4,12},{6,14},{8,0},{10,2},{12,4},{14,6},{1,9},{3,11}... | collective-permute-start | bytes 196616 | tf_op jit(solution)/shard_map/ppermute | solution.py:30
  80.0 3.9 %copy-start.13 = (bf16[128,512]{1,0:T(8,128)(2,1)}, bf16[128,512]{1,0:T(8,128)(2,1)S(1)}, u32[]{:S(2)}) copy-start(bf16[128,512]{1,0:T(8,128)(2,1)S(1)} %collective-permute-done.16.refs_12_) | copy-start | bytes 393220
  80.0 3.9 %copy-start.14 = (f32[64,512]{1,0:T(8,128)}, f32[64,512]{1,0:T(8,128)S(1)}, u32[]{:S(2)}) copy-start(f32[64,512]{1,0:T(8,128)S(1)} %collective-permute-done.17.refs_14_) | copy-start | bytes 393220
  81.9 2.1 %copy-start.16 = (bf16[1,128,256]{2,1,0:T(8,128)(2,1)}, bf16[1,128,256]{2,1,0:T(8,128)(2,1)S(1)}, u32[]{:S(2)}) copy-start(bf16[1,128,256]{2,1,0:T(8,128)(2,1)S(1)} %collective-permute-done.11.refs_6_) | copy-start | bytes 196612
  83.9 0.6 copy-start.17
  88.4 1.6 %collective-permute-start.18 = (f32[264,128]{1,0:T(8,128)}, f32[264,128]{1,0:T(8,128)S(1)}, u32[]{:S(2)}, u32[]{:S(2)}) collective-permute-start(f32[264,128]{1,0:T(8,128)} %get-tuple-element.52), channel_id=1, source_target_pairs={{0,1},{1,0},{2,3},{3,2},{4,5},{5,4},{6,7},{7,6},{8,9},{9,8},{10,11... | collective-permute-start | bytes 405512 | tf_op jit(solution)/shard_map/ppermute | solution.py:34
  89.9 0.7 copy-start.12
  92.2 8.4 %collective-permute-start.19 = (bf16[416,128]{1,0:T(8,128)(2,1)}, bf16[416,128]{1,0:T(8,128)(2,1)S(1)}, u32[]{:S(2)}, u32[]{:S(2)}) collective-permute-start(bf16[416,128]{1,0:T(8,128)(2,1)} %joined.3.mine_ref), channel_id=1, source_target_pairs={{0,8},{2,10},{4,12},{6,14},{8,0},{10,2},{12,4},{14,6},{1,9},{3,11}... | collective-permute-start | bytes 319496 | tf_op jit(solution)/shard_map/ppermute | solution.py:30
  100.6 0.7 copy-start.15
  102.9 5.3 %collective-permute-start.20 = (bf16[544,128]{1,0:T(8,128)(2,1)}, bf16[544,128]{1,0:T(8,128)(2,1)S(1)}, u32[]{:S(2)}, u32[]{:S(2)}) collective-permute-start(bf16[544,128]{1,0:T(8,128)(2,1)} %joined.4.mine_ref), channel_id=1, source_target_pairs={{0,4},{2,6},{4,0},{6,2},{8,12},{10,14},{12,8},{14,10},{1,5},{3,7},... | collective-permute-start | bytes 417800 | tf_op jit(solution)/shard_map/ppermute | solution.py:30
  108.2 0.7 copy-start.11
  110.5 6.0 %collective-permute-start.21 = (bf16[800,128]{1,0:T(8,128)(2,1)}, bf16[800,128]{1,0:T(8,128)(2,1)S(1)}, u32[]{:S(2)}, u32[]{:S(2)}) collective-permute-start(bf16[800,128]{1,0:T(8,128)(2,1)} %joined.5.mine_ref), channel_id=1, source_target_pairs={{0,2},{2,0},{4,6},{6,4},{8,10},{10,8},{12,14},{14,12},{1,3},{3,1},... | collective-permute-start | bytes 614408 | tf_op jit(solution)/shard_map/ppermute | solution.py:30
  116.5 0.7 copy-start.10
  121.9 1.8 %collective-permute-start.22 = (f32[512,128]{1,0:T(8,128)}, f32[512,128]{1,0:T(8,128)S(1)}, u32[]{:S(2)}, u32[]{:S(2)}) collective-permute-start(f32[512,128]{1,0:T(8,128)} %get-tuple-element.56), channel_id=1, source_target_pairs={{0,1},{1,0},{2,3},{3,2},{4,5},{5,4},{6,7},{7,6},{8,9},{9,8},{10,11... | collective-permute-start | bytes 786440 | tf_op jit(solution)/shard_map/ppermute | solution.py:34

commit v4 on v3

--- a/solution.py
+++ b/solution.py
@@ -38,6 +38,12 @@
     return lax.dot_general(
         lhs, rhs, (((lhs_dim,), (rhs_dim,)), ((), ())), preferred_element_type=F32
     )
+
+
+def gain_row(gain_ref, mine):
+    if len(gain_ref.shape) == 1:
+        return gain_ref[mine].reshape(1, mine.size).astype(F32)
+    return gain_ref[:, mine].astype(F32)
 
 
 def block_products(here, bits, block, chunks, x_ref, table_ref, outs):
@@ -94,8 +100,8 @@
     ]
     for copy in copies:
         copy.start()
-    gain_in = gain_in_ref[:, mine].astype(F32)
-    gain_both = gain_in * gain_out_ref[:, mine].astype(F32)
+    gain_in = gain_row(gain_in_ref, mine)
+    gain_both = gain_in * gain_row(gain_out_ref, mine)
     copies[0].wait()
     scaled_ref[...] = (head_ref[...].astype(F32) * gain_both).astype(BF16)
     table_ref[2 * rank :, :] = scaled_ref[...]
@@ -135,6 +141,8 @@
 
 
 def far_kernel(bits, block, chunks, x_ref, table_ref, *outs):
+    outs, zero_ref = outs[:-1], outs[-1]
+    zero_ref[...] = jnp.zeros(zero_ref.shape, F32)
     pairs = list(zip(outs[0::2], outs[1::2]))
     block_products(lax.axis_index("seq"), bits, block, chunks, x_ref, table_ref, pairs)
 
@@ -142,6 +150,7 @@
 def far_products(x, table, chunks, count, block):
     bits = count.bit_length() - 1
     shapes = chunk_shapes(chunks, count, block)
+    shapes.append(jax.ShapeDtypeStruct((1, LANES), F32))
     return pl.pallas_call(
         functools.partial(far_kernel, bits, block, chunks),
         in_specs=[VMEM] * 2,
@@ -322,10 +331,10 @@
     ).astype(BF16)
     packed = summed[parts * rank :, :]
     gram = jnp.concatenate([packed[:, :rank], packed[:, rank:]], axis=0).astype(BF16)
-    from_x = mm(order_ref[...], x_ref[...], 0, 0) * gain_in_ref[:, mine].astype(F32)
+    from_x = mm(order_ref[...], x_ref[...], 0, 0) * gain_row(gain_in_ref, mine)
     for copy in copies:
         copy.wait()
-    from_head = mm(table, head_ref[...], 1, 0) * gain_out_ref[:, mine].astype(F32)
+    from_head = mm(table, head_ref[...], 1, 0) * gain_row(gain_out_ref, mine)
     from_out = mm(gram, small_ref[...], 1, 0)
     total = jnp.concatenate([from_x[:rank], from_x[rank:] + from_head + from_out], axis=0)
     turned_ref[...] = total.T
@@ -369,7 +378,9 @@
     half = rank // 2
     slice_width = head.shape[0]
     vocabulary = 2 * slice_width
-    in_row, out_row = in_gain.reshape(1, depth), final_gain.reshape(1, depth)
+    in_row, out_row = in_gain, final_gain
+    if columns % (2 * LANES):
+        in_row, out_row = in_gain.reshape(1, depth), final_gain.reshape(1, depth)
 
     width = 2 * rank + slice_width
     early = [(0, width - 256, False), (width - 256, 256, True)]
@@ -412,14 +423,14 @@
             swap_with(send, (1 << (1 - step if flip and step < 2 else step)), count)
             for send, flip in zip(sends, flips)
         ]
-        if step == 0:
-            first_gots, _ = lax.optimization_barrier((gots[: len(early)], more[0]))
-            gots = list(first_gots) + gots[len(early) :]
         left = count >> (step + 1)
         stats = stats[:, :left] + swap_with(stats[:, left:], 1 << step, count)
         if step == bits - 1:
             break
         keeps = [keep[:left] + got.astype(F32) for keep, got in zip(keeps, gots)]
+        if step == 0:
+            for index, (_, wide, _) in enumerate(early):
+                keeps[index] = keeps[index] + jnp.broadcast_to(more[-1][0, 0], keeps[index].shape)
         sends = [value[left // 2 :].astype(BF16) for value in keeps]
 
     factor, table, away, gram_out = owner_step(

time: 126 us -> 120 us (0.952)
  starting transfers between devices: 26.9 us -> 21.1 us
  other arithmetic: 11.5 us -> 14 us
  local copies, waits for them, and re-layouts: 12 us -> 10 us
    ppermute x18, starting transfers between devices: 26.2 us -> 19.9 us  [swap_with(): return lax.ppermute(value, 'seq', [(i, i ^ bit) for i in range(count)])]
    add x0 -> x2, other arithmetic: none -> 3.7 us  [on_device(): keeps[index] + jnp.broadcast_to(more[-1][0, 0], keeps[index].shape)]
    reshape x2 -> x0, local copies, waits for them, and re-layouts: 2.68 us -> none  [on_device(): in_row, out_row = (in_gain.reshape(1, depth), final_gain.reshape(1, depth))]
    unnamed x40 -> x54, local copies, waits for them, and re-layouts: 3.3 us -> 4.94 us
    add x8 -> x6, other arithmetic: 4.49 us -> 3.24 us  [on_device(): keeps = [keep[:left] + got.astype(F32) for keep, got in zip(keeps, gots)]]
  transfers between devices with their start and end apart: 23 -> 23, of which waited for: 15 -> 12; matrix products, arithmetic and copies ran while one was open for 18% -> 21% of each run, Pallas kernels for 3% -> 4%
where the time goes in v4:
time: 120 us; the launch traced here: 119 us
  waiting for transfers between devices  42.4 us (35%)
  Pallas kernels  23.7 us (20%)
  starting transfers between devices  21.1 us (18%)
  other arithmetic  14 us (12%)
  local copies, waits for them, and re-layouts  10 us (8%)
  matrix products  7.19 us (6%)
    ppermute x18, waiting for transfers between devices, swap_with(): return lax.ppermute(value, 'seq', [(i, i ^ bit) for i in range(count)])  39.1 us
    ppermute x18, starting transfers between devices, swap_with(): return lax.ppermute(value, 'seq', [(i, i ^ bit) for i in range(count)])  19.9 us
    dot_general x2, matrix products, mm(): lax.dot_general(lhs, rhs, (((lhs_dim,), (rhs_dim,)), ((), ())), preferred...  7.19 us
    pallas_call x1, Pallas kernels, own_products(): pl.pallas_call(functools.partial(own_kernel, bits, block, chunks), in_spe...  6.04 us
    pallas_call x3, Pallas kernels, joined(): pl.pallas_call(kernel, in_specs=[VMEM] * len(operands), out_specs=VMEM, o...  4.98 us
    unnamed x54, local copies, waits for them, and re-layouts  4.94 us
    pallas_call x1, Pallas kernels, final_step(): pl.pallas_call(functools.partial(final_kernel, bits, block, rank), in_spe...  4.66 us
    pallas_call x1, Pallas kernels, far_products(): pl.pallas_call(functools.partial(far_kernel, bits, block, chunks), in_spe...  4.22 us
  transfers between devices with their start and end apart: 23, of which 12 were waited for; matrix products, arithmetic and copies ran while one was open for 21% of the time, Pallas kernels for 4%

profile of v4, /device:TPU:0, one launch (start us, length us, event | category | flops | bytes accessed | tf_op | source)
XLA Modules:
  0.0 119.5 jit_solution(6408071712172095298)
XLA Ops:
  0.7 6.0 %own_products.1 = (bf16[4,128,384]{2,1,0:T(8,128)(2,1)}, f32[4,128,384]{2,1,0:T(8,128)}, bf16[4,128,256]{2,1,0:T(8,128)(2,1)}, f32[4,128,256]{2,1,0:T(8,128)}, bf16[512,1024]{1,0:T(8,128)(2,1)}) custom-call(bf16[1024,1024]{1,0:T(8,128)(2,1)} %bitcast.25, bf16[512,8192]{1,0:T(8,128)(2,1)} %head_hbm.3, bf16[64,8192]{1,0:T(8,128)(2,1)} %in_hbm.1, ...), custom_call_target="tpu_custom_call" | custom-call | flops 1342177280 | bytes 3407872 | tf_op jit(solution)/shard_map/own_products/pallas_call | solution.py:122
  7.3 2.6 %collective-permute-start = (bf16[4,128,384]{2,1,0:T(8,128)(2,1)}, bf16[4,128,384]{2,1,0:T(8,128)(2,1)S(1)}, u32[]{:S(2)}, u32[]{:S(2)}) collective-permute-start(bf16[4,128,384]{2,1,0:T(8,128)(2,1)} %get-tuple-element.31), channel_id=1, source_target_pairs={{0,2},{2,0},{4,6},{6,4},{8,10},{10,8},{12,14},{14,12},{1,3},{3,1},... | collective-permute-start | bytes 1179656 | tf_op jit(solution)/shard_map/ppermute | solution.py:30
  9.8 1.6 %collective-permute-start.3 = (bf16[4,128,256]{2,1,0:T(8,128)(2,1)}, bf16[4,128,256]{2,1,0:T(8,128)(2,1)}, u32[]{:S(2)}, u32[]{:S(2)}) collective-permute-start(bf16[4,128,256]{2,1,0:T(8,128)(2,1)} %get-tuple-element.40), channel_id=1, source_target_pairs={{0,4},{2,6},{4,0},{6,2},{8,12},{10,14},{12,8},{14,10},{1,5},{3,7},... | collective-permute-start | bytes 786440 | tf_op jit(solution)/shard_map/ppermute | solution.py:30
  11.5 4.2 %far_products.1 = (bf16[4,128,256]{2,1,0:T(8,128)(2,1)}, f32[4,128,256]{2,1,0:T(8,128)}, bf16[4,128,256]{2,1,0:T(8,128)(2,1)}, f32[4,128,256]{2,1,0:T(8,128)}, f32[1,128]{1,0:T(1,128)}) custom-call(bf16[1024,1024]{1,0:T(8,128)(2,1)} %bitcast.26, bf16[512,1024]{1,0:T(8,128)(2,1)} %collective-permute-done.1.table_ref), custom_call_target="tpu_custom_call" | custom-call | flops 1073741824 | bytes 3145728 | tf_op jit(solution)/shard_map/far_products/pallas_call | solution.py:154
  15.7 1.3 %collective-permute-start.5 = (bf16[4,128,256]{2,1,0:T(8,128)(2,1)}, bf16[4,128,256]{2,1,0:T(8,128)(2,1)}, u32[]{:S(2)}, u32[]{:S(2)}) collective-permute-start(bf16[4,128,256]{2,1,0:T(8,128)(2,1)} %get-tuple-element.33), channel_id=1, source_target_pairs={{0,2},{2,0},{4,6},{6,4},{8,10},{10,8},{12,14},{14,12},{1,3},{3,1},... | collective-permute-start | bytes 786440 | tf_op jit(solution)/shard_map/ppermute | solution.py:30
  17.0 0.7 collective-permute-start.7
  17.7 2.3 %collective-permute-done = bf16[4,128,384]{2,1,0:T(8,128)(2,1)S(1)} collective-permute-done((bf16[4,128,384]{2,1,0:T(8,128)(2,1)}, bf16[4,128,384]{2,1,0:T(8,128)(2,1)S(1)}, u32[]{:S(2)}, u32[]{:S(2)}) %collective-permute-start) | collective-permute-done | bytes 393248 | tf_op jit(solution)/shard_map/ppermute | solution.py:30
  20.0 1.9 %add_add_fusion = f32[4,128,384]{2,1,0:T(8,128)S(1)} fusion(f32[4,128,384]{2,1,0:T(8,128)} %get-tuple-element.30, bf16[4,128,384]{2,1,0:T(8,128)(2,1)S(1)} %collective-permute-done, f32[]{:T(128)} %bitcast.33), kind=kLoop, calls=%fused_computation.7 | loop fusion | flops 589824 | bytes 1966084 | tf_op jit(solution)/shard_map/add | solution.py:433
  21.9 0.9 copy-done.3
  22.8 0.7 slice.131
  23.5 2.1 %collective-permute-start.2 = (bf16[2,128,384]{2,1,0:T(8,128)(2,1)}, bf16[2,128,384]{2,1,0:T(8,128)(2,1)}, u32[]{:S(2)}, u32[]{:S(2)}) collective-permute-start(bf16[2,128,384]{2,1,0:T(8,128)(2,1)} %slice.131), channel_id=1, source_target_pairs={{0,4},{2,6},{4,0},{6,2},{8,12},{10,14},{12,8},{14,10},{1,5},{3,7},... | collective-permute-start | bytes 589832 | tf_op jit(solution)/shard_map/ppermute | solution.py:30
  25.6 1.8 %add_add_fusion.1 = f32[4,128,256]{2,1,0:T(8,128)S(1)} fusion(f32[4,128,256]{2,1,0:T(8,128)} %get-tuple-element.39, bf16[4,128,256]{2,1,0:T(8,128)(2,1)} %collective-permute-done.3, f32[]{:T(128)} %bitcast.34), kind=kLoop, calls=%fused_computation.10 | loop fusion | flops 393216 | bytes 1310724 | tf_op jit(solution)/shard_map/add | solution.py:433
  27.4 0.8 copy-done.6
  28.9 1.5 %collective-permute-start.4 = (bf16[2,128,256]{2,1,0:T(8,128)(2,1)}, bf16[2,128,256]{2,1,0:T(8,128)(2,1)S(1)}, u32[]{:S(2)}, u32[]{:S(2)}) collective-permute-start(bf16[2,128,256]{2,1,0:T(8,128)(2,1)} %slice.134), channel_id=1, source_target_pairs={{0,2},{2,0},{4,6},{6,4},{8,10},{10,8},{12,14},{14,12},{1,3},{3,1},... | collective-permute-start | bytes 393224 | tf_op jit(solution)/shard_map/ppermute | solution.py:30
  30.4 0.7 convert_multiply_fusion.1
  31.1 0.8 fusion
  34.1 0.7 convert_element_type.70
  34.8 1.0 fusion.9.refs_15_
  36.1 0.7 dynamic-slice_bitcast_fusion
  36.9 6.2 %fusion.1.refs_13_ = f32[64,512]{1,0:T(8,128)S(1)} fusion(bf16[512,8192]{1,0:T(8,128)(2,1)} %head_hbm.3, bf16[64,8192]{1,0:T(8,128)(2,1)S(1)} %copy-done.1, f32[8192]{0:T(1024)S(1)} %convert_element_type.70), kind=kOutput, calls=%fused_computation.5 | convolution fusion | flops 538443776 | bytes 9601024 | tf_op jit(solution)/shard_map/dot_general | solution.py:38
  43.1 0.8 pad_maximum_fusion.refs_10_
  44.0 0.7 copy.32.refs_9_
  44.7 4.2 %collective-permute-done.14 = f32[2,2,128]{0,2,1:T(8,128)S(1)} collective-permute-done((f32[2,2,128]{0,2,1:T(8,128)S(1)}, f32[2,2,128]{0,2,1:T(8,128)S(1)}, u32[]{:S(2)}, u32[]{:S(2)}) %collective-permute-start.14) | collective-permute-done | bytes 2080 | tf_op jit(solution)/shard_map/ppermute | solution.py:30
  49.6 2.7 %collective-permute-start.15 = (f32[2,1,128]{0,2,1:T(8,128)S(1)}, f32[2,1,128]{0,2,1:T(8,128)S(1)}, u32[]{:S(2)}, u32[]{:S(2)}) collective-permute-start(f32[2,1,128]{0,2,1:T(8,128)S(1)} %slice.112), channel_id=1, source_target_pairs={{0,8},{2,10},{4,12},{6,14},{8,0},{10,2},{12,4},{14,6},{1,9},{3,11}... | collective-permute-start | bytes 3080 | tf_op jit(solution)/shard_map/ppermute | solution.py:30
  52.3 1.0 slice_add_fusion.refs_0_
  53.7 1.2 convert_add_fusion.1
  55.1 1.0 convert_add_fusion
  56.2 5.0 %collective-permute-done.6 = bf16[2,128,256]{2,1,0:T(8,128)(2,1)S(1)} collective-permute-done((bf16[2,128,256]{2,1,0:T(8,128)(2,1)S(1)}, bf16[2,128,256]{2,1,0:T(8,128)(2,1)S(1)}, u32[]{:S(2)}, u32[]{:S(2)}) %collective-permute-start.6) | collective-permute-done | bytes 131104 | tf_op jit(solution)/shard_map/ppermute | solution.py:30
  61.3 4.9 %collective-permute-done.8 = bf16[2,128,256]{2,1,0:T(8,128)(2,1)S(1)} collective-permute-done((bf16[2,128,256]{2,1,0:T(8,128)(2,1)S(1)}, bf16[2,128,256]{2,1,0:T(8,128)(2,1)S(1)}, u32[]{:S(2)}, u32[]{:S(2)}) %collective-permute-start.8) | collective-permute-done | bytes 131104 | tf_op jit(solution)/shard_map/ppermute | solution.py:30
  66.2 1.7 %collective-permute-start.9 = (bf16[1,128,384]{2,1,0:T(8,128)(2,1)S(1)}, bf16[1,128,384]{2,1,0:T(8,128)(2,1)S(1)}, u32[]{:S(2)}, u32[]{:S(2)}) collective-permute-start(bf16[1,128,384]{2,1,0:T(8,128)(2,1)S(1)} %slice.135), channel_id=1, source_target_pairs={{0,8},{2,10},{4,12},{6,14},{8,0},{10,2},{12,4},{14,6},{1,9},{3,11}... | collective-permute-start | bytes 294920 | tf_op jit(solution)/shard_map/ppermute | solution.py:30
  67.9 1.3 %collective-permute-start.11 = (bf16[1,128,256]{2,1,0:T(8,128)(2,1)S(1)}, bf16[1,128,256]{2,1,0:T(8,128)(2,1)S(1)}, u32[]{:S(2)}, u32[]{:S(2)}) collective-permute-start(bf16[1,128,256]{2,1,0:T(8,128)(2,1)S(1)} %slice.137), channel_id=1, source_target_pairs={{0,8},{2,10},{4,12},{6,14},{8,0},{10,2},{12,4},{14,6},{1,9},{3,11}... | collective-permute-start | bytes 196616 | tf_op jit(solution)/shard_map/ppermute | solution.py:30
  69.3 1.7 %collective-permute-start.12 = (bf16[1,128,256]{2,1,0:T(8,128)(2,1)S(1)}, bf16[1,128,256]{2,1,0:T(8,128)(2,1)S(1)}, u32[]{:S(2)}, u32[]{:S(2)}) collective-permute-start(bf16[1,128,256]{2,1,0:T(8,128)(2,1)S(1)} %slice.136), channel_id=1, source_target_pairs={{0,8},{2,10},{4,12},{6,14},{8,0},{10,2},{12,4},{14,6},{1,9},{3,11}... | collective-permute-start | bytes 196616 | tf_op jit(solution)/shard_map/ppermute | solution.py:30
  71.6 5.0 %collective-permute-done.9.refs_4_ = bf16[1,128,384]{2,1,0:T(8,128)(2,1)S(1)} collective-permute-done((bf16[1,128,384]{2,1,0:T(8,128)(2,1)S(1)}, bf16[1,128,384]{2,1,0:T(8,128)(2,1)S(1)}, u32[]{:S(2)}, u32[]{:S(2)}) %collective-permute-start.9) | collective-permute-done | bytes 98336 | tf_op jit(solution)/shard_map/ppermute | solution.py:30
  76.6 0.7 collective-permute-done.11.refs_6_
  77.3 0.7 collective-permute-done.12.refs_7_
  78.6 3.8 %owner.1 = (bf16[128,128]{1,0:T(8,128)(2,1)}, f32[264,128]{1,0:T(8,128)}, f32[264,128]{1,0:T(8,128)}, bf16[32,128]{1,0:T(8,128)(2,1)}) custom-call(f32[2,128,384]{2,1,0:T(8,128)} %copy-done.5, f32[2,128,256]{2,1,0:T(8,128)} %copy-done.8, f32[2,128,256]{2,1,0:T(8,128)} %copy-done.9, f32[2,128,256]{2,1,0:T(8,128)} %copy-done.10, ...), custom_call_target="tpu_custom_call" | custom-call | tf_op jit(solution)/shard_map/owner/pallas_call | solution.py:260
  82.4 1.6 %collective-permute-done.18.got_ref = f32[264,128]{1,0:T(8,128)S(1)} collective-permute-done((f32[264,128]{1,0:T(8,128)}, f32[264,128]{1,0:T(8,128)S(1)}, u32[]{:S(2)}, u32[]{:S(2)}) %collective-permute-start.18) | collective-permute-done | bytes 135200 | tf_op jit(solution)/shard_map/ppermute | solution.py:34
  84.6 1.7 %joined.3.mine_ref = bf16[416,128]{1,0:T(8,128)(2,1)} custom-call(bf16[128,128]{1,0:T(8,128)(2,1)} %get-tuple-element.50.factor_ref, f32[264,128]{1,0:T(8,128)} %get-tuple-element.51.table_ref, f32[264,128]{1,0:T(8,128)} %copy-done.16, bf16[32,128]{1,0:T(8,128)(2,1)} %get-tuple-element.53.gram_ref), custom_call_target="tpu_custom_call" | custom-call | tf_op jit(solution)/shard_map/joined/pallas_call | solution.py:291
  86.3 8.4 %collective-permute-done.19.got_ref = bf16[416,128]{1,0:T(8,128)(2,1)S(1)} collective-permute-done((bf16[416,128]{1,0:T(8,128)(2,1)}, bf16[416,128]{1,0:T(8,128)(2,1)S(1)}, u32[]{:S(2)}, u32[]{:S(2)}) %collective-permute-start.19) | collective-permute-done | bytes 106528 | tf_op jit(solution)/shard_map/ppermute | solution.py:30
  95.3 1.6 %joined.4.mine_ref = bf16[544,128]{1,0:T(8,128)(2,1)} custom-call(bf16[416,128]{1,0:T(8,128)(2,1)} %joined.3.mine_ref, bf16[416,128]{1,0:T(8,128)(2,1)} %copy-done.20), custom_call_target="tpu_custom_call" | custom-call | tf_op jit(solution)/shard_map/joined/pallas_call | solution.py:291
  98.9 3.4 %collective-permute-done.20.got_ref = bf16[544,128]{1,0:T(8,128)(2,1)S(1)} collective-permute-done((bf16[544,128]{1,0:T(8,128)(2,1)}, bf16[544,128]{1,0:T(8,128)(2,1)S(1)}, u32[]{:S(2)}, u32[]{:S(2)}) %collective-permute-start.20) | collective-permute-done | bytes 139296 | tf_op jit(solution)/shard_map/ppermute | solution.py:30
  102.9 1.7 %joined.5.mine_ref = bf16[800,128]{1,0:T(8,128)(2,1)} custom-call(bf16[544,128]{1,0:T(8,128)(2,1)} %joined.4.mine_ref, bf16[544,128]{1,0:T(8,128)(2,1)} %copy-done.15), custom_call_target="tpu_custom_call" | custom-call | tf_op jit(solution)/shard_map/joined/pallas_call | solution.py:291
  104.6 1.5 %collective-permute-start.21 = (bf16[800,128]{1,0:T(8,128)(2,1)}, bf16[800,128]{1,0:T(8,128)(2,1)S(1)}, u32[]{:S(2)}, u32[]{:S(2)}) collective-permute-start(bf16[800,128]{1,0:T(8,128)(2,1)} %joined.5.mine_ref), channel_id=1, source_target_pairs={{0,2},{2,0},{4,6},{6,4},{8,10},{10,8},{12,14},{14,12},{1,3},{3,1},... | collective-permute-start | bytes 614408 | tf_op jit(solution)/shard_map/ppermute | solution.py:30
  106.1 4.5 %collective-permute-done.21.got_ref = bf16[800,128]{1,0:T(8,128)(2,1)S(1)} collective-permute-done((bf16[800,128]{1,0:T(8,128)(2,1)}, bf16[800,128]{1,0:T(8,128)(2,1)S(1)}, u32[]{:S(2)}, u32[]{:S(2)}) %collective-permute-start.21) | collective-permute-done | bytes 204832 | tf_op jit(solution)/shard_map/ppermute | solution.py:30
  110.6 0.7 copy-done.14
  111.3 4.7 %final.1 = (f32[512,128]{1,0:T(8,128)}, f32[512,128]{1,0:T(8,128)}) custom-call(bf16[1024,1024]{1,0:T(8,128)(2,1)} %bitcast.27, bf16[512,8192]{1,0:T(8,128)(2,1)} %head_hbm.3, bf16[64,8192]{1,0:T(8,128)(2,1)} %out_hbm.3, bf16[8192]{0:T(1024)(128)(2,1)} %gain_in_ref.3, bf16[8192]{0:T(1024)(128)(2,1)} %gain_out_ref.3, bf16[800,128]{1,0:T(8,128)(2,1)} %joined.5.mine_ref, ...), custom_call_target="tpu_custom_call" | custom-call | tf_op jit(solution)/shard_map/final/pallas_call | solution.py:351
  116.0 1.7 %collective-permute-done.22 = f32[512,128]{1,0:T(8,128)S(1)} collective-permute-done((f32[512,128]{1,0:T(8,128)}, f32[512,128]{1,0:T(8,128)S(1)}, u32[]{:S(2)}, u32[]{:S(2)}) %collective-permute-start.22) | collective-permute-done | bytes 262176 | tf_op jit(solution)/shard_map/ppermute | solution.py:34
  117.8 1.7 %add.96 = f32[512,128]{1,0:T(8,128)} add(f32[512,128]{1,0:T(8,128)} %get-tuple-element.55, f32[512,128]{1,0:T(8,128)S(1)} %collective-permute-done.22) | non-fusion elementwise | flops 65536 | bytes 786432 | tf_op jit(solution)/shard_map/add | solution.py:462
  (105 shorter events, 10.5 us)
Async XLA Ops:
  0.6 35.2 %copy-start = (s32[2,128]{1,0:T(2,128)S(1)}, s32[2,128]{1,0:T(2,128)}, u32[]{:S(2)}) copy-start(s32[2,128]{1,0:T(2,128)} %param.14) | copy-start | bytes 3076
  0.6 10.8 %copy-start.25 = (s32[8]{0:T(128)S(1)}, s32[8]{0:T(128)}, u32[]{:S(2)}) copy-start(s32[8]{0:T(128)} %constant.61.clone) | copy-start | bytes 100
  6.7 24.4 %copy-start.2 = (bf16[1,1024,1024]{2,1,0:T(8,128)(2,1)S(1)}, bf16[1,1024,1024]{2,1,0:T(8,128)(2,1)}, u32[]{:S(2)}) copy-start(bf16[1,1024,1024]{2,1,0:T(8,128)(2,1)} %param.11) | copy-start | bytes 6291460
  6.7 4.7 %collective-permute-start.1 = (bf16[512,1024]{1,0:T(8,128)(2,1)}, bf16[512,1024]{1,0:T(8,128)(2,1)}, u32[]{:S(2)}, u32[]{:S(2)}) collective-permute-start(bf16[512,1024]{1,0:T(8,128)(2,1)} %get-tuple-element.32), channel_id=1, source_target_pairs={{0,1},{1,0},{2,3},{3,2},{4,5},{5,4},{6,7},{7,6},{8,9},{9,8},{10,11... | collective-permute-start | bytes 3145736 | tf_op jit(solution)/shard_map/ppermute | solution.py:34
  7.3 12.7 %collective-permute-start = (bf16[4,128,384]{2,1,0:T(8,128)(2,1)}, bf16[4,128,384]{2,1,0:T(8,128)(2,1)S(1)}, u32[]{:S(2)}, u32[]{:S(2)}) collective-permute-start(bf16[4,128,384]{2,1,0:T(8,128)(2,1)} %get-tuple-element.31), channel_id=1, source_target_pairs={{0,2},{2,0},{4,6},{6,4},{8,10},{10,8},{12,14},{14,12},{1,3},{3,1},... | collective-permute-start | bytes 1179656 | tf_op jit(solution)/shard_map/ppermute | solution.py:30
  9.8 15.8 %collective-permute-start.3 = (bf16[4,128,256]{2,1,0:T(8,128)(2,1)}, bf16[4,128,256]{2,1,0:T(8,128)(2,1)}, u32[]{:S(2)}, u32[]{:S(2)}) collective-permute-start(bf16[4,128,256]{2,1,0:T(8,128)(2,1)} %get-tuple-element.40), channel_id=1, source_target_pairs={{0,4},{2,6},{4,0},{6,2},{8,12},{10,14},{12,8},{14,10},{1,5},{3,7},... | collective-permute-start | bytes 786440 | tf_op jit(solution)/shard_map/ppermute | solution.py:30
  15.7 19.1 %copy-start.1 = (bf16[64,8192]{1,0:T(8,128)(2,1)S(1)}, bf16[64,8192]{1,0:T(8,128)(2,1)}, u32[]{:S(2)}) copy-start(bf16[64,8192]{1,0:T(8,128)(2,1)} %out_hbm.3) | copy-start | bytes 3145732
  15.7 37.6 %collective-permute-start.5 = (bf16[4,128,256]{2,1,0:T(8,128)(2,1)}, bf16[4,128,256]{2,1,0:T(8,128)(2,1)}, u32[]{:S(2)}, u32[]{:S(2)}) collective-permute-start(bf16[4,128,256]{2,1,0:T(8,128)(2,1)} %get-tuple-element.33), channel_id=1, source_target_pairs={{0,2},{2,0},{4,6},{6,4},{8,10},{10,8},{12,14},{14,12},{1,3},{3,1},... | collective-permute-start | bytes 786440 | tf_op jit(solution)/shard_map/ppermute | solution.py:30
  17.0 37.9 %collective-permute-start.7 = (bf16[4,128,256]{2,1,0:T(8,128)(2,1)}, bf16[4,128,256]{2,1,0:T(8,128)(2,1)}, u32[]{:S(2)}, u32[]{:S(2)}) collective-permute-start(bf16[4,128,256]{2,1,0:T(8,128)(2,1)} %get-tuple-element.35), channel_id=1, source_target_pairs={{0,2},{2,0},{4,6},{6,4},{8,10},{10,8},{12,14},{14,12},{1,3},{3,1},... | collective-permute-start | bytes 786440 | tf_op jit(solution)/shard_map/ppermute | solution.py:30
  21.9 0.9 copy-start.3
  22.8 13.3 %copy-start.13 = (bf16[2,128,512]{2,1,0:T(8,128)(2,1)S(1)}, bf16[2,128,512]{2,1,0:T(8,128)(2,1)}, u32[]{:S(2)}) copy-start(bf16[2,128,512]{2,1,0:T(8,128)(2,1)} %param.15) | copy-start | bytes 786436
  23.5 26.1 %collective-permute-start.2 = (bf16[2,128,384]{2,1,0:T(8,128)(2,1)}, bf16[2,128,384]{2,1,0:T(8,128)(2,1)}, u32[]{:S(2)}, u32[]{:S(2)}) collective-permute-start(bf16[2,128,384]{2,1,0:T(8,128)(2,1)} %slice.131), channel_id=1, source_target_pairs={{0,4},{2,6},{4,0},{6,2},{8,12},{10,14},{12,8},{14,10},{1,5},{3,7},... | collective-permute-start | bytes 589832 | tf_op jit(solution)/shard_map/ppermute | solution.py:30
  27.4 0.8 copy-start.6
  28.9 20.1 %collective-permute-start.4 = (bf16[2,128,256]{2,1,0:T(8,128)(2,1)}, bf16[2,128,256]{2,1,0:T(8,128)(2,1)S(1)}, u32[]{:S(2)}, u32[]{:S(2)}) collective-permute-start(bf16[2,128,256]{2,1,0:T(8,128)(2,1)} %slice.134), channel_id=1, source_target_pairs={{0,2},{2,0},{4,6},{6,4},{8,10},{10,8},{12,14},{14,12},{1,3},{3,1},... | collective-permute-start | bytes 393224 | tf_op jit(solution)/shard_map/ppermute | solution.py:30
  32.8 11.0 %collective-permute-start.13 = (f32[2,4,128]{0,2,1:T(8,128)S(1)}, f32[2,4,128]{0,2,1:T(8,128)S(1)}, u32[]{:S(2)}, u32[]{:S(2)}) collective-permute-start(f32[2,4,128]{0,2,1:T(8,128)S(1)} %slice.108), channel_id=1, source_target_pairs={{0,2},{2,0},{4,6},{6,4},{8,10},{10,8},{12,14},{14,12},{1,3},{3,1},... | collective-permute-start | bytes 12296 | tf_op jit(solution)/shard_map/ppermute | solution.py:30
  36.9 7.0 %copy-start.26 = (s32[2,128]{1,0:T(2,128)S(1)}, s32[2,128]{1,0:T(2,128)}, u32[]{:S(2)}) copy-start(s32[2,128]{1,0:T(2,128)} %param.13) | copy-start | bytes 3076
  36.9 12.1 %copy-start.19 = (bf16[128,512]{1,0:T(8,128)(2,1)S(1)}, bf16[128,512]{1,0:T(8,128)(2,1)}, u32[]{:S(2)}) copy-start(bf16[128,512]{1,0:T(8,128)(2,1)} %get-tuple-element.62) | copy-start | bytes 393220
  36.9 12.7 %copy-start.7 = (f32[4,128,256]{2,1,0:T(8,128)S(1)}, f32[4,128,256]{2,1,0:T(8,128)}, u32[]{:S(2)}) copy-start(f32[4,128,256]{2,1,0:T(8,128)} %copy-done.6) | copy-start | bytes 1572868
  36.9 15.4 %copy-start.4 = (f32[4,128,384]{2,1,0:T(8,128)S(1)}, f32[4,128,384]{2,1,0:T(8,128)}, u32[]{:S(2)}) copy-start(f32[4,128,384]{2,1,0:T(8,128)} %copy-done.3) | copy-start | bytes 2359300
  43.0 24.9 %copy-start.11 = (f32[64,512]{1,0:T(8,128)}, f32[64,512]{1,0:T(8,128)S(1)}, u32[]{:S(2)}) copy-start(f32[64,512]{1,0:T(8,128)S(1)} %fusion.1.refs_13_) | copy-start | bytes 393220
  43.1 12.1 %copy-start.12 = (f32[4,128,256]{2,1,0:T(8,128)S(1)}, f32[4,128,256]{2,1,0:T(8,128)}, u32[]{:S(2)}) copy-start(f32[4,128,256]{2,1,0:T(8,128)} %get-tuple-element.36) | copy-start | bytes 1572868
  43.9 5.0 %collective-permute-start.14 = (f32[2,2,128]{0,2,1:T(8,128)S(1)}, f32[2,2,128]{0,2,1:T(8,128)S(1)}, u32[]{:S(2)}, u32[]{:S(2)}) collective-permute-start(f32[2,2,128]{0,2,1:T(8,128)S(1)} %slice.110), channel_id=1, source_target_pairs={{0,4},{2,6},{4,0},{6,2},{8,12},{10,14},{12,8},{14,10},{1,5},{3,7},... | collective-permute-start | bytes 6152 | tf_op jit(solution)/shard_map/ppermute | solution.py:30
  48.9 20.3 %collective-permute-start.16 = (bf16[128,512]{1,0:T(8,128)(2,1)S(1)}, bf16[128,512]{1,0:T(8,128)(2,1)S(1)}, u32[]{:S(2)}, u32[]{:S(2)}) collective-permute-start(bf16[128,512]{1,0:T(8,128)(2,1)S(1)} %copy-done.19), channel_id=1, source_target_pairs={{0,1},{1,0},{2,3},{3,2},{4,5},{5,4},{6,7},{7,6},{8,9},{9,8},{10,11... | collective-permute-start | bytes 393224 | tf_op jit(solution)/shard_map/ppermute | solution.py:34
  49.0 22.6 %collective-permute-start.17 = (f32[64,512]{1,0:T(8,128)S(1)}, f32[64,512]{1,0:T(8,128)S(1)}, u32[]{:S(2)}, u32[]{:S(2)}) collective-permute-start(f32[64,512]{1,0:T(8,128)S(1)} %fusion.1.refs_13_), channel_id=1, source_target_pairs={{0,1},{1,0},{2,3},{3,2},{4,5},{5,4},{6,7},{7,6},{8,9},{9,8},{10,11... | collective-permute-start | bytes 393224 | tf_op jit(solution)/shard_map/ppermute | solution.py:34
  49.6 28.4 %copy-start.8 = (f32[2,128,256]{2,1,0:T(8,128)}, f32[2,128,256]{2,1,0:T(8,128)S(1)}, u32[]{:S(2)}) copy-start(f32[2,128,256]{2,1,0:T(8,128)S(1)} %slice_add_fusion.4.refs_1_) | copy-start | bytes 786436
  49.6 18.3 %collective-permute-start.15 = (f32[2,1,128]{0,2,1:T(8,128)S(1)}, f32[2,1,128]{0,2,1:T(8,128)S(1)}, u32[]{:S(2)}, u32[]{:S(2)}) collective-permute-start(f32[2,1,128]{0,2,1:T(8,128)S(1)} %slice.112), channel_id=1, source_target_pairs={{0,8},{2,10},{4,12},{6,14},{8,0},{10,2},{12,4},{14,6},{1,9},{3,11}... | collective-permute-start | bytes 3080 | tf_op jit(solution)/shard_map/ppermute | solution.py:30
  53.3 24.7 %copy-start.5 = (f32[2,128,384]{2,1,0:T(8,128)}, f32[2,128,384]{2,1,0:T(8,128)S(1)}, u32[]{:S(2)}) copy-start(f32[2,128,384]{2,1,0:T(8,128)S(1)} %slice_add_fusion.refs_0_) | copy-start | bytes 1179652
  53.3 18.3 %collective-permute-start.10 = (bf16[1,128,256]{2,1,0:T(8,128)(2,1)S(1)}, bf16[1,128,256]{2,1,0:T(8,128)(2,1)S(1)}, u32[]{:S(2)}, u32[]{:S(2)}) collective-permute-start(bf16[1,128,256]{2,1,0:T(8,128)(2,1)S(1)} %slice.138), channel_id=1, source_target_pairs={{0,8},{2,10},{4,12},{6,14},{8,0},{10,2},{12,4},{14,6},{1,9},{3,11}... | collective-permute-start | bytes 196616 | tf_op jit(solution)/shard_map/ppermute | solution.py:30
  54.9 6.3 %collective-permute-start.6 = (bf16[2,128,256]{2,1,0:T(8,128)(2,1)S(1)}, bf16[2,128,256]{2,1,0:T(8,128)(2,1)S(1)}, u32[]{:S(2)}, u32[]{:S(2)}) collective-permute-start(bf16[2,128,256]{2,1,0:T(8,128)(2,1)S(1)} %slice.133), channel_id=1, source_target_pairs={{0,4},{2,6},{4,0},{6,2},{8,12},{10,14},{12,8},{14,10},{1,5},{3,7},... | collective-permute-start | bytes 393224 | tf_op jit(solution)/shard_map/ppermute | solution.py:30
  61.2 5.0 %collective-permute-start.8 = (bf16[2,128,256]{2,1,0:T(8,128)(2,1)S(1)}, bf16[2,128,256]{2,1,0:T(8,128)(2,1)S(1)}, u32[]{:S(2)}, u32[]{:S(2)}) collective-permute-start(bf16[2,128,256]{2,1,0:T(8,128)(2,1)S(1)} %slice.132), channel_id=1, source_target_pairs={{0,4},{2,6},{4,0},{6,2},{8,12},{10,14},{12,8},{14,10},{1,5},{3,7},... | collective-permute-start | bytes 393224 | tf_op jit(solution)/shard_map/ppermute | solution.py:30
  61.3 16.7 %copy-start.9 = (f32[2,128,256]{2,1,0:T(8,128)}, f32[2,128,256]{2,1,0:T(8,128)S(1)}, u32[]{:S(2)}) copy-start(f32[2,128,256]{2,1,0:T(8,128)S(1)} %slice_add_fusion.3.refs_2_) | copy-start | bytes 786436
  66.2 10.4 %collective-permute-start.9 = (bf16[1,128,384]{2,1,0:T(8,128)(2,1)S(1)}, bf16[1,128,384]{2,1,0:T(8,128)(2,1)S(1)}, u32[]{:S(2)}, u32[]{:S(2)}) collective-permute-start(bf16[1,128,384]{2,1,0:T(8,128)(2,1)S(1)} %slice.135), channel_id=1, source_target_pairs={{0,8},{2,10},{4,12},{6,14},{8,0},{10,2},{12,4},{14,6},{1,9},{3,11}... | collective-permute-start | bytes 294920 | tf_op jit(solution)/shard_map/ppermute | solution.py:30
  67.9 10.1 %copy-start.10 = (f32[2,128,256]{2,1,0:T(8,128)}, f32[2,128,256]{2,1,0:T(8,128)S(1)}, u32[]{:S(2)}) copy-start(f32[2,128,256]{2,1,0:T(8,128)S(1)} %slice_add_fusion.2.refs_3_) | copy-start | bytes 786436
  67.9 9.3 %collective-permute-start.11 = (bf16[1,128,256]{2,1,0:T(8,128)(2,1)S(1)}, bf16[1,128,256]{2,1,0:T(8,128)(2,1)S(1)}, u32[]{:S(2)}, u32[]{:S(2)}) collective-permute-start(bf16[1,128,256]{2,1,0:T(8,128)(2,1)S(1)} %slice.137), channel_id=1, source_target_pairs={{0,8},{2,10},{4,12},{6,14},{8,0},{10,2},{12,4},{14,6},{1,9},{3,11}... | collective-permute-start | bytes 196616 | tf_op jit(solution)/shard_map/ppermute | solution.py:30
  69.3 8.7 %copy-start.17 = (bf16[128,512]{1,0:T(8,128)(2,1)}, bf16[128,512]{1,0:T(8,128)(2,1)S(1)}, u32[]{:S(2)}) copy-start(bf16[128,512]{1,0:T(8,128)(2,1)S(1)} %collective-permute-done.16.refs_12_) | copy-start | bytes 393220
  69.3 8.7 %collective-permute-start.12 = (bf16[1,128,256]{2,1,0:T(8,128)(2,1)S(1)}, bf16[1,128,256]{2,1,0:T(8,128)(2,1)S(1)}, u32[]{:S(2)}, u32[]{:S(2)}) collective-permute-start(bf16[1,128,256]{2,1,0:T(8,128)(2,1)S(1)} %slice.136), channel_id=1, source_target_pairs={{0,8},{2,10},{4,12},{6,14},{8,0},{10,2},{12,4},{14,6},{1,9},{3,11}... | collective-permute-start | bytes 196616 | tf_op jit(solution)/shard_map/ppermute | solution.py:30
  71.6 6.4 %copy-start.18 = (f32[64,512]{1,0:T(8,128)}, f32[64,512]{1,0:T(8,128)S(1)}, u32[]{:S(2)}) copy-start(f32[64,512]{1,0:T(8,128)S(1)} %collective-permute-done.17.refs_14_) | copy-start | bytes 393220
  71.6 6.4 %copy-start.22 = (bf16[1,128,256]{2,1,0:T(8,128)(2,1)}, bf16[1,128,256]{2,1,0:T(8,128)(2,1)S(1)}, u32[]{:S(2)}) copy-start(bf16[1,128,256]{2,1,0:T(8,128)(2,1)S(1)} %collective-permute-done.10.refs_5_) | copy-start | bytes 196612
  76.6 1.5 %copy-start.21 = (bf16[1,128,384]{2,1,0:T(8,128)(2,1)}, bf16[1,128,384]{2,1,0:T(8,128)(2,1)S(1)}, u32[]{:S(2)}) copy-start(bf16[1,128,384]{2,1,0:T(8,128)(2,1)S(1)} %collective-permute-done.9.refs_4_) | copy-start | bytes 294916
  77.3 0.8 copy-start.23
  82.4 1.6 %collective-permute-start.18 = (f32[264,128]{1,0:T(8,128)}, f32[264,128]{1,0:T(8,128)S(1)}, u32[]{:S(2)}, u32[]{:S(2)}) collective-permute-start(f32[264,128]{1,0:T(8,128)} %get-tuple-element.52), channel_id=1, source_target_pairs={{0,1},{1,0},{2,3},{3,2},{4,5},{5,4},{6,7},{7,6},{8,9},{9,8},{10,11... | collective-permute-start | bytes 405512 | tf_op jit(solution)/shard_map/ppermute | solution.py:34
  84.0 0.7 copy-start.16
  86.3 8.4 %collective-permute-start.19 = (bf16[416,128]{1,0:T(8,128)(2,1)}, bf16[416,128]{1,0:T(8,128)(2,1)S(1)}, u32[]{:S(2)}, u32[]{:S(2)}) collective-permute-start(bf16[416,128]{1,0:T(8,128)(2,1)} %joined.3.mine_ref), channel_id=1, source_target_pairs={{0,8},{2,10},{4,12},{6,14},{8,0},{10,2},{12,4},{14,6},{1,9},{3,11}... | collective-permute-start | bytes 319496 | tf_op jit(solution)/shard_map/ppermute | solution.py:30
  97.0 5.3 %collective-permute-start.20 = (bf16[544,128]{1,0:T(8,128)(2,1)}, bf16[544,128]{1,0:T(8,128)(2,1)S(1)}, u32[]{:S(2)}, u32[]{:S(2)}) collective-permute-start(bf16[544,128]{1,0:T(8,128)(2,1)} %joined.4.mine_ref), channel_id=1, source_target_pairs={{0,4},{2,6},{4,0},{6,2},{8,12},{10,14},{12,8},{14,10},{1,5},{3,7},... | collective-permute-start | bytes 417800 | tf_op jit(solution)/shard_map/ppermute | solution.py:30
  102.3 0.7 copy-start.15
  104.6 6.0 %collective-permute-start.21 = (bf16[800,128]{1,0:T(8,128)(2,1)}, bf16[800,128]{1,0:T(8,128)(2,1)S(1)}, u32[]{:S(2)}, u32[]{:S(2)}) collective-permute-start(bf16[800,128]{1,0:T(8,128)(2,1)} %joined.5.mine_ref), channel_id=1, source_target_pairs={{0,2},{2,0},{4,6},{6,4},{8,10},{10,8},{12,14},{14,12},{1,3},{3,1},... | collective-permute-start | bytes 614408 | tf_op jit(solution)/shard_map/ppermute | solution.py:30
  110.6 0.7 copy-start.14
  116.0 1.8 %collective-permute-start.22 = (f32[512,128]{1,0:T(8,128)}, f32[512,128]{1,0:T(8,128)S(1)}, u32[]{:S(2)}, u32[]{:S(2)}) collective-permute-start(f32[512,128]{1,0:T(8,128)} %get-tuple-element.56), channel_id=1, source_target_pairs={{0,1},{1,0},{2,3},{3,2},{4,5},{5,4},{6,7},{7,6},{8,9},{9,8},{10,11... | collective-permute-start | bytes 786440 | tf_op jit(solution)/shard_map/ppermute | solution.py:34
  (2 other events, 1.3 us)
